TPU v7x, 512 devices: a whole 4x8x8 slice. The times are simulated.
512 devices in a mesh: pix: 32 (over x, y), tm: 16 (over z, core).
Axes of the slice: x: 4, y: 8, z: 8, core: 2. Of those that a mesh axis runs over, the one named last changes fastest.
Arguments:
- movie_frames: bfloat16 [128, 1024, 4096], P('tm', 'pix'), may hold values from -48 to 48
- depth_index: int32 [1024], P('pix'), may hold values from 0 to 5
- depth_width: float32 [6], replicated, may hold values from 0.7 to 3
- temporal_test_matrix: float32 [128, 96], replicated, may hold values from -4 to 4
- merge_probe: float32 [192, 96], replicated, may hold values from -4 to 4
Outputs:
- temporal_rows: float32 [96, 128], P(None, 'tm')
- loadings: bfloat16 [96, 1024, 4096], P(None, 'pix', 'tm')
All inputs are finite; a program needn't handle non-finite values.
Results may differ from a plain program's by a relative error of at most 0.0062.
Values may be sent and summed in bfloat16 or wider, within the bound.
No kernel may reach another device: no remote copies, remote signals or barrier semaphores. Data moves between devices by JAX's collectives and lax.ppermute only.
A program may use at most 64 MiB of HBM per device.

v0:
```python
import math

import jax
import jax.numpy as jnp
from jax import lax
from jax.sharding import PartitionSpec as P

ROWS_DEV = 32
COLS = 4096
HW = 4
NDEPTH = 6


greatest_rank = lax.Precision.HIGHEST
reduction_multiplier = math.sqrt(0.5)
growth_multiplier = math.sqrt(2.0)


def with_halo(block, sides, width):
    for axis, dim in sides:
        count = lax.axis_size(axis)
        forward = [(i, i + 1) for i in range(count - 1)]
        backward = [(target, source) for source, target in forward]
        low = lax.ppermute(
            lax.slice_in_dim(block, block.shape[dim] - width, None, axis=dim), axis, forward
        )
        high = lax.ppermute(lax.slice_in_dim(block, 0, width, axis=dim), axis, backward)
        block = jnp.concatenate([low, block, high], axis=dim)
    return block


def partner_2(value, axis, distance):
    mask = 2**distance
    pairs = [(source, source ^ mask) for source in range(lax.axis_size(axis))]
    return lax.ppermute(value, axis, pairs)


def taps_table(depth_width):
    offsets = jnp.arange(-HW, HW + 1).astype(jnp.float32)
    kernel_raw = jnp.exp(-offsets[None, :] ** 2 / (2.0 * depth_width[:, None] ** 2))
    return kernel_raw / jnp.sum(kernel_raw, axis=1, keepdims=True)


def row_weights(row_depth, depth_width):
    classes = jnp.arange(NDEPTH)
    onehot = (row_depth[:, None] == classes[None, :]).astype(jnp.float32)
    return jnp.dot(onehot, taps_table(depth_width), precision=greatest_rank)


def smooth_rows(padded, weights):
    row_count = weights.shape[0]
    summed = jnp.zeros((padded.shape[0], row_count, padded.shape[2]), jnp.float32)
    for offset in range(2 * HW + 1):
        summed = summed + weights[:, offset][None, :, None] * padded[
            :, offset : offset + row_count, :
        ].astype(jnp.float32)
    return summed.astype(jnp.bfloat16)


def orthonormal(sketch):
    factor = jnp.linalg.cholesky(jnp.dot(sketch.T, sketch, precision=greatest_rank))
    return lax.linalg.triangular_solve(
        factor, sketch, left_side=False, lower=True, transpose_a=True
    )


def tile_basis(scatter_matrix, temporal_test_matrix):
    basis_cols = orthonormal(jnp.dot(scatter_matrix, temporal_test_matrix, precision=greatest_rank))
    projected = jnp.dot(basis_cols.T, scatter_matrix, precision=greatest_rank)
    inner_gram = jnp.dot(projected, basis_cols, precision=greatest_rank)
    factor = jnp.linalg.cholesky(inner_gram)
    coefficient = lax.linalg.triangular_solve(
        factor, basis_cols, left_side=False, lower=True, transpose_a=True
    )
    return (factor, projected, coefficient)


def body(movie_frames, depth_index, depth_width, temporal_test_matrix, merge_probe):
    weights = row_weights(depth_index, depth_width)
    padded = with_halo(movie_frames, (("pix", 1),), HW)
    smoothed = smooth_rows(padded, weights)
    columns = lax.all_to_all(smoothed, "tm", split_axis=2, concat_axis=0, tiled=True)
    frame_total = columns.shape[0]
    flattened = columns.reshape(frame_total, -1)
    partial_cov = lax.dot_general(
        flattened, flattened, (((1,), (1,)), ((), ())), preferred_element_type=jnp.float32
    )
    scatter_matrix = lax.psum(partial_cov, "tm") / (ROWS_DEV * COLS)
    factor, projected, coefficient = tile_basis(scatter_matrix, temporal_test_matrix)
    span_length = movie_frames.shape[0]
    span_start = lax.axis_index("tm") * span_length
    rank_count = projected.shape[0]
    tree_level_count = lax.axis_size("pix").bit_length() - 1
    pix_position = lax.axis_index("pix")
    path_product = jnp.eye(rank_count, dtype=jnp.float32)
    own_projected = lax.dynamic_slice_in_dim(projected, span_start, span_length, 1)
    own_rows = lax.linalg.triangular_solve(factor, own_projected, left_side=True, lower=True)
    for merge_level in range(tree_level_count):
        partner = partner_2(own_rows, "pix", merge_level)
        is_first = pix_position >> merge_level & 1 == 0
        first_rows = jnp.where(is_first, own_rows, partner)
        second_rows = jnp.where(is_first, partner, own_rows)
        stacked = jnp.concatenate([first_rows, second_rows], axis=0)
        stacked_gram = lax.psum(jnp.dot(stacked, stacked.T, precision=greatest_rank), "tm")
        rotation = orthonormal(jnp.dot(stacked_gram, merge_probe, precision=greatest_rank))
        own_rows = jnp.dot(rotation.T, stacked, precision=greatest_rank) * reduction_multiplier
        rotation_block = (
            jnp.where(is_first, rotation[:rank_count], rotation[rank_count:]) * growth_multiplier
        )
        path_product = jnp.dot(path_product, rotation_block, precision=greatest_rank)
    weights_table = jnp.dot(coefficient, path_product, precision=greatest_rank).astype(jnp.bfloat16)
    loading_flat = lax.dot_general(
        weights_table, flattened, (((0,), (0,)), ((), ())), preferred_element_type=jnp.float32
    )
    loadings = loading_flat.astype(jnp.bfloat16).reshape(
        rank_count, columns.shape[1], columns.shape[2]
    )
    return (own_rows, loadings)


def solution(mesh):
    in_specs = (P("tm", "pix", None), P("pix"), P(), P(), P())
    out_specs = (P(None, "tm"), P(None, "pix", "tm"))
    return jax.shard_map(body, mesh=mesh, in_specs=in_specs, out_specs=out_specs, check_vma=False)
```

profile of v0, /device:TPU:1, one launch (start us, length us, event | category | flops | bytes accessed | tf_op | source)
XLA Modules:
  0.0 986.0 jit_solution(14767062543887843147)
XLA Ops:
  10.5 4.7 collective-permute-start
  19.0 6.4 add_convert_fusion
  25.3 9.2 copy.75
  34.5 13.4 %reshape.80 = bf16[16,2,32768]{2,1,0:T(2,128)(2,1)S(1)} reshape(bf16[4096,8,32]{2,1,0:T(8,128)(2,1)} %bitcast.158) | data formatting | bytes 4194304
  47.9 64.5 %all_to_all.15 = bf16[16,2,32768]{2,1,0:T(2,128)(2,1)} all-to-all(bf16[16,2,32768]{2,1,0:T(2,128)(2,1)S(1)} %reshape.80), channel_id=1, replica_groups=mesh['pix'=32,'tm'=16] {'tm'}, dimensions={0} | all-to-all | bytes 4194304 | tf_op jit(solution)/shard_map/all_to_all | solution.py:82
  112.4 12.9 %reshape.81 = bf16[4096,8,32]{2,1,0:T(8,128)(2,1)} reshape(bf16[16,2,32768]{2,1,0:T(2,128)(2,1)} %all_to_all.15) | data formatting | bytes 4194304
  125.3 8.8 copy.86
  135.9 105.2 %all-reduce.7.cloned.1.call-done = f32[128,128]{1,0:T(8,128)} async-done(((f32[128,128]{1,0:T(8,128)}), f32[128,128]{1,0:T(8,128)}) %all-reduce.7.cloned.1.call-update) | async-done | bytes 65552 | tf_op jit(solution)/shard_map/psum | solution.py:88
  242.5 8.8 cholesky.119
  252.6 7.4 custom-call.17
  261.6 8.8 cholesky.130
  271.7 7.4 custom-call.11
  279.4 3.1 collective-permute-start.2
  285.5 110.7 %all-reduce.9.cloned.1.call-done = f32[192,192]{1,0:T(8,128)} async-done(((f32[192,192]{1,0:T(8,128)}), f32[192,192]{1,0:T(8,128)}) %all-reduce.9.cloned.1.call-update) | async-done | bytes 147472 | tf_op jit(solution)/shard_map/psum | solution.py:104
  397.9 8.8 cholesky.141
  408.0 7.4 custom-call.18
  415.9 4.1 collective-permute-start.3
  422.4 113.0 %all-reduce.11.cloned.1.call-done = f32[192,192]{1,0:T(8,128)} async-done(((f32[192,192]{1,0:T(8,128)}), f32[192,192]{1,0:T(8,128)}) %all-reduce.11.cloned.1.call-update) | async-done | bytes 147472 | tf_op jit(solution)/shard_map/psum | solution.py:104
  537.1 8.8 cholesky.152
  547.2 7.4 custom-call.19
  555.1 7.1 collective-permute-start.4
  565.1 112.5 %all-reduce.13.cloned.1.call-done = f32[192,192]{1,0:T(8,128)} async-done(((f32[192,192]{1,0:T(8,128)}), f32[192,192]{1,0:T(8,128)}) %all-reduce.13.cloned.1.call-update) | async-done | bytes 147472 | tf_op jit(solution)/shard_map/psum | solution.py:104
  679.3 8.8 cholesky.163
  689.5 7.4 custom-call.20
  697.4 3.1 collective-permute-start.5
  703.3 112.7 %all-reduce.15.cloned.1.call-done = f32[192,192]{1,0:T(8,128)} async-done(((f32[192,192]{1,0:T(8,128)}), f32[192,192]{1,0:T(8,128)}) %all-reduce.15.cloned.1.call-update) | async-done | bytes 147472 | tf_op jit(solution)/shard_map/psum | solution.py:104
  817.7 8.8 cholesky.174
  827.8 7.4 custom-call.21
  835.7 4.9 collective-permute-start.6
  843.1 112.7 %all-reduce.17.cloned.1.call-done = f32[192,192]{1,0:T(8,128)} async-done(((f32[192,192]{1,0:T(8,128)}), f32[192,192]{1,0:T(8,128)}) %all-reduce.17.cloned.1.call-update) | async-done | bytes 147472 | tf_op jit(solution)/shard_map/psum | solution.py:104
  957.5 8.8 cholesky.185
  967.6 7.4 custom-call.22
  (122 shorter events, 49.2 us)
Async XLA Ops:
  7.2 389.0 %copy-start = (f32[192,96]{1,0:T(8,128)S(1)}, f32[192,96]{1,0:T(8,128)}, u32[]{:S(2)}) copy-start(f32[192,96]{1,0:T(8,128)} %param.14) | copy-start | bytes 221188
  7.2 11.8 %copy-start.1 = (bf16[8,32,4096]{2,1,0:T(8,128)(2,1)S(1)}, bf16[8,32,4096]{2,1,0:T(8,128)(2,1)}, u32[]{:S(2)}) copy-start(bf16[8,32,4096]{2,1,0:T(8,128)(2,1)} %param.10) | copy-start | bytes 6291460
  7.2 9.7 copy-start.3
  7.2 9.9 %copy-start.4 = (s32[32]{0:T(128)S(1)}, s32[32]{0:T(128)}, u32[]{:S(2)}) copy-start(s32[32]{0:T(128)} %param.11) | copy-start | bytes 388
  7.2 233.9 %all-reduce.7.cloned.1.call-start = ((), (), s32[]{:S(2)}) async-start(), calls=%async_computation.1 | async-start | bytes 131072 | tf_op jit(solution)/shard_map/psum | solution.py:88
  9.0 9.6 collective-permute-start.1
  10.5 8.0 collective-permute-start
  134.2 106.9 %copy-start.2 = (f32[128,96]{0,1:T(8,128)S(1)}, f32[128,96]{0,1:T(8,128)}, u32[]{:S(2)}) copy-start(f32[128,96]{0,1:T(8,128)} %param.13) | copy-start | bytes 147460
  135.5 260.6 %all-reduce.9.cloned.1.call-start = ((), (), s32[]{:S(2)}) async-start(), calls=%async_computation.2 | async-start | bytes 393216 | tf_op jit(solution)/shard_map/psum | solution.py:104
  279.4 4.4 collective-permute-start.2
  284.9 250.5 %all-reduce.11.cloned.1.call-start = ((), (), s32[]{:S(2)}) async-start(), calls=%async_computation.3 | async-start | bytes 393216 | tf_op jit(solution)/shard_map/psum | solution.py:104
  415.9 5.3 collective-permute-start.3
  422.3 255.3 %all-reduce.13.cloned.1.call-start = ((), (), s32[]{:S(2)}) async-start(), calls=%async_computation.4 | async-start | bytes 393216 | tf_op jit(solution)/shard_map/psum | solution.py:104
  555.1 8.3 collective-permute-start.4
  564.6 251.4 %all-reduce.15.cloned.1.call-start = ((), (), s32[]{:S(2)}) async-start(), calls=%async_computation.5 | async-start | bytes 393216 | tf_op jit(solution)/shard_map/psum | solution.py:104
  697.4 4.4 collective-permute-start.5
  702.9 252.9 %all-reduce.17.cloned.1.call-start = ((), (), s32[]{:S(2)}) async-start(), calls=%async_computation.6 | async-start | bytes 393216 | tf_op jit(solution)/shard_map/psum | solution.py:104
  835.7 5.9 collective-permute-start.6
Sparse Core Ops, SparseCore 0:
  135.7 105.3 all-reduce.6
  285.0 111.0 all-reduce.8
  422.5 112.8 all-reduce.10
  564.7 112.8 all-reduce.12
  703.0 112.8 all-reduce.14
  842.9 112.8 all-reduce.16
where the time goes:
time: 992 us; the launch traced here: 986 us
  waiting for transfers between devices  673 us (68%)
  other arithmetic  129 us (13%)
  blocking collectives  64.5 us (7%)
  local copies, waits for them, and re-layouts  50.7 us (5%)
  starting transfers between devices  29.5 us (3%)
  matrix products  24.3 us (2%)
  between operations  15 us (2%)
    psum x5, waiting for transfers between devices, body(): lax.psum(jnp.dot(stacked, stacked.T, precision=greatest_rank), 'tm')  562 us
    psum x1, waiting for transfers between devices, body(): scatter_matrix = lax.psum(partial_cov, 'tm') / (ROWS_DEV * COLS)  105 us
    all_to_all x1, blocking collectives, body(): lax.all_to_all(smoothed, 'tm', split_axis=2, concat_axis=0, tiled=True)  64.5 us
    another operation x18, other arithmetic, orthonormal(): jnp.linalg.cholesky(jnp.dot(sketch.T, sketch, precision=greatest_rank))  56.7 us
    another operation x12, other arithmetic, orthonormal(): lax.linalg.triangular_solve(factor, sketch, left_side=False, lower=True,...  48.1 us
    unnamed x17, local copies, waits for them, and re-layouts  38.8 us
    ppermute x5, starting transfers between devices, partner_2(): return lax.ppermute(value, axis, pairs)  22.3 us
  transfers between devices with their start and end apart: 13, of which 12 were waited for; matrix products, arithmetic and copies ran while one was open for 0% of the time, Pallas kernels for 0%

commit v1 on v0

v1 whole, which is shorter than its diff:
```python
import math

import jax
import jax.numpy as jnp
from jax import lax
from jax.experimental import pallas as pl
from jax.experimental.pallas import tpu as pltpu
from jax.sharding import PartitionSpec as P

ROWS_DEV = 32
COLS = 4096
FRAMES = 128
RANK = 96
HW = 4
NDEPTH = 6
BLOCK = 8

highest = lax.Precision.HIGHEST
reduction_multiplier = math.sqrt(0.5)
growth_multiplier = math.sqrt(2.0)
vmem = pl.BlockSpec(memory_space=pltpu.VMEM)
smem = pl.BlockSpec(memory_space=pltpu.SMEM)


def taps_table(depth_width):
    offsets = jnp.arange(-HW, HW + 1).astype(jnp.float32)
    kernel_raw = jnp.exp(-offsets[None, :] ** 2 / (2.0 * depth_width[:, None] ** 2))
    return kernel_raw / jnp.sum(kernel_raw, axis=1, keepdims=True)


def row_weights(row_depth, depth_width):
    classes = jnp.arange(NDEPTH)
    onehot = (row_depth[:, None] == classes[None, :]).astype(jnp.float32)
    return jnp.dot(onehot, taps_table(depth_width), precision=highest)


def split_bf16(value):
    high = lax.reduce_precision(value, exponent_bits=8, mantissa_bits=7)
    return high.astype(jnp.bfloat16), (value - high).astype(jnp.bfloat16)


def smoothing_matrices(weights, frames):
    rows = ROWS_DEV * frames
    spread = jnp.repeat(weights, frames, axis=0)
    out_row = (jnp.arange(rows) // frames)[:, None]
    out_frame = (jnp.arange(rows) % frames)[:, None]
    halo = jnp.arange(2 * frames * HW)
    frame_in = jnp.concatenate([jnp.arange(rows) // ROWS_DEV, halo // HW % frames])[None, :]
    row_in = jnp.concatenate(
        [jnp.arange(rows) % ROWS_DEV + HW, halo % HW + jnp.where(halo < frames * HW, 0, HW + ROWS_DEV)]
    )[None, :]
    tap = jnp.where(frame_in == out_frame, row_in - out_row, -1)
    matrix = jnp.zeros(tap.shape, jnp.float32)
    for offset in range(2 * HW + 1):
        matrix = matrix + jnp.where(tap == offset, spread[:, offset : offset + 1], 0.0)
    return split_bf16(matrix)


def dot_bf16(left, right):
    return lax.dot_general(left, right, (((1,), (0,)), ((), ())), preferred_element_type=jnp.float32)


def smooth_kernel(movie_ref, low_ref, high_ref, coarse_ref, fine_ref, out_ref):
    frames, rows, cols = movie_ref.shape
    movie = movie_ref[...].reshape(frames * rows, cols)
    halo = jnp.concatenate([low_ref[...], high_ref[...]], axis=0)
    data = jnp.concatenate([movie, halo], axis=0)
    out_ref[0] = (dot_bf16(coarse_ref[...], data) + dot_bf16(fine_ref[...], data)).astype(jnp.bfloat16)


def smooth_tile(movie, low, high, coarse, fine, parts):
    frames = movie.shape[0]
    width = COLS // parts
    rows = frames * ROWS_DEV
    halo = pl.BlockSpec((frames * HW, width), lambda i: (0, i))
    matrix = pl.BlockSpec(coarse.shape, lambda i: (0, 0))
    return pl.pallas_call(
        smooth_kernel,
        grid=(parts,),
        in_specs=[pl.BlockSpec((frames, ROWS_DEV, width), lambda i: (0, 0, i)), halo, halo, matrix, matrix],
        out_specs=pl.BlockSpec((1, rows, width), lambda i: (i, 0, 0)),
        out_shape=jax.ShapeDtypeStruct((parts, rows, width), jnp.bfloat16),
        name="smooth",
    )(movie, low, high, coarse, fine)


def spread_selector(parity, frames):
    row = lax.broadcasted_iota(jnp.int32, (2 * FRAMES, FRAMES), 0)
    col = lax.broadcasted_iota(jnp.int32, (2 * FRAMES, FRAMES), 1)
    wanted = col // frames * (2 * frames) + parity * frames + col % frames
    return row == wanted


def covariance_kernel(data_ref, out_ref, total_ref):
    step = pl.program_id(0)
    parts, pair, width = data_ref.shape
    frames = pair // 2

    @pl.when(step == 0)
    def _():
        total_ref[...] = jnp.zeros_like(total_ref)

    data = data_ref[...].reshape(parts * pair, width)
    total_ref[...] += lax.dot_general(data, data, (((1,), (1,)), ((), ())), preferred_element_type=jnp.float32)

    @pl.when(step == pl.num_programs(0) - 1)
    def _():
        total = total_ref[...].reshape(parts, 2, frames, parts * pair)
        result = None
        for parity in range(2):
            rows = total[:, parity].reshape(parts * frames, parts * pair)
            selector = jnp.where(spread_selector(parity, frames), 1.0, 0.0)
            term = jnp.dot(rows, selector, precision=highest, preferred_element_type=jnp.float32)
            result = term if result is None else result + term
        out_ref[...] = result


def covariance_part(columns):
    parts, rows, width = columns.shape
    pair = 2 * rows // ROWS_DEV
    return pl.pallas_call(
        covariance_kernel,
        grid=(rows // pair,),
        in_specs=[pl.BlockSpec((parts, pair, width), lambda i: (0, i, 0))],
        out_specs=pl.BlockSpec((FRAMES, FRAMES), lambda i: (0, 0)),
        out_shape=jax.ShapeDtypeStruct((FRAMES, FRAMES), jnp.float32),
        scratch_shapes=[pltpu.VMEM((2 * FRAMES, 2 * FRAMES), jnp.float32)],
        name="covariance",
    )(columns)


def loading_kernel(weights_ref, data_ref, out_ref, matrix_ref):
    parts, pair, width = data_ref.shape
    frames = pair // 2

    @pl.when(pl.program_id(0) == 0)
    def _():
        weights = weights_ref[...].astype(jnp.bfloat16)
        for parity in range(2):
            selector = jnp.where(spread_selector(parity, frames), 1.0, 0.0).astype(jnp.bfloat16)
            spread = lax.dot_general(
                weights, selector, (((1,), (1,)), ((), ())), preferred_element_type=jnp.float32
            )
            matrix_ref[parity * RANK : (parity + 1) * RANK, :] = spread.astype(jnp.bfloat16)

    data = data_ref[...].reshape(parts * pair, width)
    result = dot_bf16(matrix_ref[...], data).astype(jnp.bfloat16)
    out_ref[0] = result[:RANK]
    out_ref[1] = result[RANK:]


def loading_rows(weights, columns):
    parts, rows, width = columns.shape
    pair = 2 * rows // ROWS_DEV
    return pl.pallas_call(
        loading_kernel,
        grid=(rows // pair,),
        in_specs=[
            pl.BlockSpec((RANK, FRAMES), lambda i: (0, 0)),
            pl.BlockSpec((parts, pair, width), lambda i: (0, i, 0)),
        ],
        out_specs=pl.BlockSpec((2, RANK, width), lambda i: (i, 0, 0)),
        out_shape=jax.ShapeDtypeStruct((ROWS_DEV, RANK, width), jnp.bfloat16),
        scratch_shapes=[pltpu.VMEM((2 * RANK, 2 * FRAMES), jnp.bfloat16)],
        name="loadings",
    )(weights, columns)


def transposed_dot(left, right):
    return lax.dot_general(
        left, right, (((0,), (0,)), ((), ())), precision=highest, preferred_element_type=jnp.float32
    )


def plain_dot(left, right):
    return jnp.dot(left, right, precision=highest, preferred_element_type=jnp.float32)


def solve_with_factor(system):
    size = system.shape[0]
    width = system.shape[1]
    lanes = 128
    sub = lax.broadcasted_iota(jnp.int32, (BLOCK, 1), 0)
    current = system
    done = []
    for start in range(0, size, BLOCK):
        panel = current[:BLOCK]
        a = {}
        for i in range(BLOCK):
            for j in range(i + 1):
                a[i, j] = jnp.broadcast_to(panel[j : j + 1, start + i : start + i + 1], (BLOCK, lanes))
        factor = {}
        inverse_diag = []
        for j in range(BLOCK):
            root = lax.rsqrt(a[j, j])
            inverse_diag.append(root)
            for i in range(j + 1, BLOCK):
                factor[i, j] = a[i, j] * root
            for i in range(j + 1, BLOCK):
                for k in range(j + 1, i + 1):
                    a[i, k] = a[i, k] - factor[i, j] * factor[k, j]
        inverse = {}
        for j in range(BLOCK):
            inverse[j, j] = inverse_diag[j]
            for i in range(j + 1, BLOCK):
                total = factor[i, j] * inverse[j, j]
                for k in range(j + 1, i):
                    total = total + factor[i, k] * inverse[k, j]
                inverse[i, j] = -total * inverse_diag[i]
        solved = None
        for j in range(BLOCK):
            column = jnp.where(sub == j, inverse[j, j], 0.0)
            for i in range(j + 1, BLOCK):
                column = jnp.where(sub == i, inverse[i, j], column)
            term = jnp.concatenate([column] * (width // lanes), axis=1) * jnp.broadcast_to(
                panel[j : j + 1], (BLOCK, width)
            )
            solved = term if solved is None else solved + term
        done.append(solved[:, lanes:])
        if start + BLOCK < size:
            update = transposed_dot(solved[:, :lanes], solved)
            current = current[BLOCK:] - update[start + BLOCK : size]
    return jnp.concatenate(done, axis=0)


def basis_kernel(covariance_ref, test_ref, rows_ref, weights_ref):
    covariance = covariance_ref[...] * (1.0 / (ROWS_DEV * COLS))
    sketch = plain_dot(covariance, test_ref[...])
    image = plain_dot(covariance, sketch)
    row = lax.broadcasted_iota(jnp.int32, (FRAMES, FRAMES), 0)
    col = lax.broadcasted_iota(jnp.int32, (FRAMES, FRAMES), 1)
    identity = jnp.where(row == col, 1.0, 0.0)
    system = transposed_dot(sketch, jnp.concatenate([image, covariance, identity], axis=1))
    solved = solve_with_factor(system[:RANK])
    rows_ref[...] = solved[:, :FRAMES]
    weights_ref[...] = solved[:, FRAMES:]


def tile_basis(covariance, test_matrix):
    shape = jax.ShapeDtypeStruct((RANK, FRAMES), jnp.float32)
    return pl.pallas_call(
        basis_kernel,
        in_specs=[vmem, vmem],
        out_specs=[vmem, vmem],
        out_shape=[shape, shape],
        name="basis",
    )(covariance, test_matrix)


def merge_kernel(first_ref, own_ref, partner_ref, weights_ref, probe_ref, rows_ref, new_weights_ref):
    is_first = first_ref[0] == 1
    own = own_ref[...]
    partner = partner_ref[...]
    weights = weights_ref[...]
    stacked = jnp.concatenate([jnp.where(is_first, own, partner), jnp.where(is_first, partner, own)], axis=0)
    placed = jnp.concatenate([jnp.where(is_first, weights, 0.0), jnp.where(is_first, 0.0, weights)], axis=0)
    sketch = plain_dot(stacked, transposed_dot(stacked, probe_ref[...]))
    system = transposed_dot(sketch, jnp.concatenate([sketch, stacked, placed], axis=1))
    solved = solve_with_factor(system[:RANK])
    rows_ref[...] = solved[:, :FRAMES] * reduction_multiplier
    new_weights_ref[...] = solved[:, FRAMES:] * growth_multiplier


def merge(is_first, own, partner, weights, probe):
    shape = jax.ShapeDtypeStruct((RANK, FRAMES), jnp.float32)
    return pl.pallas_call(
        merge_kernel,
        in_specs=[smem, vmem, vmem, vmem, vmem],
        out_specs=[vmem, vmem],
        out_shape=[shape, shape],
        name="merge",
    )(is_first, own, partner, weights, probe)


def sum_over_tm(partial):
    parts = lax.axis_size("tm")
    height = partial.shape[0] // parts
    pieces = lax.all_to_all(partial.reshape(parts, height, -1), "tm", 0, 0, tiled=True)
    own = jnp.sum(pieces, axis=0, keepdims=True)
    whole = lax.all_to_all(jnp.broadcast_to(own, pieces.shape), "tm", 0, 0, tiled=True)
    return whole.reshape(partial.shape)


def body(movie_frames, depth_index, depth_width, temporal_test_matrix, merge_probe):
    frames = movie_frames.shape[0]
    parts = lax.axis_size("tm")
    count = lax.axis_size("pix")
    forward = [(i, i + 1) for i in range(count - 1)]
    backward = [(target, source) for source, target in forward]
    low = lax.ppermute(movie_frames[:, ROWS_DEV - HW :].reshape(frames * HW, COLS), "pix", forward)
    high = lax.ppermute(movie_frames[:, :HW].reshape(frames * HW, COLS), "pix", backward)
    coarse, fine = smoothing_matrices(row_weights(depth_index, depth_width), frames)
    smoothed = smooth_tile(movie_frames, low, high, coarse, fine, parts)
    columns = lax.all_to_all(smoothed, "tm", 0, 0, tiled=True)
    covariance = sum_over_tm(covariance_part(columns))
    spare = FRAMES - RANK
    test_matrix = jnp.pad(temporal_test_matrix, ((0, 0), (0, spare)))
    probe = jnp.pad(merge_probe, ((0, 0), (0, spare)))
    own_rows, weights = tile_basis(covariance, test_matrix)
    position = lax.axis_index("pix")
    for level in range(count.bit_length() - 1):
        pairs = [(source, source ^ (1 << level)) for source in range(count)]
        partner = lax.ppermute(own_rows, "pix", pairs)
        is_first = (1 - (position >> level & 1)).astype(jnp.int32).reshape(1)
        own_rows, weights = merge(is_first, own_rows, partner, weights, probe)
    loadings = jnp.transpose(loading_rows(weights, columns), (1, 0, 2))
    own_times = lax.dynamic_slice_in_dim(own_rows, lax.axis_index("tm") * frames, frames, 1)
    return (own_times, loadings)


def solution(mesh):
    in_specs = (P("tm", "pix", None), P("pix"), P(), P(), P())
    out_specs = (P(None, "tm"), P(None, "pix", "tm"))
    return jax.shard_map(body, mesh=mesh, in_specs=in_specs, out_specs=out_specs, check_vma=False)
```

time: 992 us -> 238 us (0.24)
  the two profiles are of different devices: /device:TPU:1 before, /device:TPU:8 now
where the time goes in v1:
time: 238 us; the launch traced here: 236 us
  Pallas kernels  88.4 us (37%)
  blocking collectives  72.2 us (30%)
  starting transfers between devices  34.7 us (15%)
  waiting for transfers between devices  26 us (11%)
  local copies, waits for them, and re-layouts  12.4 us (5%)
    all_to_all x1, blocking collectives, body(): columns = lax.all_to_all(smoothed, 'tm', 0, 0, tiled=True)  60.2 us
    pallas_call x5, Pallas kernels, merge(): pl.pallas_call(merge_kernel, in_specs=[smem, vmem, vmem, vmem, vmem], out...  46.6 us
    ppermute x5, starting transfers between devices, body(): partner = lax.ppermute(own_rows, 'pix', pairs)  22.2 us
    ppermute x5, waiting for transfers between devices, body(): partner = lax.ppermute(own_rows, 'pix', pairs)  16.9 us
    all_to_all x1, blocking collectives, sum_over_tm(): lax.all_to_all(partial.reshape(parts, height, -1), 'tm', 0, 0, tiled=True)  12.1 us
    pallas_call x1, Pallas kernels, smooth_tile(): pl.pallas_call(smooth_kernel, grid=(parts,), in_specs=[pl.BlockSpec((fram...  11.7 us
    pallas_call x1, Pallas kernels, loading_rows(): pl.pallas_call(loading_kernel, grid=(rows // pair,), in_specs=[pl.BlockSp...  10.6 us
    pallas_call x1, Pallas kernels, covariance_part(): pl.pallas_call(covariance_kernel, grid=(rows // pair,), in_specs=[pl.Bloc...  10.6 us
  transfers between devices with their start and end apart: 8, of which 8 were waited for; matrix products, arithmetic and copies ran while one was open for 1% of the time, Pallas kernels for 0%

profile of v1, /device:TPU:8, one launch (start us, length us, event | category | flops | bytes accessed | tf_op | source)
XLA Modules:
  0.0 236.4 jit_solution(9191012317903342976)
XLA Ops:
  0.6 1.5 fusion.24
  2.2 3.5 %collective-permute-start = (bf16[32,4096]{1,0:T(8,128)(2,1)S(1)}, bf16[32,4096]{1,0:T(8,128)(2,1)S(1)}, u32[]{:S(2)}, u32[]{:S(2)}) collective-permute-start(bf16[32,4096]{1,0:T(8,128)(2,1)S(1)} %reshape.80), channel_id=1, source_target_pairs={{0,16},{16,32},{32,48},{48,64},{64,80},{80,96},{96,112},{112,128},... | collective-permute-start | bytes 786440 | tf_op jit(solution)/shard_map/ppermute | solution.py:290
  5.8 5.5 %collective-permute-start.1 = (bf16[32,4096]{1,0:T(8,128)(2,1)S(1)}, bf16[32,4096]{1,0:T(8,128)(2,1)S(1)}, u32[]{:S(2)}, u32[]{:S(2)}) collective-permute-start(bf16[32,4096]{1,0:T(8,128)(2,1)S(1)} %reshape.81), channel_id=1, source_target_pairs={{16,0},{32,16},{48,32},{64,48},{80,64},{96,80},{112,96},{128,112},... | collective-permute-start | bytes 786440 | tf_op jit(solution)/shard_map/ppermute | solution.py:291
  12.1 1.2 fusion
  13.6 1.8 collective-permute-done.1.high_ref
  15.4 0.7 copy-done.1
  16.1 11.7 %smooth.1 = bf16[16,256,256]{2,1,0:T(8,128)(2,1)} custom-call(bf16[8,32,4096]{2,1,0:T(8,128)(2,1)} %movie_ref.1, bf16[32,4096]{1,0:T(8,128)(2,1)} %copy-done, bf16[32,4096]{1,0:T(8,128)(2,1)} %copy-done.1, bf16[256,320]{1,0:T(8,128)(2,1)} %get-tuple-element.46.coarse_ref, bf16[256,320]{1,0:T(8,128)(2,1)} %get-tuple-element.45.fine_ref), custom_call_target="tpu_custom_call" | custom-call | tf_op jit(solution)/shard_map/smooth/pallas_call | solution.py:77
  27.8 60.2 %all_to_all.15.data_ref = bf16[16,256,256]{2,1,0:T(8,128)(2,1)} all-to-all(bf16[16,256,256]{2,1,0:T(8,128)(2,1)} %smooth.1), channel_id=1, replica_groups=mesh['pix'=32,'tm'=16] {'tm'}, dimensions={0} | all-to-all | bytes 4194304 | tf_op jit(solution)/shard_map/all_to_all | solution.py:294
  88.0 10.6 %covariance.1 = f32[128,128]{1,0:T(8,128)} custom-call(bf16[16,256,256]{2,1,0:T(8,128)(2,1)} %all_to_all.15.data_ref), custom_call_target="tpu_custom_call" | custom-call | tf_op jit(solution)/shard_map/covariance/pallas_call | solution.py:121
  98.5 12.1 %all_to_all.16 = f32[16,8,128]{2,1,0:T(8,128)S(1)} all-to-all(f32[16,8,128]{2,1,0:T(8,128)} %bitcast.20), channel_id=1, replica_groups=mesh['pix'=32,'tm'=16] {'tm'}, dimensions={0} | all-to-all | bytes 131072 | tf_op jit(solution)/shard_map/all_to_all | solution.py:278
  111.2 3.5 %all-to-all-start.2 = ((f32[16,8,128]{2,1,0:T(8,128)}), f32[16,8,128]{2,1,0:T(8,128)S(1)}, u32[]{:S(2)}, u32[]{:S(2)}) async-start(f32[16,8,128]{2,1,0:T(8,128)} %broadcast_in_dim.128), calls=%async_computation.2 | async-start | bytes 131072 | tf_op jit(solution)/shard_map/all_to_all | solution.py:280
  115.5 7.0 %all-to-all-done.2 = f32[16,8,128]{2,1,0:T(8,128)S(1)} async-done(((f32[16,8,128]{2,1,0:T(8,128)}), f32[16,8,128]{2,1,0:T(8,128)S(1)}, u32[]{:S(2)}, u32[]{:S(2)}) %all-to-all-start.2) | async-done | bytes 65568 | tf_op jit(solution)/shard_map/all_to_all | solution.py:280
  123.1 8.9 %basis.1 = (f32[96,128]{1,0:T(8,128)}, f32[96,128]{1,0:T(8,128)}) custom-call(f32[128,128]{1,0:T(8,128)} %bitcast.21, f32[128,128]{1,0:T(8,128)} %pad.8.test_ref), custom_call_target="tpu_custom_call" | custom-call | tf_op jit(solution)/shard_map/basis/pallas_call | solution.py:241
  132.1 2.5 %collective-permute-start.2 = (f32[96,128]{1,0:T(8,128)}, f32[96,128]{1,0:T(8,128)S(1)}, u32[]{:S(2)}, u32[]{:S(2)}) collective-permute-start(f32[96,128]{1,0:T(8,128)} %get-tuple-element.14.own_ref), channel_id=1, source_target_pairs={{0,16},{16,0},{32,48},{48,32},{64,80},{80,64},{96,112},{112,96},{1... | collective-permute-start | bytes 147464 | tf_op jit(solution)/shard_map/ppermute | solution.py:303
  134.6 0.7 pad.9.probe_ref
  135.3 3.0 %collective-permute-done.2.partner_ref = f32[96,128]{1,0:T(8,128)S(1)} collective-permute-done((f32[96,128]{1,0:T(8,128)}, f32[96,128]{1,0:T(8,128)S(1)}, u32[]{:S(2)}, u32[]{:S(2)}) %collective-permute-start.2) | collective-permute-done | bytes 49184 | tf_op jit(solution)/shard_map/ppermute | solution.py:303
  138.9 9.3 %merge.5 = (f32[96,128]{1,0:T(8,128)}, f32[96,128]{1,0:T(8,128)}) custom-call(s32[1]{0:T(128)} %bitcast.4.first_ref, f32[96,128]{1,0:T(8,128)} %get-tuple-element.14.own_ref, f32[96,128]{1,0:T(8,128)} %copy-done.7, f32[96,128]{1,0:T(8,128)} %get-tuple-element.15.weights_ref, f32[192,128]{1,0:T(8,128)} %pad.9.probe_ref), custom_call_target="tpu_custom_call" | custom-call | tf_op jit(solution)/shard_map/merge/pallas_call | solution.py:266
  148.2 6.9 %collective-permute-start.3 = (f32[96,128]{1,0:T(8,128)}, f32[96,128]{1,0:T(8,128)S(1)}, u32[]{:S(2)}, u32[]{:S(2)}) collective-permute-start(f32[96,128]{1,0:T(8,128)} %get-tuple-element.16.own_ref), channel_id=1, source_target_pairs={{0,32},{16,48},{32,0},{48,16},{64,96},{80,112},{96,64},{112,80},{1... | collective-permute-start | bytes 147464 | tf_op jit(solution)/shard_map/ppermute | solution.py:303
  155.2 2.3 collective-permute-done.3.partner_ref
  158.0 9.3 %merge.6 = (f32[96,128]{1,0:T(8,128)}, f32[96,128]{1,0:T(8,128)}) custom-call(s32[1]{0:T(128)} %bitcast.3.first_ref, f32[96,128]{1,0:T(8,128)} %get-tuple-element.16.own_ref, f32[96,128]{1,0:T(8,128)} %copy-done.10, f32[96,128]{1,0:T(8,128)} %get-tuple-element.17.weights_ref, f32[192,128]{1,0:T(8,128)} %pad.9.probe_ref), custom_call_target="tpu_custom_call" | custom-call | tf_op jit(solution)/shard_map/merge/pallas_call | solution.py:266
  167.4 4.1 %collective-permute-start.4 = (f32[96,128]{1,0:T(8,128)}, f32[96,128]{1,0:T(8,128)S(1)}, u32[]{:S(2)}, u32[]{:S(2)}) collective-permute-start(f32[96,128]{1,0:T(8,128)} %get-tuple-element.18.own_ref), channel_id=1, source_target_pairs={{0,64},{16,80},{32,96},{48,112},{64,0},{80,16},{96,32},{112,48},{1... | collective-permute-start | bytes 147464 | tf_op jit(solution)/shard_map/ppermute | solution.py:303
  171.5 6.4 %collective-permute-done.4.partner_ref = f32[96,128]{1,0:T(8,128)S(1)} collective-permute-done((f32[96,128]{1,0:T(8,128)}, f32[96,128]{1,0:T(8,128)S(1)}, u32[]{:S(2)}, u32[]{:S(2)}) %collective-permute-start.4) | collective-permute-done | bytes 49184 | tf_op jit(solution)/shard_map/ppermute | solution.py:303
  178.5 9.3 %merge.7 = (f32[96,128]{1,0:T(8,128)}, f32[96,128]{1,0:T(8,128)}) custom-call(s32[1]{0:T(128)} %bitcast.2.first_ref, f32[96,128]{1,0:T(8,128)} %get-tuple-element.18.own_ref, f32[96,128]{1,0:T(8,128)} %copy-done.8, f32[96,128]{1,0:T(8,128)} %get-tuple-element.19.weights_ref, f32[192,128]{1,0:T(8,128)} %pad.9.probe_ref), custom_call_target="tpu_custom_call" | custom-call | tf_op jit(solution)/shard_map/merge/pallas_call | solution.py:266
  187.9 3.4 %collective-permute-start.5 = (f32[96,128]{1,0:T(8,128)}, f32[96,128]{1,0:T(8,128)S(1)}, u32[]{:S(2)}, u32[]{:S(2)}) collective-permute-start(f32[96,128]{1,0:T(8,128)} %get-tuple-element.20.own_ref), channel_id=1, source_target_pairs={{0,128},{16,144},{32,160},{48,176},{64,192},{80,208},{96,224},{112... | collective-permute-start | bytes 147464 | tf_op jit(solution)/shard_map/ppermute | solution.py:303
  191.3 2.8 %collective-permute-done.5.partner_ref = f32[96,128]{1,0:T(8,128)S(1)} collective-permute-done((f32[96,128]{1,0:T(8,128)}, f32[96,128]{1,0:T(8,128)S(1)}, u32[]{:S(2)}, u32[]{:S(2)}) %collective-permute-start.5) | collective-permute-done | bytes 49184 | tf_op jit(solution)/shard_map/ppermute | solution.py:303
  194.7 9.3 %merge.8 = (f32[96,128]{1,0:T(8,128)}, f32[96,128]{1,0:T(8,128)}) custom-call(s32[1]{0:T(128)} %bitcast.1.first_ref, f32[96,128]{1,0:T(8,128)} %get-tuple-element.20.own_ref, f32[96,128]{1,0:T(8,128)} %copy-done.9, f32[96,128]{1,0:T(8,128)} %get-tuple-element.21.weights_ref, f32[192,128]{1,0:T(8,128)} %pad.9.probe_ref), custom_call_target="tpu_custom_call" | custom-call | tf_op jit(solution)/shard_map/merge/pallas_call | solution.py:266
  204.0 5.2 %collective-permute-start.6 = (f32[96,128]{1,0:T(8,128)}, f32[96,128]{1,0:T(8,128)S(1)}, u32[]{:S(2)}, u32[]{:S(2)}) collective-permute-start(f32[96,128]{1,0:T(8,128)} %get-tuple-element.22.own_ref), channel_id=1, source_target_pairs={{0,256},{16,272},{32,288},{48,304},{64,320},{80,336},{96,352},{112... | collective-permute-start | bytes 147464 | tf_op jit(solution)/shard_map/ppermute | solution.py:303
  209.2 2.5 %collective-permute-done.6.partner_ref = f32[96,128]{1,0:T(8,128)S(1)} collective-permute-done((f32[96,128]{1,0:T(8,128)}, f32[96,128]{1,0:T(8,128)S(1)}, u32[]{:S(2)}, u32[]{:S(2)}) %collective-permute-start.6) | collective-permute-done | bytes 49184 | tf_op jit(solution)/shard_map/ppermute | solution.py:303
  212.3 9.3 %merge.9 = (f32[96,128]{1,0:T(8,128)}, f32[96,128]{1,0:T(8,128)}) custom-call(s32[1]{0:T(128)} %bitcast.first_ref, f32[96,128]{1,0:T(8,128)} %get-tuple-element.22.own_ref, f32[96,128]{1,0:T(8,128)} %copy-done.6, f32[96,128]{1,0:T(8,128)} %get-tuple-element.23.weights_ref, f32[192,128]{1,0:T(8,128)} %pad.9.probe_ref), custom_call_target="tpu_custom_call" | custom-call | tf_op jit(solution)/shard_map/merge/pallas_call | solution.py:266
  221.6 10.6 %loadings.1 = bf16[32,96,256]{2,1,0:T(8,128)(2,1)} custom-call(f32[96,128]{1,0:T(8,128)} %get-tuple-element.25.weights_ref, bf16[16,256,256]{2,1,0:T(8,128)(2,1)} %all_to_all.15.data_ref), custom_call_target="tpu_custom_call" | custom-call | tf_op jit(solution)/shard_map/loadings/pallas_call | solution.py:155
  232.2 3.4 %copy.19 = bf16[96,32,256]{2,1,0:T(8,128)(2,1)} copy(bf16[96,32,256]{2,0,1:T(8,128)(2,1)} %bitcast.19) | data formatting | bytes 3145728
  235.7 0.7 copy.18
  (46 shorter events, 6.3 us)
Async XLA Ops:
  0.6 10.7 %copy-start.11 = (f32[6]{0:T(128)S(1)}, f32[6]{0:T(128)}, u32[]{:S(2)}) copy-start(f32[6]{0:T(128)} %param.7) | copy-start | bytes 76
  0.6 10.9 %copy-start.12 = (s32[32]{0:T(128)S(1)}, s32[32]{0:T(128)}, u32[]{:S(2)}) copy-start(s32[32]{0:T(128)} %param.6) | copy-start | bytes 388
  2.2 11.4 %collective-permute-start = (bf16[32,4096]{1,0:T(8,128)(2,1)S(1)}, bf16[32,4096]{1,0:T(8,128)(2,1)S(1)}, u32[]{:S(2)}, u32[]{:S(2)}) collective-permute-start(bf16[32,4096]{1,0:T(8,128)(2,1)S(1)} %reshape.80), channel_id=1, source_target_pairs={{0,16},{16,32},{32,48},{48,64},{64,80},{80,96},{96,112},{112,128},... | collective-permute-start | bytes 786440 | tf_op jit(solution)/shard_map/ppermute | solution.py:290
  5.8 9.7 %collective-permute-start.1 = (bf16[32,4096]{1,0:T(8,128)(2,1)S(1)}, bf16[32,4096]{1,0:T(8,128)(2,1)S(1)}, u32[]{:S(2)}, u32[]{:S(2)}) collective-permute-start(bf16[32,4096]{1,0:T(8,128)(2,1)S(1)} %reshape.81), channel_id=1, source_target_pairs={{16,0},{32,16},{48,32},{64,48},{80,64},{96,80},{112,96},{128,112},... | collective-permute-start | bytes 786440 | tf_op jit(solution)/shard_map/ppermute | solution.py:291
  13.6 1.8 copy-start
  15.4 0.7 copy-start.1
  88.0 26.8 %copy-start.4 = (f32[128,96]{0,1:T(8,128)S(1)}, f32[128,96]{0,1:T(8,128)}, u32[]{:S(2)}) copy-start(f32[128,96]{0,1:T(8,128)} %param.8) | copy-start | bytes 147460
  88.0 46.7 %copy-start.3 = (f32[192,96]{1,0:T(8,128)S(1)}, f32[192,96]{1,0:T(8,128)}, u32[]{:S(2)}) copy-start(f32[192,96]{1,0:T(8,128)} %param.9) | copy-start | bytes 221188
  111.2 11.3 %all-to-all-start.2 = ((f32[16,8,128]{2,1,0:T(8,128)}), f32[16,8,128]{2,1,0:T(8,128)S(1)}, u32[]{:S(2)}, u32[]{:S(2)}) async-start(f32[16,8,128]{2,1,0:T(8,128)} %broadcast_in_dim.128), calls=%async_computation.2 | async-start | bytes 131072 | tf_op jit(solution)/shard_map/all_to_all | solution.py:280
  122.5 0.6 copy-start.2
  132.1 6.2 %collective-permute-start.2 = (f32[96,128]{1,0:T(8,128)}, f32[96,128]{1,0:T(8,128)S(1)}, u32[]{:S(2)}, u32[]{:S(2)}) collective-permute-start(f32[96,128]{1,0:T(8,128)} %get-tuple-element.14.own_ref), channel_id=1, source_target_pairs={{0,16},{16,0},{32,48},{48,32},{64,80},{80,64},{96,112},{112,96},{1... | collective-permute-start | bytes 147464 | tf_op jit(solution)/shard_map/ppermute | solution.py:303
  138.3 0.6 copy-start.7
  148.2 9.2 %collective-permute-start.3 = (f32[96,128]{1,0:T(8,128)}, f32[96,128]{1,0:T(8,128)S(1)}, u32[]{:S(2)}, u32[]{:S(2)}) collective-permute-start(f32[96,128]{1,0:T(8,128)} %get-tuple-element.16.own_ref), channel_id=1, source_target_pairs={{0,32},{16,48},{32,0},{48,16},{64,96},{80,112},{96,64},{112,80},{1... | collective-permute-start | bytes 147464 | tf_op jit(solution)/shard_map/ppermute | solution.py:303
  157.4 0.6 copy-start.10
  167.4 10.6 %collective-permute-start.4 = (f32[96,128]{1,0:T(8,128)}, f32[96,128]{1,0:T(8,128)S(1)}, u32[]{:S(2)}, u32[]{:S(2)}) collective-permute-start(f32[96,128]{1,0:T(8,128)} %get-tuple-element.18.own_ref), channel_id=1, source_target_pairs={{0,64},{16,80},{32,96},{48,112},{64,0},{80,16},{96,32},{112,48},{1... | collective-permute-start | bytes 147464 | tf_op jit(solution)/shard_map/ppermute | solution.py:303
  177.9 0.6 copy-start.8
  187.9 6.2 %collective-permute-start.5 = (f32[96,128]{1,0:T(8,128)}, f32[96,128]{1,0:T(8,128)S(1)}, u32[]{:S(2)}, u32[]{:S(2)}) collective-permute-start(f32[96,128]{1,0:T(8,128)} %get-tuple-element.20.own_ref), channel_id=1, source_target_pairs={{0,128},{16,144},{32,160},{48,176},{64,192},{80,208},{96,224},{112... | collective-permute-start | bytes 147464 | tf_op jit(solution)/shard_map/ppermute | solution.py:303
  194.0 0.6 copy-start.9
  204.0 7.7 %collective-permute-start.6 = (f32[96,128]{1,0:T(8,128)}, f32[96,128]{1,0:T(8,128)S(1)}, u32[]{:S(2)}, u32[]{:S(2)}) collective-permute-start(f32[96,128]{1,0:T(8,128)} %get-tuple-element.22.own_ref), channel_id=1, source_target_pairs={{0,256},{16,272},{32,288},{48,304},{64,320},{80,336},{96,352},{112... | collective-permute-start | bytes 147464 | tf_op jit(solution)/shard_map/ppermute | solution.py:303
  211.7 0.6 copy-start.6
  232.2 3.4 %copy-start.5 = (f32[96,128]{1,0:T(8,128)S(1)}, f32[96,128]{1,0:T(8,128)}, u32[]{:S(2)}) copy-start(f32[96,128]{1,0:T(8,128)} %get-tuple-element.24) | copy-start | bytes 147460

commit v2 on v1

v2 whole, which is shorter than its diff:
```python
import math

import jax
import jax.numpy as jnp
from jax import lax
from jax.experimental import pallas as pl
from jax.experimental.pallas import tpu as pltpu
from jax.sharding import PartitionSpec as P

ROWS_DEV = 32
COLS = 4096
FRAMES = 128
RANK = 96
HW = 4
NDEPTH = 6
BLOCK = 8
SMOOTH_GROUP = 4
PAIR_GROUP = 4
LOADING_ROWS = 8

highest = lax.Precision.HIGHEST
reduction_multiplier = math.sqrt(0.5)
growth_multiplier = math.sqrt(2.0)
vmem = pl.BlockSpec(memory_space=pltpu.VMEM)
smem = pl.BlockSpec(memory_space=pltpu.SMEM)


def near(*values):
    return [pltpu.with_memory_space_constraint(value, pltpu.VMEM) for value in values]


def taps_table(depth_width):
    offsets = jnp.arange(-HW, HW + 1).astype(jnp.float32)
    kernel_raw = jnp.exp(-offsets[None, :] ** 2 / (2.0 * depth_width[:, None] ** 2))
    return kernel_raw / jnp.sum(kernel_raw, axis=1, keepdims=True)


def row_weights(row_depth, depth_width):
    classes = jnp.arange(NDEPTH)
    onehot = (row_depth[:, None] == classes[None, :]).astype(jnp.float32)
    return jnp.dot(onehot, taps_table(depth_width), precision=highest)


def split_bf16(value):
    high = lax.reduce_precision(value, exponent_bits=8, mantissa_bits=7)
    return high.astype(jnp.bfloat16), (value - high).astype(jnp.bfloat16)


def smoothing_matrices(weights, frames):
    rows = ROWS_DEV * frames
    spread = jnp.repeat(weights, frames, axis=0)
    out_row = (jnp.arange(rows) // frames)[:, None]
    out_frame = (jnp.arange(rows) % frames)[:, None]
    halo = jnp.arange(2 * frames * HW)
    frame_in = jnp.concatenate([jnp.arange(rows) // ROWS_DEV, halo // HW % frames])[None, :]
    row_in = jnp.concatenate(
        [jnp.arange(rows) % ROWS_DEV + HW, halo % HW + jnp.where(halo < frames * HW, 0, HW + ROWS_DEV)]
    )[None, :]
    tap = jnp.where(frame_in == out_frame, row_in - out_row, -1)
    matrix = jnp.zeros(tap.shape, jnp.float32)
    for offset in range(2 * HW + 1):
        matrix = matrix + jnp.where(tap == offset, spread[:, offset : offset + 1], 0.0)
    high, low = split_bf16(matrix)
    return jnp.concatenate([high, low], axis=0)


def dot_bf16(left, right):
    return lax.dot_general(left, right, (((1,), (0,)), ((), ())), preferred_element_type=jnp.float32)


def smooth_kernel(movie_ref, low_ref, high_ref, matrix_ref, out_ref):
    frames, rows, cols = movie_ref.shape
    count, out_rows, width = out_ref.shape
    start = pl.program_id(0) * cols
    matrix = matrix_ref[...]
    for part in range(count):
        movie = movie_ref[:, :, part * width : (part + 1) * width].reshape(frames * rows, width)
        lanes = pl.ds(pl.multiple_of(start + part * width, width), width)
        data = jnp.concatenate([movie, low_ref[:, lanes], high_ref[:, lanes]], axis=0)
        both = dot_bf16(matrix, data)
        out_ref[part] = (both[:out_rows] + both[out_rows:]).astype(jnp.bfloat16)


def smooth_tile(movie, low, high, matrix, parts):
    frames = movie.shape[0]
    width = COLS // parts
    rows = frames * ROWS_DEV
    group = SMOOTH_GROUP
    return pl.pallas_call(
        smooth_kernel,
        grid=(parts // group,),
        in_specs=[
            pl.BlockSpec((frames, ROWS_DEV, group * width), lambda i: (0, 0, i)),
            vmem,
            vmem,
            vmem,
        ],
        out_specs=pl.BlockSpec((group, rows, width), lambda i: (i, 0, 0)),
        out_shape=jax.ShapeDtypeStruct((parts, rows, width), jnp.bfloat16),
        name="smooth",
    )(movie, *near(low, high, matrix))


def spread_selector(parity, frames):
    row = lax.broadcasted_iota(jnp.int32, (2 * FRAMES, FRAMES), 0)
    col = lax.broadcasted_iota(jnp.int32, (2 * FRAMES, FRAMES), 1)
    wanted = col // frames * (2 * frames) + parity * frames + col % frames
    return row == wanted


def covariance_kernel(data_ref, out_ref, total_ref):
    step = pl.program_id(0)
    parts, rows, width = data_ref.shape
    pair = rows // PAIR_GROUP
    frames = pair // 2

    @pl.when(step == 0)
    def _():
        total_ref[...] = jnp.zeros_like(total_ref)

    pieces = [
        data_ref[:, i * pair : (i + 1) * pair, :].reshape(parts * pair, width) for i in range(PAIR_GROUP)
    ]
    data = jnp.concatenate(pieces, axis=1)
    total_ref[...] += lax.dot_general(data, data, (((1,), (1,)), ((), ())), preferred_element_type=jnp.float32)

    @pl.when(step == pl.num_programs(0) - 1)
    def _():
        total = total_ref[...].reshape(parts, 2, frames, parts * pair)
        result = None
        for parity in range(2):
            rows = total[:, parity].reshape(parts * frames, parts * pair)
            selector = jnp.where(spread_selector(parity, frames), 1.0, 0.0)
            term = jnp.dot(rows, selector, precision=highest, preferred_element_type=jnp.float32)
            result = term if result is None else result + term
        out_ref[...] = result


def covariance_part(columns):
    parts, rows, width = columns.shape
    block = PAIR_GROUP * 2 * rows // ROWS_DEV
    return pl.pallas_call(
        covariance_kernel,
        grid=(rows // block,),
        in_specs=[pl.BlockSpec((parts, block, width), lambda i: (0, i, 0))],
        out_specs=pl.BlockSpec((FRAMES, FRAMES), lambda i: (0, 0)),
        out_shape=pltpu.VMEM((FRAMES, FRAMES), jnp.float32),
        scratch_shapes=[pltpu.VMEM((2 * FRAMES, 2 * FRAMES), jnp.float32)],
        name="covariance",
    )(columns)


def loading_kernel(weights_ref, data_ref, out_ref, matrix_ref, turn_ref):
    rank, height, width = out_ref.shape
    parts, rows, _ = data_ref.shape
    frames = rows // height
    pair = 2 * frames

    @pl.when(pl.program_id(0) == 0)
    def _():
        weights = weights_ref[...].astype(jnp.bfloat16)
        for parity in range(2):
            selector = jnp.where(spread_selector(parity, frames), 1.0, 0.0).astype(jnp.bfloat16)
            spread = lax.dot_general(
                weights, selector, (((1,), (1,)), ((), ())), preferred_element_type=jnp.float32
            )
            matrix_ref[parity * rank : (parity + 1) * rank, :] = spread.astype(jnp.bfloat16)

    matrix = matrix_ref[...]
    for i in range(height // 2):
        data = data_ref[:, i * pair : (i + 1) * pair, :].reshape(parts * pair, width)
        result = dot_bf16(matrix, data)
        for parity in range(2):
            for half in range(width // 128):
                lanes = slice(half * 128, (half + 1) * 128)
                turn_ref[half, pl.ds(2 * i + parity, rank, stride=height), :] = result[
                    parity * rank : (parity + 1) * rank, lanes
                ]
    for half in range(width // 128):
        lanes = slice(half * 128, (half + 1) * 128)
        out_ref[:, :, lanes] = turn_ref[half].reshape(rank, height, 128).astype(jnp.bfloat16)


def loading_rows(weights, columns):
    parts, rows, width = columns.shape
    height = LOADING_ROWS
    return pl.pallas_call(
        loading_kernel,
        grid=(ROWS_DEV // height,),
        in_specs=[vmem, pl.BlockSpec((parts, height * (rows // ROWS_DEV), width), lambda i: (0, i, 0))],
        out_specs=pl.BlockSpec((RANK, height, width), lambda i: (0, i, 0)),
        out_shape=jax.ShapeDtypeStruct((RANK, ROWS_DEV, width), jnp.bfloat16),
        scratch_shapes=[
            pltpu.VMEM((2 * RANK, 2 * FRAMES), jnp.bfloat16),
            pltpu.VMEM((width // 128, RANK * height, 128), jnp.float32),
        ],
        name="loadings",
    )(*near(weights), columns)


def split_in_three(value):
    high = value.astype(jnp.bfloat16).astype(jnp.float32)
    rest = value - high
    middle = rest.astype(jnp.bfloat16).astype(jnp.float32)
    return high, middle, rest - middle


def exact_dot(left, right):
    rows = left.shape[0]
    high, middle, low = [part.astype(jnp.bfloat16) for part in split_in_three(left)]
    right_high, right_middle, right_low = [part.astype(jnp.bfloat16) for part in split_in_three(right)]
    first = dot_bf16(jnp.concatenate([high, middle, low], axis=0), right_high)
    second = dot_bf16(jnp.concatenate([high, middle], axis=0), right_middle)
    third = dot_bf16(high, right_low)
    small = first[2 * rows :] + (second[rows:] + third)
    return first[:rows] + (first[rows : 2 * rows] + second[:rows] + small)


def solve_with_factor(system):
    size, width = system.shape
    lanes = 128
    sub = lax.broadcasted_iota(jnp.int32, (BLOCK, lanes), 0)

    def wide(value):
        return jnp.concatenate([value] * (width // lanes), axis=1)

    def spread_row(value, j):
        return jnp.broadcast_to(value[j : j + 1], value.shape)

    def spread_columns(value, start):
        return [
            jnp.broadcast_to(value[:, start + k : start + k + 1], (BLOCK, lanes)) for k in range(BLOCK)
        ]

    panel = system[:BLOCK]
    rest = system[BLOCK:]
    done = []
    for start in range(0, size, BLOCK):
        after = start + BLOCK
        last = after == size
        columns = spread_columns(panel, start)
        if not last:
            following = rest[:BLOCK]
            next_columns = spread_columns(following, start)
        scale = None
        for j in range(BLOCK):
            root = lax.rsqrt(spread_row(columns[j], j))
            inverse = root * root
            for k in range(j + 1, BLOCK):
                ratio = spread_row(columns[j], k) * inverse
                columns[k] = columns[k] - columns[j] * ratio
                if not last:
                    next_columns[k] = next_columns[k] - next_columns[j] * ratio
            pivot_row = spread_row(panel, j) * wide(inverse)
            if j < BLOCK - 1:
                panel = panel - wide(jnp.where(sub > j, columns[j], 0.0)) * pivot_row
            if not last:
                following = following - wide(next_columns[j]) * pivot_row
            scale = root if scale is None else jnp.where(sub == j, root, scale)
        solved = panel * wide(scale)
        done.append(solved[:, lanes:])
        if last:
            break
        panel = following
        if after + BLOCK < size:
            high, middle, low = split_in_three(solved)
            left = jnp.concatenate([x[:, :lanes] for x in (high, high, middle, high, middle, low)], axis=0)
            left = left.T[after + BLOCK : size].astype(jnp.bfloat16)
            right = jnp.concatenate([high, middle, high, low, middle, high], axis=0).astype(jnp.bfloat16)
            rest = rest[BLOCK:] - dot_bf16(left, right)
    return jnp.concatenate(done, axis=0)


def basis_kernel(covariance_ref, test_ref, rows_ref, weights_ref):
    covariance = covariance_ref[...] * (1.0 / (ROWS_DEV * COLS))
    sketch = exact_dot(covariance, test_ref[...])
    image = exact_dot(covariance, sketch)
    turned = sketch.T[:RANK]
    system = exact_dot(turned, jnp.concatenate([image, covariance], axis=1))
    solved = solve_with_factor(jnp.concatenate([system, turned], axis=1))
    rows_ref[...] = solved[:, :FRAMES]
    weights_ref[...] = solved[:, FRAMES:]


def tile_basis(covariance, test_matrix):
    shape = pltpu.VMEM((RANK, FRAMES), jnp.float32)
    return pl.pallas_call(
        basis_kernel,
        in_specs=[vmem, vmem],
        out_specs=[vmem, vmem],
        out_shape=[shape, shape],
        name="basis",
    )(*near(covariance, test_matrix))


def merge_kernel(first_ref, own_ref, partner_ref, weights_ref, probe_ref, rows_ref, new_weights_ref):
    is_first = first_ref[0] == 1
    own = own_ref[...]
    partner = partner_ref[...]
    weights = weights_ref[...]
    stacked = jnp.concatenate([jnp.where(is_first, own, partner), jnp.where(is_first, partner, own)], axis=0)
    placed = jnp.concatenate([jnp.where(is_first, weights, 0.0), jnp.where(is_first, 0.0, weights)], axis=0)
    sketch = exact_dot(stacked, exact_dot(stacked.T, probe_ref[...]))
    system = exact_dot(sketch.T[:RANK], jnp.concatenate([sketch, stacked, placed], axis=1))
    solved = solve_with_factor(system)
    rows_ref[...] = solved[:, :FRAMES] * reduction_multiplier
    new_weights_ref[...] = solved[:, FRAMES:] * growth_multiplier


def merge(is_first, own, partner, weights, probe):
    shape = pltpu.VMEM((RANK, FRAMES), jnp.float32)
    return pl.pallas_call(
        merge_kernel,
        in_specs=[smem, vmem, vmem, vmem, vmem],
        out_specs=[vmem, vmem],
        out_shape=[shape, shape],
        name="merge",
    )(is_first, *near(own, partner, weights, probe))


def sum_over_tm(partial):
    parts = lax.axis_size("tm")
    height = partial.shape[0] // parts
    pieces = lax.all_to_all(partial.reshape(parts, height, -1), "tm", 0, 0, tiled=True)
    own = jnp.sum(pieces, axis=0, keepdims=True)
    whole = lax.all_to_all(jnp.broadcast_to(own, pieces.shape), "tm", 0, 0, tiled=True)
    return whole.reshape(partial.shape)


def body(movie_frames, depth_index, depth_width, temporal_test_matrix, merge_probe):
    frames = movie_frames.shape[0]
    parts = lax.axis_size("tm")
    count = lax.axis_size("pix")
    forward = [(i, i + 1) for i in range(count - 1)]
    backward = [(target, source) for source, target in forward]
    low = lax.ppermute(movie_frames[:, ROWS_DEV - HW :].reshape(frames * HW, COLS), "pix", forward)
    high = lax.ppermute(movie_frames[:, :HW].reshape(frames * HW, COLS), "pix", backward)
    matrix = smoothing_matrices(row_weights(depth_index, depth_width), frames)
    smoothed = smooth_tile(movie_frames, low, high, matrix, parts)
    columns = lax.all_to_all(smoothed, "tm", 0, 0, tiled=True)
    covariance = sum_over_tm(covariance_part(columns))
    spare = FRAMES - RANK
    test_matrix = jnp.pad(temporal_test_matrix, ((0, 0), (0, spare)))
    probe = jnp.pad(merge_probe, ((0, 0), (0, spare)))
    own_rows, weights = tile_basis(covariance, test_matrix)
    position = lax.axis_index("pix")
    for level in range(count.bit_length() - 1):
        pairs = [(source, source ^ (1 << level)) for source in range(count)]
        partner = lax.ppermute(own_rows, "pix", pairs)
        is_first = (1 - (position >> level & 1)).astype(jnp.int32).reshape(1)
        own_rows, weights = merge(is_first, own_rows, partner, weights, probe)
    loadings = loading_rows(weights, columns)
    own_times = lax.dynamic_slice_in_dim(own_rows, lax.axis_index("tm") * frames, frames, 1)
    return (own_times, loadings)


def solution(mesh):
    in_specs = (P("tm", "pix", None), P("pix"), P(), P(), P())
    out_specs = (P(None, "tm"), P(None, "pix", "tm"))
    return jax.shard_map(body, mesh=mesh, in_specs=in_specs, out_specs=out_specs, check_vma=False)
```

time: 238 us -> 176 us (0.74)
  the two profiles are of different devices: /device:TPU:8 before, /device:TPU:24 now
where the time goes in v2:
time: 176 us
  blocking collectives  72 us (41%)
  Pallas kernels  36.8 us (21%)
  waiting for transfers between devices  35.2 us (20%)
  starting transfers between devices  26.4 us (15%)
  local copies, waits for them, and re-layouts  3.36 us (2%)
    all_to_all x1, blocking collectives, body(): columns = lax.all_to_all(smoothed, 'tm', 0, 0, tiled=True)  60.2 us
    ppermute x5, waiting for transfers between devices, body(): partner = lax.ppermute(own_rows, 'pix', pairs)  20 us
    pallas_call x5, Pallas kernels, merge(): pl.pallas_call(merge_kernel, in_specs=[smem, vmem, vmem, vmem, vmem], out...  19.8 us
    ppermute x5, starting transfers between devices, body(): partner = lax.ppermute(own_rows, 'pix', pairs)  16.2 us
    all_to_all x1, blocking collectives, sum_over_tm(): lax.all_to_all(partial.reshape(parts, height, -1), 'tm', 0, 0, tiled=True)  11.8 us
    all_to_all x1, waiting for transfers between devices, sum_over_tm(): lax.all_to_all(jnp.broadcast_to(own, pieces.shape), 'tm', 0, 0, tiled=True)  7.65 us
    ppermute x1, waiting for transfers between devices, body(): lax.ppermute(movie_frames[:, :HW].reshape(frames * HW, COLS), 'pix', back...  5.4 us
    pallas_call x1, Pallas kernels, smooth_tile(): pl.pallas_call(smooth_kernel, grid=(parts // group,), in_specs=[pl.BlockS...  5.29 us
  transfers between devices with their start and end apart: 8, of which 8 were waited for; matrix products, arithmetic and copies ran while one was open for 1% of the time, Pallas kernels for 0%

profile of v2, /device:TPU:24, one launch (start us, length us, event | category | flops | bytes accessed | tf_op | source)
XLA Modules:
  0.0 175.8 jit_solution(17418261671702676336)
XLA Ops:
  0.6 1.5 fusion.24
  2.2 4.7 %collective-permute-start = (bf16[32,4096]{1,0:T(8,128)(2,1)S(1)}, bf16[32,4096]{1,0:T(8,128)(2,1)S(1)}, u32[]{:S(2)}, u32[]{:S(2)}) collective-permute-start(bf16[32,4096]{1,0:T(8,128)(2,1)S(1)} %reshape.80), channel_id=1, source_target_pairs={{0,16},{16,32},{32,48},{48,64},{64,80},{80,96},{96,112},{112,128},... | collective-permute-start | bytes 786440 | tf_op jit(solution)/shard_map/ppermute | solution.py:336
  7.0 1.9 %collective-permute-start.1 = (bf16[32,4096]{1,0:T(8,128)(2,1)S(1)}, bf16[32,4096]{1,0:T(8,128)(2,1)S(1)}, u32[]{:S(2)}, u32[]{:S(2)}) collective-permute-start(bf16[32,4096]{1,0:T(8,128)(2,1)S(1)} %reshape.81), channel_id=1, source_target_pairs={{16,0},{32,16},{48,32},{64,48},{80,64},{96,80},{112,96},{128,112},... | collective-permute-start | bytes 786440 | tf_op jit(solution)/shard_map/ppermute | solution.py:337
  9.2 0.3 fusion.10
  9.7 0.5 reduce-precision_convert_fusion
  10.3 2.2 %collective-permute-done.low_ref = bf16[32,4096]{1,0:T(8,128)(2,1)S(1)} collective-permute-done((bf16[32,4096]{1,0:T(8,128)(2,1)S(1)}, bf16[32,4096]{1,0:T(8,128)(2,1)S(1)}, u32[]{:S(2)}, u32[]{:S(2)}) %collective-permute-start) | collective-permute-done | bytes 262176 | tf_op jit(solution)/shard_map/ppermute | solution.py:336
  12.4 5.4 %collective-permute-done.1.high_ref = bf16[32,4096]{1,0:T(8,128)(2,1)S(1)} collective-permute-done((bf16[32,4096]{1,0:T(8,128)(2,1)S(1)}, bf16[32,4096]{1,0:T(8,128)(2,1)S(1)}, u32[]{:S(2)}, u32[]{:S(2)}) %collective-permute-start.1) | collective-permute-done | bytes 262176 | tf_op jit(solution)/shard_map/ppermute | solution.py:337
  17.8 5.3 %smooth.1 = bf16[16,256,256]{2,1,0:T(8,128)(2,1)} custom-call(bf16[8,32,4096]{2,1,0:T(8,128)(2,1)} %movie_ref.1, bf16[32,4096]{1,0:T(8,128)(2,1)S(1)} %collective-permute-done.low_ref, bf16[32,4096]{1,0:T(8,128)(2,1)S(1)} %collective-permute-done.1.high_ref, bf16[512,320]{1,0:T(8,128)(2,1)S(1)} %pad_maximum_fusion.matrix_ref), custom_call_target="tpu_custom_call" | custom-call | tf_op jit(solution)/shard_map/smooth/pallas_call | solution.py:89
  23.1 60.2 %all_to_all.15.data_ref = bf16[16,256,256]{2,1,0:T(8,128)(2,1)} all-to-all(bf16[16,256,256]{2,1,0:T(8,128)(2,1)} %smooth.1), channel_id=1, replica_groups=mesh['pix'=32,'tm'=16] {'tm'}, dimensions={0} | all-to-all | bytes 4194304 | tf_op jit(solution)/shard_map/all_to_all | solution.py:340
  83.3 3.6 %covariance.1 = f32[128,128]{1,0:T(8,128)S(1)} custom-call(bf16[16,256,256]{2,1,0:T(8,128)(2,1)} %all_to_all.15.data_ref), custom_call_target="tpu_custom_call" | custom-call | tf_op jit(solution)/shard_map/covariance/pallas_call | solution.py:142
  86.9 11.8 %all_to_all.16 = f32[16,8,128]{2,1,0:T(8,128)S(1)} all-to-all(f32[16,8,128]{2,1,0:T(8,128)S(1)} %bitcast.18), channel_id=1, replica_groups=mesh['pix'=32,'tm'=16] {'tm'}, dimensions={0} | all-to-all | bytes 131072 | tf_op jit(solution)/shard_map/all_to_all | solution.py:324
  98.8 0.6 broadcast_in_dim.128
  99.4 3.5 %all-to-all-start.2 = ((f32[16,8,128]{2,1,0:T(8,128)}), f32[16,8,128]{2,1,0:T(8,128)S(1)}, u32[]{:S(2)}, u32[]{:S(2)}) async-start(f32[16,8,128]{2,1,0:T(8,128)} %broadcast_in_dim.128), calls=%async_computation.2 | async-start | bytes 131072 | tf_op jit(solution)/shard_map/all_to_all | solution.py:326
  103.0 7.6 %all-to-all-done.2 = f32[16,8,128]{2,1,0:T(8,128)S(1)} async-done(((f32[16,8,128]{2,1,0:T(8,128)}), f32[16,8,128]{2,1,0:T(8,128)S(1)}, u32[]{:S(2)}, u32[]{:S(2)}) %all-to-all-start.2) | async-done | bytes 65568 | tf_op jit(solution)/shard_map/all_to_all | solution.py:326
  110.7 3.6 %basis.1 = (f32[96,128]{1,0:T(8,128)S(1)}, f32[96,128]{1,0:T(8,128)S(1)}) custom-call(f32[128,128]{1,0:T(8,128)S(1)} %bitcast.19, f32[128,128]{1,0:T(8,128)S(1)} %pad.8.test_ref), custom_call_target="tpu_custom_call" | custom-call | tf_op jit(solution)/shard_map/basis/pallas_call | solution.py:287
  114.3 1.9 %collective-permute-start.2 = (f32[96,128]{1,0:T(8,128)S(1)}, f32[96,128]{1,0:T(8,128)S(1)}, u32[]{:S(2)}, u32[]{:S(2)}) collective-permute-start(f32[96,128]{1,0:T(8,128)S(1)} %get-tuple-element.14.own_ref), channel_id=1, source_target_pairs={{0,16},{16,0},{32,48},{48,32},{64,80},{80,64},{96,112},{112,96},{1... | collective-permute-start | bytes 147464 | tf_op jit(solution)/shard_map/ppermute | solution.py:349
  116.3 4.0 %collective-permute-done.2.partner_ref = f32[96,128]{1,0:T(8,128)S(1)} collective-permute-done((f32[96,128]{1,0:T(8,128)S(1)}, f32[96,128]{1,0:T(8,128)S(1)}, u32[]{:S(2)}, u32[]{:S(2)}) %collective-permute-start.2) | collective-permute-done | bytes 49184 | tf_op jit(solution)/shard_map/ppermute | solution.py:349
  120.3 4.0 %merge.5 = (f32[96,128]{1,0:T(8,128)S(1)}, f32[96,128]{1,0:T(8,128)S(1)}) custom-call(s32[1]{0:T(128)} %bitcast.4.first_ref, f32[96,128]{1,0:T(8,128)S(1)} %get-tuple-element.14.own_ref, f32[96,128]{1,0:T(8,128)S(1)} %collective-permute-done.2.partner_ref, f32[96,128]{1,0:T(8,128)S(1)} %get-tuple-element.15.weights_ref, f32[192,128]{1,0:T(8,128)S(1)} %pad.9.probe_ref), custom_call_target="tpu_custom_call" | custom-call | tf_op jit(solution)/shard_map/merge/pallas_call | solution.py:312
  124.3 1.9 %collective-permute-start.3 = (f32[96,128]{1,0:T(8,128)S(1)}, f32[96,128]{1,0:T(8,128)S(1)}, u32[]{:S(2)}, u32[]{:S(2)}) collective-permute-start(f32[96,128]{1,0:T(8,128)S(1)} %get-tuple-element.16.own_ref), channel_id=1, source_target_pairs={{0,32},{16,48},{32,0},{48,16},{64,96},{80,112},{96,64},{112,80},{1... | collective-permute-start | bytes 147464 | tf_op jit(solution)/shard_map/ppermute | solution.py:349
  126.2 5.1 %collective-permute-done.3.partner_ref = f32[96,128]{1,0:T(8,128)S(1)} collective-permute-done((f32[96,128]{1,0:T(8,128)S(1)}, f32[96,128]{1,0:T(8,128)S(1)}, u32[]{:S(2)}, u32[]{:S(2)}) %collective-permute-start.3) | collective-permute-done | bytes 49184 | tf_op jit(solution)/shard_map/ppermute | solution.py:349
  131.3 4.0 %merge.6 = (f32[96,128]{1,0:T(8,128)S(1)}, f32[96,128]{1,0:T(8,128)S(1)}) custom-call(s32[1]{0:T(128)} %bitcast.3.first_ref, f32[96,128]{1,0:T(8,128)S(1)} %get-tuple-element.16.own_ref, f32[96,128]{1,0:T(8,128)S(1)} %collective-permute-done.3.partner_ref, f32[96,128]{1,0:T(8,128)S(1)} %get-tuple-element.17.weights_ref, f32[192,128]{1,0:T(8,128)S(1)} %pad.9.probe_ref), custom_call_target="tpu_custom_call" | custom-call | tf_op jit(solution)/shard_map/merge/pallas_call | solution.py:312
  135.3 3.9 %collective-permute-start.4 = (f32[96,128]{1,0:T(8,128)S(1)}, f32[96,128]{1,0:T(8,128)S(1)}, u32[]{:S(2)}, u32[]{:S(2)}) collective-permute-start(f32[96,128]{1,0:T(8,128)S(1)} %get-tuple-element.18.own_ref), channel_id=1, source_target_pairs={{0,64},{16,80},{32,96},{48,112},{64,0},{80,16},{96,32},{112,48},{1... | collective-permute-start | bytes 147464 | tf_op jit(solution)/shard_map/ppermute | solution.py:349
  139.1 6.0 %collective-permute-done.4.partner_ref = f32[96,128]{1,0:T(8,128)S(1)} collective-permute-done((f32[96,128]{1,0:T(8,128)S(1)}, f32[96,128]{1,0:T(8,128)S(1)}, u32[]{:S(2)}, u32[]{:S(2)}) %collective-permute-start.4) | collective-permute-done | bytes 49184 | tf_op jit(solution)/shard_map/ppermute | solution.py:349
  145.2 4.0 %merge.7 = (f32[96,128]{1,0:T(8,128)S(1)}, f32[96,128]{1,0:T(8,128)S(1)}) custom-call(s32[1]{0:T(128)} %bitcast.2.first_ref, f32[96,128]{1,0:T(8,128)S(1)} %get-tuple-element.18.own_ref, f32[96,128]{1,0:T(8,128)S(1)} %collective-permute-done.4.partner_ref, f32[96,128]{1,0:T(8,128)S(1)} %get-tuple-element.19.weights_ref, f32[192,128]{1,0:T(8,128)S(1)} %pad.9.probe_ref), custom_call_target="tpu_custom_call" | custom-call | tf_op jit(solution)/shard_map/merge/pallas_call | solution.py:312
  149.1 3.6 %collective-permute-start.5 = (f32[96,128]{1,0:T(8,128)S(1)}, f32[96,128]{1,0:T(8,128)S(1)}, u32[]{:S(2)}, u32[]{:S(2)}) collective-permute-start(f32[96,128]{1,0:T(8,128)S(1)} %get-tuple-element.20.own_ref), channel_id=1, source_target_pairs={{0,128},{16,144},{32,160},{48,176},{64,192},{80,208},{96,224},{112... | collective-permute-start | bytes 147464 | tf_op jit(solution)/shard_map/ppermute | solution.py:349
  152.7 2.4 %collective-permute-done.5.partner_ref = f32[96,128]{1,0:T(8,128)S(1)} collective-permute-done((f32[96,128]{1,0:T(8,128)S(1)}, f32[96,128]{1,0:T(8,128)S(1)}, u32[]{:S(2)}, u32[]{:S(2)}) %collective-permute-start.5) | collective-permute-done | bytes 49184 | tf_op jit(solution)/shard_map/ppermute | solution.py:349
  155.1 4.0 %merge.8 = (f32[96,128]{1,0:T(8,128)S(1)}, f32[96,128]{1,0:T(8,128)S(1)}) custom-call(s32[1]{0:T(128)} %bitcast.1.first_ref, f32[96,128]{1,0:T(8,128)S(1)} %get-tuple-element.20.own_ref, f32[96,128]{1,0:T(8,128)S(1)} %collective-permute-done.5.partner_ref, f32[96,128]{1,0:T(8,128)S(1)} %get-tuple-element.21.weights_ref, f32[192,128]{1,0:T(8,128)S(1)} %pad.9.probe_ref), custom_call_target="tpu_custom_call" | custom-call | tf_op jit(solution)/shard_map/merge/pallas_call | solution.py:312
  159.1 5.0 %collective-permute-start.6 = (f32[96,128]{1,0:T(8,128)S(1)}, f32[96,128]{1,0:T(8,128)S(1)}, u32[]{:S(2)}, u32[]{:S(2)}) collective-permute-start(f32[96,128]{1,0:T(8,128)S(1)} %get-tuple-element.22.own_ref), channel_id=1, source_target_pairs={{0,256},{16,272},{32,288},{48,304},{64,320},{80,336},{96,352},{112... | collective-permute-start | bytes 147464 | tf_op jit(solution)/shard_map/ppermute | solution.py:349
  164.0 2.5 %collective-permute-done.6.partner_ref = f32[96,128]{1,0:T(8,128)S(1)} collective-permute-done((f32[96,128]{1,0:T(8,128)S(1)}, f32[96,128]{1,0:T(8,128)S(1)}, u32[]{:S(2)}, u32[]{:S(2)}) %collective-permute-start.6) | collective-permute-done | bytes 49184 | tf_op jit(solution)/shard_map/ppermute | solution.py:349
  166.6 4.0 %merge.9 = (f32[96,128]{1,0:T(8,128)S(1)}, f32[96,128]{1,0:T(8,128)S(1)}) custom-call(s32[1]{0:T(128)} %bitcast.first_ref, f32[96,128]{1,0:T(8,128)S(1)} %get-tuple-element.22.own_ref, f32[96,128]{1,0:T(8,128)S(1)} %collective-permute-done.6.partner_ref, f32[96,128]{1,0:T(8,128)S(1)} %get-tuple-element.23.weights_ref, f32[192,128]{1,0:T(8,128)S(1)} %pad.9.probe_ref), custom_call_target="tpu_custom_call" | custom-call | tf_op jit(solution)/shard_map/merge/pallas_call | solution.py:312
  170.6 0.7 copy.15
  171.3 4.5 %loadings.1 = bf16[96,32,256]{2,1,0:T(8,128)(2,1)} custom-call(f32[96,128]{1,0:T(8,128)S(1)} %get-tuple-element.25.weights_ref, bf16[16,256,256]{2,1,0:T(8,128)(2,1)} %all_to_all.15.data_ref), custom_call_target="tpu_custom_call" | custom-call | tf_op jit(solution)/shard_map/loadings/pallas_call | solution.py:187
  (28 shorter events, 0.9 us)
Async XLA Ops:
  0.6 8.3 %copy-start.2 = (f32[6]{0:T(128)S(1)}, f32[6]{0:T(128)}, u32[]{:S(2)}) copy-start(f32[6]{0:T(128)} %param.7) | copy-start | bytes 76
  0.6 8.5 %copy-start.3 = (s32[32]{0:T(128)S(1)}, s32[32]{0:T(128)}, u32[]{:S(2)}) copy-start(s32[32]{0:T(128)} %param.6) | copy-start | bytes 388
  2.2 10.2 %collective-permute-start = (bf16[32,4096]{1,0:T(8,128)(2,1)S(1)}, bf16[32,4096]{1,0:T(8,128)(2,1)S(1)}, u32[]{:S(2)}, u32[]{:S(2)}) collective-permute-start(bf16[32,4096]{1,0:T(8,128)(2,1)S(1)} %reshape.80), channel_id=1, source_target_pairs={{0,16},{16,32},{32,48},{48,64},{64,80},{80,96},{96,112},{112,128},... | collective-permute-start | bytes 786440 | tf_op jit(solution)/shard_map/ppermute | solution.py:336
  7.0 10.9 %collective-permute-start.1 = (bf16[32,4096]{1,0:T(8,128)(2,1)S(1)}, bf16[32,4096]{1,0:T(8,128)(2,1)S(1)}, u32[]{:S(2)}, u32[]{:S(2)}) collective-permute-start(bf16[32,4096]{1,0:T(8,128)(2,1)S(1)} %reshape.81), channel_id=1, source_target_pairs={{16,0},{32,16},{48,32},{64,48},{80,64},{96,80},{112,96},{128,112},... | collective-permute-start | bytes 786440 | tf_op jit(solution)/shard_map/ppermute | solution.py:337
  83.3 19.6 %copy-start.1 = (f32[128,96]{0,1:T(8,128)S(1)}, f32[128,96]{0,1:T(8,128)}, u32[]{:S(2)}) copy-start(f32[128,96]{0,1:T(8,128)} %param.8) | copy-start | bytes 147460
  83.3 33.0 %copy-start = (f32[192,96]{1,0:T(8,128)S(1)}, f32[192,96]{1,0:T(8,128)}, u32[]{:S(2)}) copy-start(f32[192,96]{1,0:T(8,128)} %param.9) | copy-start | bytes 221188
  99.4 11.3 %all-to-all-start.2 = ((f32[16,8,128]{2,1,0:T(8,128)}), f32[16,8,128]{2,1,0:T(8,128)S(1)}, u32[]{:S(2)}, u32[]{:S(2)}) async-start(f32[16,8,128]{2,1,0:T(8,128)} %broadcast_in_dim.128), calls=%async_computation.2 | async-start | bytes 131072 | tf_op jit(solution)/shard_map/all_to_all | solution.py:326
  114.3 6.0 %collective-permute-start.2 = (f32[96,128]{1,0:T(8,128)S(1)}, f32[96,128]{1,0:T(8,128)S(1)}, u32[]{:S(2)}, u32[]{:S(2)}) collective-permute-start(f32[96,128]{1,0:T(8,128)S(1)} %get-tuple-element.14.own_ref), channel_id=1, source_target_pairs={{0,16},{16,0},{32,48},{48,32},{64,80},{80,64},{96,112},{112,96},{1... | collective-permute-start | bytes 147464 | tf_op jit(solution)/shard_map/ppermute | solution.py:349
  124.3 7.0 %collective-permute-start.3 = (f32[96,128]{1,0:T(8,128)S(1)}, f32[96,128]{1,0:T(8,128)S(1)}, u32[]{:S(2)}, u32[]{:S(2)}) collective-permute-start(f32[96,128]{1,0:T(8,128)S(1)} %get-tuple-element.16.own_ref), channel_id=1, source_target_pairs={{0,32},{16,48},{32,0},{48,16},{64,96},{80,112},{96,64},{112,80},{1... | collective-permute-start | bytes 147464 | tf_op jit(solution)/shard_map/ppermute | solution.py:349
  135.3 9.9 %collective-permute-start.4 = (f32[96,128]{1,0:T(8,128)S(1)}, f32[96,128]{1,0:T(8,128)S(1)}, u32[]{:S(2)}, u32[]{:S(2)}) collective-permute-start(f32[96,128]{1,0:T(8,128)S(1)} %get-tuple-element.18.own_ref), channel_id=1, source_target_pairs={{0,64},{16,80},{32,96},{48,112},{64,0},{80,16},{96,32},{112,48},{1... | collective-permute-start | bytes 147464 | tf_op jit(solution)/shard_map/ppermute | solution.py:349
  149.1 6.0 %collective-permute-start.5 = (f32[96,128]{1,0:T(8,128)S(1)}, f32[96,128]{1,0:T(8,128)S(1)}, u32[]{:S(2)}, u32[]{:S(2)}) collective-permute-start(f32[96,128]{1,0:T(8,128)S(1)} %get-tuple-element.20.own_ref), channel_id=1, source_target_pairs={{0,128},{16,144},{32,160},{48,176},{64,192},{80,208},{96,224},{112... | collective-permute-start | bytes 147464 | tf_op jit(solution)/shard_map/ppermute | solution.py:349
  159.1 7.5 %collective-permute-start.6 = (f32[96,128]{1,0:T(8,128)S(1)}, f32[96,128]{1,0:T(8,128)S(1)}, u32[]{:S(2)}, u32[]{:S(2)}) collective-permute-start(f32[96,128]{1,0:T(8,128)S(1)} %get-tuple-element.22.own_ref), channel_id=1, source_target_pairs={{0,256},{16,272},{32,288},{48,304},{64,320},{80,336},{96,352},{112... | collective-permute-start | bytes 147464 | tf_op jit(solution)/shard_map/ppermute | solution.py:349

commit v3 on v2

--- a/solution.py
+++ b/solution.py
@@ -47,41 +47,64 @@
 
 
 def smoothing_matrices(weights, frames):
-    rows = ROWS_DEV * frames
-    spread = jnp.repeat(weights, frames, axis=0)
-    out_row = (jnp.arange(rows) // frames)[:, None]
-    out_frame = (jnp.arange(rows) % frames)[:, None]
-    halo = jnp.arange(2 * frames * HW)
-    frame_in = jnp.concatenate([jnp.arange(rows) // ROWS_DEV, halo // HW % frames])[None, :]
-    row_in = jnp.concatenate(
-        [jnp.arange(rows) % ROWS_DEV + HW, halo % HW + jnp.where(halo < frames * HW, 0, HW + ROWS_DEV)]
-    )[None, :]
-    tap = jnp.where(frame_in == out_frame, row_in - out_row, -1)
-    matrix = jnp.zeros(tap.shape, jnp.float32)
-    for offset in range(2 * HW + 1):
-        matrix = matrix + jnp.where(tap == offset, spread[:, offset : offset + 1], 0.0)
-    high, low = split_bf16(matrix)
-    return jnp.concatenate([high, low], axis=0)
+    def matrix(spread, out_row, out_frame, in_row, in_frame):
+        tap = jnp.where(in_frame[None, :] == out_frame[:, None], in_row[None, :] - out_row[:, None], -1)
+        total = jnp.zeros(tap.shape, jnp.float32)
+        for offset in range(2 * HW + 1):
+            total = total + jnp.where(tap == offset, spread[:, offset : offset + 1], 0.0)
+        high, low = split_bf16(total)
+        return jnp.concatenate([high, low], axis=0)
+
+    index = jnp.arange(frames * ROWS_DEV)
+    own = matrix(
+        jnp.repeat(weights, frames, axis=0),
+        index // frames,
+        index % frames,
+        index % ROWS_DEV + HW,
+        index // ROWS_DEV,
+    )
+    index = jnp.arange(frames * HW)
+    edge_rows = index // frames
+    sides = [
+        matrix(
+            jnp.repeat(weights[first : first + HW], frames, axis=0),
+            edge_rows + first,
+            index % frames,
+            index % HW + (first + 2 * HW if first else 0),
+            index // HW,
+        )
+        for first in (0, ROWS_DEV - HW)
+    ]
+    return own, jnp.concatenate(sides, axis=0)
 
 
 def dot_bf16(left, right):
     return lax.dot_general(left, right, (((1,), (0,)), ((), ())), preferred_element_type=jnp.float32)
 
 
-def smooth_kernel(movie_ref, low_ref, high_ref, matrix_ref, out_ref):
+def smooth_kernel(movie_ref, low_ref, high_ref, own_ref, edge_ref, out_ref):
     frames, rows, cols = movie_ref.shape
     count, out_rows, width = out_ref.shape
     start = pl.program_id(0) * cols
-    matrix = matrix_ref[...]
+    own = own_ref[...]
+    edge = edge_ref.shape[0] // 4
+    low_matrix = edge_ref[: 2 * edge]
+    high_matrix = edge_ref[2 * edge :]
     for part in range(count):
         movie = movie_ref[:, :, part * width : (part + 1) * width].reshape(frames * rows, width)
         lanes = pl.ds(pl.multiple_of(start + part * width, width), width)
-        data = jnp.concatenate([movie, low_ref[:, lanes], high_ref[:, lanes]], axis=0)
-        both = dot_bf16(matrix, data)
-        out_ref[part] = (both[:out_rows] + both[out_rows:]).astype(jnp.bfloat16)
-
-
-def smooth_tile(movie, low, high, matrix, parts):
+        both = dot_bf16(own, movie)
+        total = both[:out_rows] + both[out_rows:]
+        low = dot_bf16(low_matrix, low_ref[:, lanes])
+        high = dot_bf16(high_matrix, high_ref[:, lanes])
+        out_ref[part, :edge] = (total[:edge] + (low[:edge] + low[edge:])).astype(jnp.bfloat16)
+        out_ref[part, edge : out_rows - edge] = total[edge : out_rows - edge].astype(jnp.bfloat16)
+        out_ref[part, out_rows - edge :] = (
+            total[out_rows - edge :] + (high[:edge] + high[edge:])
+        ).astype(jnp.bfloat16)
+
+
+def smooth_tile(movie, low, high, matrices, parts):
     frames = movie.shape[0]
     width = COLS // parts
     rows = frames * ROWS_DEV
@@ -94,11 +117,12 @@
             vmem,
             vmem,
             vmem,
+            vmem,
         ],
         out_specs=pl.BlockSpec((group, rows, width), lambda i: (i, 0, 0)),
         out_shape=jax.ShapeDtypeStruct((parts, rows, width), jnp.bfloat16),
         name="smooth",
-    )(movie, *near(low, high, matrix))
+    )(movie, *near(low, high, *matrices))
 
 
 def spread_selector(parity, frames):
@@ -216,8 +240,8 @@
     return first[:rows] + (first[rows : 2 * rows] + second[:rows] + small)
 
 
-def solve_with_factor(system):
-    size, width = system.shape
+def solve_with_factors(systems):
+    size, width = systems[0].shape
     lanes = 128
     sub = lax.broadcasted_iota(jnp.int32, (BLOCK, lanes), 0)
 
@@ -232,43 +256,65 @@
             jnp.broadcast_to(value[:, start + k : start + k + 1], (BLOCK, lanes)) for k in range(BLOCK)
         ]
 
-    panel = system[:BLOCK]
-    rest = system[BLOCK:]
-    done = []
+    total = range(len(systems))
+    panel = [system[:BLOCK] for system in systems]
+    rest = [system[BLOCK:] for system in systems]
+    done = [[] for _ in total]
     for start in range(0, size, BLOCK):
         after = start + BLOCK
         last = after == size
-        columns = spread_columns(panel, start)
+        columns = [spread_columns(panel[i], start) for i in total]
         if not last:
-            following = rest[:BLOCK]
-            next_columns = spread_columns(following, start)
-        scale = None
+            following = [rest[i][:BLOCK] for i in total]
+            next_columns = [spread_columns(following[i], start) for i in total]
+        scale = [None for _ in total]
         for j in range(BLOCK):
-            root = lax.rsqrt(spread_row(columns[j], j))
-            inverse = root * root
-            for k in range(j + 1, BLOCK):
-                ratio = spread_row(columns[j], k) * inverse
-                columns[k] = columns[k] - columns[j] * ratio
+            for i in total:
+                own = columns[i]
+                root = lax.rsqrt(spread_row(own[j], j))
+                inverse = root * root
+                for k in range(j + 1, BLOCK):
+                    ratio = spread_row(own[j], k) * inverse
+                    own[k] = own[k] - own[j] * ratio
+                    if not last:
+                        next_columns[i][k] = next_columns[i][k] - next_columns[i][j] * ratio
+                pivot_row = spread_row(panel[i], j) * wide(inverse)
+                if j < BLOCK - 1:
+                    panel[i] = panel[i] - wide(jnp.where(sub > j, own[j], 0.0)) * pivot_row
                 if not last:
-                    next_columns[k] = next_columns[k] - next_columns[j] * ratio
-            pivot_row = spread_row(panel, j) * wide(inverse)
-            if j < BLOCK - 1:
-                panel = panel - wide(jnp.where(sub > j, columns[j], 0.0)) * pivot_row
-            if not last:
-                following = following - wide(next_columns[j]) * pivot_row
-            scale = root if scale is None else jnp.where(sub == j, root, scale)
-        solved = panel * wide(scale)
-        done.append(solved[:, lanes:])
-        if last:
-            break
-        panel = following
-        if after + BLOCK < size:
-            high, middle, low = split_in_three(solved)
-            left = jnp.concatenate([x[:, :lanes] for x in (high, high, middle, high, middle, low)], axis=0)
-            left = left.T[after + BLOCK : size].astype(jnp.bfloat16)
-            right = jnp.concatenate([high, middle, high, low, middle, high], axis=0).astype(jnp.bfloat16)
-            rest = rest[BLOCK:] - dot_bf16(left, right)
-    return jnp.concatenate(done, axis=0)
+                    following[i] = following[i] - wide(next_columns[i][j]) * pivot_row
+                scale[i] = root if scale[i] is None else jnp.where(sub == j, root, scale[i])
+        for i in total:
+            solved = panel[i] * wide(scale[i])
+            done[i].append(solved[:, lanes:])
+            if last:
+                continue
+            panel[i] = following[i]
+            if after + BLOCK < size:
+                high, middle, low = split_in_three(solved)
+                left = jnp.concatenate(
+                    [part[:, :lanes] for part in (high, high, middle, high, middle, low)], axis=0
+                )
+                left = left.T[after + BLOCK : size].astype(jnp.bfloat16)
+                right = jnp.concatenate([high, middle, high, low, middle, high], axis=0)
+                rest[i] = rest[i][BLOCK:] - dot_bf16(left, right.astype(jnp.bfloat16))
+    return [jnp.concatenate(rows, axis=0) for rows in done]
+
+
+def store_rows(rows_ref, rows):
+    if len(rows_ref.shape) == 2:
+        rows_ref[...] = rows
+    else:
+        for copy in range(rows_ref.shape[0]):
+            rows_ref[copy] = rows
+
+
+def rows_and_weights(copies):
+    shape = (RANK, FRAMES) if copies == 1 else (copies, RANK, FRAMES)
+    return dict(
+        out_specs=[vmem, vmem],
+        out_shape=[pltpu.VMEM(shape, jnp.float32), pltpu.VMEM((RANK, FRAMES), jnp.float32)],
+    )
 
 
 def basis_kernel(covariance_ref, test_ref, rows_ref, weights_ref):
@@ -277,45 +323,65 @@
     image = exact_dot(covariance, sketch)
     turned = sketch.T[:RANK]
     system = exact_dot(turned, jnp.concatenate([image, covariance], axis=1))
-    solved = solve_with_factor(jnp.concatenate([system, turned], axis=1))
-    rows_ref[...] = solved[:, :FRAMES]
+    (solved,) = solve_with_factors([jnp.concatenate([system, turned], axis=1)])
+    store_rows(rows_ref, solved[:, :FRAMES])
     weights_ref[...] = solved[:, FRAMES:]
 
 
-def tile_basis(covariance, test_matrix):
-    shape = pltpu.VMEM((RANK, FRAMES), jnp.float32)
-    return pl.pallas_call(
-        basis_kernel,
-        in_specs=[vmem, vmem],
-        out_specs=[vmem, vmem],
-        out_shape=[shape, shape],
-        name="basis",
+def tile_basis(covariance, test_matrix, copies=1):
+    return pl.pallas_call(
+        basis_kernel, in_specs=[vmem, vmem], name="basis", **rows_and_weights(copies)
     )(*near(covariance, test_matrix))
 
 
-def merge_kernel(first_ref, own_ref, partner_ref, weights_ref, probe_ref, rows_ref, new_weights_ref):
-    is_first = first_ref[0] == 1
+def merge_nodes(stacks, placed, probe):
+    systems = []
+    for stacked, weights in zip(stacks, placed):
+        sketch = exact_dot(stacked, exact_dot(stacked.T, probe))
+        systems.append(exact_dot(sketch.T[:RANK], jnp.concatenate([sketch, stacked, weights], axis=1)))
+    solved = solve_with_factors(systems)
+    rows = [result[:, :FRAMES] * reduction_multiplier for result in solved]
+    weights = sum([result[:, FRAMES:] for result in solved[1:]], solved[0][:, FRAMES:])
+    return rows, weights * growth_multiplier
+
+
+def place(weights, first, second):
+    return jnp.concatenate([jnp.where(first, weights, 0.0), jnp.where(second, weights, 0.0)], axis=0)
+
+
+def merge_kernel(place_ref, own_ref, partner_ref, weights_ref, probe_ref, rows_ref, new_weights_ref):
+    is_first = place_ref[0] == 0
     own = own_ref[...]
     partner = partner_ref[...]
+    stacked = jnp.concatenate([jnp.where(is_first, own, partner), jnp.where(is_first, partner, own)], axis=0)
+    placed = place(weights_ref[...], is_first, jnp.logical_not(is_first))
+    (rows,), weights = merge_nodes([stacked], [placed], probe_ref[...])
+    store_rows(rows_ref, rows)
+    new_weights_ref[...] = weights
+
+
+def merge(place_in, own, partner, weights, probe, copies=1):
+    return pl.pallas_call(
+        merge_kernel, in_specs=[smem, vmem, vmem, vmem, vmem], name="merge", **rows_and_weights(copies)
+    )(place_in, *near(own, partner, weights, probe))
+
+
+def merge_four_kernel(place_ref, rows_in_ref, weights_ref, probe_ref, rows_ref, new_weights_ref):
+    spot = place_ref[0]
+    probe = probe_ref[...]
     weights = weights_ref[...]
-    stacked = jnp.concatenate([jnp.where(is_first, own, partner), jnp.where(is_first, partner, own)], axis=0)
-    placed = jnp.concatenate([jnp.where(is_first, weights, 0.0), jnp.where(is_first, 0.0, weights)], axis=0)
-    sketch = exact_dot(stacked, exact_dot(stacked.T, probe_ref[...]))
-    system = exact_dot(sketch.T[:RANK], jnp.concatenate([sketch, stacked, placed], axis=1))
-    solved = solve_with_factor(system)
-    rows_ref[...] = solved[:, :FRAMES] * reduction_multiplier
-    new_weights_ref[...] = solved[:, FRAMES:] * growth_multiplier
-
-
-def merge(is_first, own, partner, weights, probe):
-    shape = pltpu.VMEM((RANK, FRAMES), jnp.float32)
-    return pl.pallas_call(
-        merge_kernel,
-        in_specs=[smem, vmem, vmem, vmem, vmem],
-        out_specs=[vmem, vmem],
-        out_shape=[shape, shape],
-        name="merge",
-    )(is_first, *near(own, partner, weights, probe))
+    stacks = [rows_in_ref[2 * m : 2 * m + 2].reshape(2 * RANK, FRAMES) for m in range(2)]
+    placed = [place(weights, spot == 2 * m, spot == 2 * m + 1) for m in range(2)]
+    rows, weights = merge_nodes(stacks, placed, probe)
+    (rows,), weights = merge_nodes([jnp.concatenate(rows, axis=0)], [place(weights, spot < 2, spot >= 2)], probe)
+    store_rows(rows_ref, rows)
+    new_weights_ref[...] = weights
+
+
+def merge_four(place_in, gathered, weights, probe, copies=1):
+    return pl.pallas_call(
+        merge_four_kernel, in_specs=[smem, vmem, vmem, vmem], name="merge_four", **rows_and_weights(copies)
+    )(place_in, *near(gathered, weights, probe))
 
 
 def sum_over_tm(partial):
@@ -335,22 +401,37 @@
     backward = [(target, source) for source, target in forward]
     low = lax.ppermute(movie_frames[:, ROWS_DEV - HW :].reshape(frames * HW, COLS), "pix", forward)
     high = lax.ppermute(movie_frames[:, :HW].reshape(frames * HW, COLS), "pix", backward)
-    matrix = smoothing_matrices(row_weights(depth_index, depth_width), frames)
-    smoothed = smooth_tile(movie_frames, low, high, matrix, parts)
+    matrices = smoothing_matrices(row_weights(depth_index, depth_width), frames)
+    smoothed = smooth_tile(movie_frames, low, high, matrices, parts)
     columns = lax.all_to_all(smoothed, "tm", 0, 0, tiled=True)
     covariance = sum_over_tm(covariance_part(columns))
     spare = FRAMES - RANK
     test_matrix = jnp.pad(temporal_test_matrix, ((0, 0), (0, spare)))
     probe = jnp.pad(merge_probe, ((0, 0), (0, spare)))
-    own_rows, weights = tile_basis(covariance, test_matrix)
-    position = lax.axis_index("pix")
-    for level in range(count.bit_length() - 1):
-        pairs = [(source, source ^ (1 << level)) for source in range(count)]
-        partner = lax.ppermute(own_rows, "pix", pairs)
-        is_first = (1 - (position >> level & 1)).astype(jnp.int32).reshape(1)
-        own_rows, weights = merge(is_first, own_rows, partner, weights, probe)
+    position = lax.axis_index("pix").astype(jnp.int32)
+    levels = count.bit_length() - 1
+    sizes = []
+    while sum(sizes) < levels:
+        sizes.append(2 if levels - sum(sizes) > 1 and sizes[-1:] != [2] else 1)
+    copies = [4 if size == 2 else 1 for size in sizes[1:]] + [1]
+    rows, weights = tile_basis(covariance, test_matrix, 4 if sizes[0] == 2 else 1)
+    level = 0
+    for size, next_copies in zip(sizes, copies):
+        spot = (position >> level & (2**size - 1)).reshape(1)
+        if size == 2:
+            step = 1 << level
+            groups = [
+                [base + k * step for k in range(4)] for base in range(count) if not base & (3 * step)
+            ]
+            gathered = lax.all_to_all(rows, "pix", 0, 0, tiled=True, axis_index_groups=groups)
+            rows, weights = merge_four(spot, gathered, weights, probe, next_copies)
+        else:
+            pairs = [(source, source ^ (1 << level)) for source in range(count)]
+            partner = lax.ppermute(rows, "pix", pairs)
+            rows, weights = merge(spot, rows, partner, weights, probe, next_copies)
+        level += size
     loadings = loading_rows(weights, columns)
-    own_times = lax.dynamic_slice_in_dim(own_rows, lax.axis_index("tm") * frames, frames, 1)
+    own_times = lax.dynamic_slice_in_dim(rows, lax.axis_index("tm") * frames, frames, 1)
     return (own_times, loadings)
 
 

time: 176 us -> 176 us (level)
  the two profiles are of different devices: /device:TPU:24 before, /device:TPU:2 now
where the time goes in v3:
time: 176 us; the launch traced here: 175 us
  blocking collectives  72 us (41%)
  Pallas kernels  40 us (23%)
  waiting for transfers between devices  29.4 us (17%)
  starting transfers between devices  27.6 us (16%)
  local copies, waits for them, and re-layouts  3.89 us (2%)
    all_to_all x1, blocking collectives, body(): columns = lax.all_to_all(smoothed, 'tm', 0, 0, tiled=True)  60.2 us
    pallas_call x2, Pallas kernels, merge_four(): pl.pallas_call(merge_four_kernel, in_specs=[smem, vmem, vmem, vmem], name...  18.1 us
    all_to_all x2, waiting for transfers between devices, body(): lax.all_to_all(rows, 'pix', 0, 0, tiled=True, axis_index_groups=groups)  12.8 us
    all_to_all x2, starting transfers between devices, body(): lax.all_to_all(rows, 'pix', 0, 0, tiled=True, axis_index_groups=groups)  12.1 us
    all_to_all x1, blocking collectives, sum_over_tm(): lax.all_to_all(partial.reshape(parts, height, -1), 'tm', 0, 0, tiled=True)  11.8 us
    all_to_all x1, waiting for transfers between devices, sum_over_tm(): lax.all_to_all(jnp.broadcast_to(own, pieces.shape), 'tm', 0, 0, tiled=True)  7.65 us
    ppermute x1, waiting for transfers between devices, body(): partner = lax.ppermute(rows, 'pix', pairs)  5.83 us
    pallas_call x1, Pallas kernels, smooth_tile(): pl.pallas_call(smooth_kernel, grid=(parts // group,), in_specs=[pl.BlockS...  4.81 us
  transfers between devices with their start and end apart: 6, of which 6 were waited for; matrix products, arithmetic and copies ran while one was open for 1% of the time, Pallas kernels for 0%

profile of v3, /device:TPU:2, one launch (start us, length us, event | category | flops | bytes accessed | tf_op | source)
XLA Modules:
  0.0 175.0 jit_solution(7145308359615667011)
XLA Ops:
  0.6 1.5 fusion.42
  2.2 3.5 %collective-permute-start = (bf16[32,4096]{1,0:T(8,128)(2,1)S(1)}, bf16[32,4096]{1,0:T(8,128)(2,1)S(1)}, u32[]{:S(2)}, u32[]{:S(2)}) collective-permute-start(bf16[32,4096]{1,0:T(8,128)(2,1)S(1)} %reshape.147), channel_id=1, source_target_pairs={{0,16},{16,32},{32,48},{48,64},{64,80},{80,96},{96,112},{112,128},... | collective-permute-start | bytes 786440 | tf_op jit(solution)/shard_map/ppermute | solution.py:402
  5.8 4.5 %collective-permute-start.1 = (bf16[32,4096]{1,0:T(8,128)(2,1)S(1)}, bf16[32,4096]{1,0:T(8,128)(2,1)S(1)}, u32[]{:S(2)}, u32[]{:S(2)}) collective-permute-start(bf16[32,4096]{1,0:T(8,128)(2,1)S(1)} %reshape.148), channel_id=1, source_target_pairs={{16,0},{32,16},{48,32},{64,48},{80,64},{96,80},{112,96},{128,112},... | collective-permute-start | bytes 786440 | tf_op jit(solution)/shard_map/ppermute | solution.py:403
  10.3 0.2 fusion.33
  10.5 0.3 fusion.30
  10.8 0.1 broadcast_in_dim.270
  11.0 0.1 reshape.149
  11.5 0.1 reduce-precision_convert_fusion.2
  11.6 0.1 reduce-precision_convert_fusion.1
  11.8 0.1 copy.17.edge_ref
  11.9 0.4 reduce-precision_convert_fusion
  12.4 1.9 %collective-permute-done.low_ref = bf16[32,4096]{1,0:T(8,128)(2,1)S(1)} collective-permute-done((bf16[32,4096]{1,0:T(8,128)(2,1)S(1)}, bf16[32,4096]{1,0:T(8,128)(2,1)S(1)}, u32[]{:S(2)}, u32[]{:S(2)}) %collective-permute-start) | collective-permute-done | bytes 262176 | tf_op jit(solution)/shard_map/ppermute | solution.py:402
  14.2 1.2 collective-permute-done.1.high_ref
  15.5 4.8 %smooth.1 = bf16[16,256,256]{2,1,0:T(8,128)(2,1)} custom-call(bf16[8,32,4096]{2,1,0:T(8,128)(2,1)} %movie_ref.1, bf16[32,4096]{1,0:T(8,128)(2,1)S(1)} %collective-permute-done.low_ref, bf16[32,4096]{1,0:T(8,128)(2,1)S(1)} %collective-permute-done.1.high_ref, bf16[512,256]{1,0:T(8,128)(2,1)S(1)} %pad_maximum_fusion.own_ref, bf16[128,32]{1,0:T(8,128)(2,1)S(1)} %copy.17.edge_ref), custom_call_target="tpu_custom_call" | custom-call | tf_op jit(solution)/shard_map/smooth/pallas_call | solution.py:112
  20.3 60.2 %all_to_all.25.data_ref = bf16[16,256,256]{2,1,0:T(8,128)(2,1)} all-to-all(bf16[16,256,256]{2,1,0:T(8,128)(2,1)} %smooth.1), channel_id=1, replica_groups=mesh['pix'=32,'tm'=16] {'tm'}, dimensions={0} | all-to-all | bytes 4194304 | tf_op jit(solution)/shard_map/all_to_all | solution.py:406
  80.5 3.6 %covariance.1 = f32[128,128]{1,0:T(8,128)S(1)} custom-call(bf16[16,256,256]{2,1,0:T(8,128)(2,1)} %all_to_all.25.data_ref), custom_call_target="tpu_custom_call" | custom-call | tf_op jit(solution)/shard_map/covariance/pallas_call | solution.py:166
  84.1 11.8 %all_to_all.26 = f32[16,8,128]{2,1,0:T(8,128)S(1)} all-to-all(f32[16,8,128]{2,1,0:T(8,128)S(1)} %bitcast.56), channel_id=1, replica_groups=mesh['pix'=32,'tm'=16] {'tm'}, dimensions={0} | all-to-all | bytes 131072 | tf_op jit(solution)/shard_map/all_to_all | solution.py:390
  96.0 0.6 broadcast_in_dim.330
  96.6 3.5 %all-to-all-start.2 = ((f32[16,8,128]{2,1,0:T(8,128)}), f32[16,8,128]{2,1,0:T(8,128)S(1)}, u32[]{:S(2)}, u32[]{:S(2)}) async-start(f32[16,8,128]{2,1,0:T(8,128)} %broadcast_in_dim.330), calls=%async_computation.2 | async-start | bytes 131072 | tf_op jit(solution)/shard_map/all_to_all | solution.py:392
  100.2 7.6 %all-to-all-done.2 = f32[16,8,128]{2,1,0:T(8,128)S(1)} async-done(((f32[16,8,128]{2,1,0:T(8,128)}), f32[16,8,128]{2,1,0:T(8,128)S(1)}, u32[]{:S(2)}, u32[]{:S(2)}) %all-to-all-start.2) | async-done | bytes 65568 | tf_op jit(solution)/shard_map/all_to_all | solution.py:392
  107.9 4.3 %basis.1 = (f32[4,96,128]{2,1,0:T(8,128)}, f32[96,128]{1,0:T(8,128)S(1)}) custom-call(f32[128,128]{1,0:T(8,128)S(1)} %bitcast.57, f32[128,128]{1,0:T(8,128)S(1)} %pad.8.test_ref), custom_call_target="tpu_custom_call" | custom-call | tf_op jit(solution)/shard_map/basis/pallas_call | solution.py:332
  112.2 7.2 %all-to-all-start.3 = ((f32[4,96,128]{2,1,0:T(8,128)}), f32[4,96,128]{2,1,0:T(8,128)S(1)}, u32[]{:S(2)}, u32[]{:S(2)}) async-start(f32[4,96,128]{2,1,0:T(8,128)} %get-tuple-element.10), calls=%async_computation.3 | async-start | bytes 393216 | tf_op jit(solution)/shard_map/all_to_all | solution.py:426
  119.4 8.0 %all-to-all-done.3.rows_in_ref = f32[4,96,128]{2,1,0:T(8,128)S(1)} async-done(((f32[4,96,128]{2,1,0:T(8,128)}), f32[4,96,128]{2,1,0:T(8,128)S(1)}, u32[]{:S(2)}, u32[]{:S(2)}) %all-to-all-start.3) | async-done | bytes 196640 | tf_op jit(solution)/shard_map/all_to_all | solution.py:426
  127.4 9.0 %merge_four.2 = (f32[96,128]{1,0:T(8,128)S(1)}, f32[96,128]{1,0:T(8,128)S(1)}) custom-call(s32[1]{0:T(128)} %bitcast.2.place_ref, f32[4,96,128]{2,1,0:T(8,128)S(1)} %all-to-all-done.3.rows_in_ref, f32[96,128]{1,0:T(8,128)S(1)} %get-tuple-element.11.weights_ref, f32[192,128]{1,0:T(8,128)S(1)} %pad.9.probe_ref), custom_call_target="tpu_custom_call" | custom-call | tf_op jit(solution)/shard_map/merge_four/pallas_call | solution.py:382
  136.5 4.1 %collective-permute-start.2 = (f32[96,128]{1,0:T(8,128)S(1)}, f32[96,128]{1,0:T(8,128)S(1)}, u32[]{:S(2)}, u32[]{:S(2)}) collective-permute-start(f32[96,128]{1,0:T(8,128)S(1)} %get-tuple-element.12.own_ref), channel_id=1, source_target_pairs={{0,64},{16,80},{32,96},{48,112},{64,0},{80,16},{96,32},{112,48},{1... | collective-permute-start | bytes 147464 | tf_op jit(solution)/shard_map/ppermute | solution.py:430
  140.5 5.8 %collective-permute-done.2.partner_ref = f32[96,128]{1,0:T(8,128)S(1)} collective-permute-done((f32[96,128]{1,0:T(8,128)S(1)}, f32[96,128]{1,0:T(8,128)S(1)}, u32[]{:S(2)}, u32[]{:S(2)}) %collective-permute-start.2) | collective-permute-done | bytes 49184 | tf_op jit(solution)/shard_map/ppermute | solution.py:430
  146.3 4.7 %merge.1 = (f32[4,96,128]{2,1,0:T(8,128)}, f32[96,128]{1,0:T(8,128)S(1)}) custom-call(s32[1]{0:T(128)} %bitcast.1.place_ref, f32[96,128]{1,0:T(8,128)S(1)} %get-tuple-element.12.own_ref, f32[96,128]{1,0:T(8,128)S(1)} %collective-permute-done.2.partner_ref, f32[96,128]{1,0:T(8,128)S(1)} %get-tuple-element.13.weights_ref, f32[192,128]{1,0:T(8,128)S(1)} %pad.9.probe_ref), custom_call_target="tpu_custom_call" | custom-call | tf_op jit(solution)/shard_map/merge/pallas_call | solution.py:364
  151.0 4.8 %all-to-all-start.4 = ((f32[4,96,128]{2,1,0:T(8,128)}), f32[4,96,128]{2,1,0:T(8,128)S(1)}, u32[]{:S(2)}, u32[]{:S(2)}) async-start(f32[4,96,128]{2,1,0:T(8,128)} %get-tuple-element.14), calls=%async_computation.4 | async-start | bytes 393216 | tf_op jit(solution)/shard_map/all_to_all | solution.py:426
  155.9 4.9 %all-to-all-done.4.rows_in_ref = f32[4,96,128]{2,1,0:T(8,128)S(1)} async-done(((f32[4,96,128]{2,1,0:T(8,128)}), f32[4,96,128]{2,1,0:T(8,128)S(1)}, u32[]{:S(2)}, u32[]{:S(2)}) %all-to-all-start.4) | async-done | bytes 196640 | tf_op jit(solution)/shard_map/all_to_all | solution.py:426
  160.7 9.1 %merge_four.3 = (f32[96,128]{1,0:T(8,128)S(1)}, f32[96,128]{1,0:T(8,128)S(1)}) custom-call(s32[1]{0:T(128)} %bitcast.place_ref, f32[4,96,128]{2,1,0:T(8,128)S(1)} %all-to-all-done.4.rows_in_ref, f32[96,128]{1,0:T(8,128)S(1)} %get-tuple-element.15.weights_ref, f32[192,128]{1,0:T(8,128)S(1)} %pad.9.probe_ref), custom_call_target="tpu_custom_call" | custom-call | tf_op jit(solution)/shard_map/merge_four/pallas_call | solution.py:382
  169.9 0.7 copy.19
  170.5 4.5 %loadings.1 = bf16[96,32,256]{2,1,0:T(8,128)(2,1)} custom-call(f32[96,128]{1,0:T(8,128)S(1)} %get-tuple-element.17.weights_ref, bf16[16,256,256]{2,1,0:T(8,128)(2,1)} %all_to_all.25.data_ref), custom_call_target="tpu_custom_call" | custom-call | tf_op jit(solution)/shard_map/loadings/pallas_call | solution.py:211
  (32 shorter events, 0.9 us)
Async XLA Ops:
  0.6 9.7 %copy-start.2 = (f32[6]{0:T(128)S(1)}, f32[6]{0:T(128)}, u32[]{:S(2)}) copy-start(f32[6]{0:T(128)} %param.7) | copy-start | bytes 76
  0.6 9.9 %copy-start.3 = (s32[32]{0:T(128)S(1)}, s32[32]{0:T(128)}, u32[]{:S(2)}) copy-start(s32[32]{0:T(128)} %param.6) | copy-start | bytes 388
  2.2 12.0 %collective-permute-start = (bf16[32,4096]{1,0:T(8,128)(2,1)S(1)}, bf16[32,4096]{1,0:T(8,128)(2,1)S(1)}, u32[]{:S(2)}, u32[]{:S(2)}) collective-permute-start(bf16[32,4096]{1,0:T(8,128)(2,1)S(1)} %reshape.147), channel_id=1, source_target_pairs={{0,16},{16,32},{32,48},{48,64},{64,80},{80,96},{96,112},{112,128},... | collective-permute-start | bytes 786440 | tf_op jit(solution)/shard_map/ppermute | solution.py:402
  5.8 9.7 %collective-permute-start.1 = (bf16[32,4096]{1,0:T(8,128)(2,1)S(1)}, bf16[32,4096]{1,0:T(8,128)(2,1)S(1)}, u32[]{:S(2)}, u32[]{:S(2)}) collective-permute-start(bf16[32,4096]{1,0:T(8,128)(2,1)S(1)} %reshape.148), channel_id=1, source_target_pairs={{16,0},{32,16},{48,32},{64,48},{80,64},{96,80},{112,96},{128,112},... | collective-permute-start | bytes 786440 | tf_op jit(solution)/shard_map/ppermute | solution.py:403
  80.5 19.6 %copy-start.1 = (f32[128,96]{0,1:T(8,128)S(1)}, f32[128,96]{0,1:T(8,128)}, u32[]{:S(2)}) copy-start(f32[128,96]{0,1:T(8,128)} %param.8) | copy-start | bytes 147460
  80.5 38.9 %copy-start = (f32[192,96]{1,0:T(8,128)S(1)}, f32[192,96]{1,0:T(8,128)}, u32[]{:S(2)}) copy-start(f32[192,96]{1,0:T(8,128)} %param.9) | copy-start | bytes 221188
  96.6 11.3 %all-to-all-start.2 = ((f32[16,8,128]{2,1,0:T(8,128)}), f32[16,8,128]{2,1,0:T(8,128)S(1)}, u32[]{:S(2)}, u32[]{:S(2)}) async-start(f32[16,8,128]{2,1,0:T(8,128)} %broadcast_in_dim.330), calls=%async_computation.2 | async-start | bytes 131072 | tf_op jit(solution)/shard_map/all_to_all | solution.py:392
  112.2 15.2 %all-to-all-start.3 = ((f32[4,96,128]{2,1,0:T(8,128)}), f32[4,96,128]{2,1,0:T(8,128)S(1)}, u32[]{:S(2)}, u32[]{:S(2)}) async-start(f32[4,96,128]{2,1,0:T(8,128)} %get-tuple-element.10), calls=%async_computation.3 | async-start | bytes 393216 | tf_op jit(solution)/shard_map/all_to_all | solution.py:426
  136.5 9.9 %collective-permute-start.2 = (f32[96,128]{1,0:T(8,128)S(1)}, f32[96,128]{1,0:T(8,128)S(1)}, u32[]{:S(2)}, u32[]{:S(2)}) collective-permute-start(f32[96,128]{1,0:T(8,128)S(1)} %get-tuple-element.12.own_ref), channel_id=1, source_target_pairs={{0,64},{16,80},{32,96},{48,112},{64,0},{80,16},{96,32},{112,48},{1... | collective-permute-start | bytes 147464 | tf_op jit(solution)/shard_map/ppermute | solution.py:430
  151.0 9.7 %all-to-all-start.4 = ((f32[4,96,128]{2,1,0:T(8,128)}), f32[4,96,128]{2,1,0:T(8,128)S(1)}, u32[]{:S(2)}, u32[]{:S(2)}) async-start(f32[4,96,128]{2,1,0:T(8,128)} %get-tuple-element.14), calls=%async_computation.4 | async-start | bytes 393216 | tf_op jit(solution)/shard_map/all_to_all | solution.py:426

commit v4 on v3

--- a/solution.py
+++ b/solution.py
@@ -16,7 +16,7 @@
 BLOCK = 8
 SMOOTH_GROUP = 4
 PAIR_GROUP = 4
-LOADING_ROWS = 8
+LOADING_ROWS = 16
 
 highest = lax.Precision.HIGHEST
 reduction_multiplier = math.sqrt(0.5)
@@ -82,47 +82,58 @@
     return lax.dot_general(left, right, (((1,), (0,)), ((), ())), preferred_element_type=jnp.float32)
 
 
-def smooth_kernel(movie_ref, low_ref, high_ref, own_ref, edge_ref, out_ref):
-    frames, rows, cols = movie_ref.shape
+def smooth_kernel(movie_ref, own_ref, out_ref, edges_ref):
+    frames, rows, _ = movie_ref.shape
     count, out_rows, width = out_ref.shape
-    start = pl.program_id(0) * cols
+    edge = edges_ref.shape[1] // 2
+    start = pl.program_id(0) * count
     own = own_ref[...]
-    edge = edge_ref.shape[0] // 4
-    low_matrix = edge_ref[: 2 * edge]
-    high_matrix = edge_ref[2 * edge :]
     for part in range(count):
         movie = movie_ref[:, :, part * width : (part + 1) * width].reshape(frames * rows, width)
-        lanes = pl.ds(pl.multiple_of(start + part * width, width), width)
         both = dot_bf16(own, movie)
         total = both[:out_rows] + both[out_rows:]
-        low = dot_bf16(low_matrix, low_ref[:, lanes])
-        high = dot_bf16(high_matrix, high_ref[:, lanes])
-        out_ref[part, :edge] = (total[:edge] + (low[:edge] + low[edge:])).astype(jnp.bfloat16)
-        out_ref[part, edge : out_rows - edge] = total[edge : out_rows - edge].astype(jnp.bfloat16)
-        out_ref[part, out_rows - edge :] = (
-            total[out_rows - edge :] + (high[:edge] + high[edge:])
-        ).astype(jnp.bfloat16)
+        out_ref[part] = total.astype(jnp.bfloat16)
+        edges_ref[start + part, :edge] = total[:edge]
+        edges_ref[start + part, edge:] = total[out_rows - edge :]
+
+
+def edge_kernel(_, edges_ref, low_ref, high_ref, matrix_ref, out_ref):
+    count, edge, width = out_ref.shape
+    side = pl.program_id(0)
+    rows = pl.ds(pl.multiple_of(side * edge, edge), edge)
+    matrix = matrix_ref[pl.ds(pl.multiple_of(side * 2 * edge, 2 * edge), 2 * edge), :]
+    for part in range(count):
+        lanes = slice(part * width, (part + 1) * width)
+        halo = jnp.where(side == 0, low_ref[:, lanes], high_ref[:, lanes])
+        both = dot_bf16(matrix, halo)
+        out_ref[part] = (edges_ref[part, rows, :] + (both[:edge] + both[edge:])).astype(jnp.bfloat16)
 
 
 def smooth_tile(movie, low, high, matrices, parts):
     frames = movie.shape[0]
     width = COLS // parts
     rows = frames * ROWS_DEV
+    edge = frames * HW
     group = SMOOTH_GROUP
-    return pl.pallas_call(
+    own, sides = matrices
+    shape = jax.ShapeDtypeStruct((parts, rows, width), jnp.bfloat16)
+    smoothed, edges = pl.pallas_call(
         smooth_kernel,
         grid=(parts // group,),
-        in_specs=[
-            pl.BlockSpec((frames, ROWS_DEV, group * width), lambda i: (0, 0, i)),
-            vmem,
-            vmem,
-            vmem,
-            vmem,
-        ],
-        out_specs=pl.BlockSpec((group, rows, width), lambda i: (i, 0, 0)),
-        out_shape=jax.ShapeDtypeStruct((parts, rows, width), jnp.bfloat16),
+        in_specs=[pl.BlockSpec((frames, ROWS_DEV, group * width), lambda i: (0, 0, i)), vmem],
+        out_specs=[pl.BlockSpec((group, rows, width), lambda i: (i, 0, 0)), vmem],
+        out_shape=[shape, pltpu.VMEM((parts, 2 * edge, width), jnp.float32)],
         name="smooth",
-    )(movie, *near(low, high, *matrices))
+    )(movie, *near(own))
+    return pl.pallas_call(
+        edge_kernel,
+        grid=(2,),
+        in_specs=[pl.BlockSpec(memory_space=pl.ANY), vmem, vmem, vmem, vmem],
+        out_specs=pl.BlockSpec((parts, edge, width), lambda i: (0, i * (rows // edge - 1), 0)),
+        out_shape=shape,
+        input_output_aliases={0: 0},
+        name="edges",
+    )(smoothed, *near(edges, low, high, sides))
 
 
 def spread_selector(parity, frames):
@@ -412,7 +423,7 @@
     levels = count.bit_length() - 1
     sizes = []
     while sum(sizes) < levels:
-        sizes.append(2 if levels - sum(sizes) > 1 and sizes[-1:] != [2] else 1)
+        sizes.append(2 if levels - sum(sizes) == 2 else 1)
     copies = [4 if size == 2 else 1 for size in sizes[1:]] + [1]
     rows, weights = tile_basis(covariance, test_matrix, 4 if sizes[0] == 2 else 1)
     level = 0

time: 176 us -> 171 us (0.972)
  the two profiles are of different devices: /device:TPU:2 before, /device:TPU:24 now
where the time goes in v4:
time: 171 us
  blocking collectives  72 us (42%)
  Pallas kernels  38.6 us (23%)
  waiting for transfers between devices  31.8 us (19%)
  starting transfers between devices  22.1 us (13%)
  local copies, waits for them, and re-layouts  3.89 us (2%)
    all_to_all x1, blocking collectives, body(): columns = lax.all_to_all(smoothed, 'tm', 0, 0, tiled=True)  60.2 us
    ppermute x3, waiting for transfers between devices, body(): partner = lax.ppermute(rows, 'pix', pairs)  15.7 us
    pallas_call x3, Pallas kernels, merge(): pl.pallas_call(merge_kernel, in_specs=[smem, vmem, vmem, vmem, vmem], nam...  12.6 us
    all_to_all x1, blocking collectives, sum_over_tm(): lax.all_to_all(partial.reshape(parts, height, -1), 'tm', 0, 0, tiled=True)  11.8 us
    pallas_call x1, Pallas kernels, merge_four(): pl.pallas_call(merge_four_kernel, in_specs=[smem, vmem, vmem, vmem], name...  9.05 us
    ppermute x3, starting transfers between devices, body(): partner = lax.ppermute(rows, 'pix', pairs)  7.7 us
    all_to_all x1, waiting for transfers between devices, sum_over_tm(): lax.all_to_all(jnp.broadcast_to(own, pieces.shape), 'tm', 0, 0, tiled=True)  7.65 us
    all_to_all x1, waiting for transfers between devices, body(): lax.all_to_all(rows, 'pix', 0, 0, tiled=True, axis_index_groups=groups)  6.33 us
  transfers between devices with their start and end apart: 7, of which 6 were waited for; matrix products, arithmetic and copies ran while one was open for 1% of the time, Pallas kernels for 3%

profile of v4, /device:TPU:24, one launch (start us, length us, event | category | flops | bytes accessed | tf_op | source)
XLA Modules:
  0.0 170.7 jit_solution(17476720667253651304)
XLA Ops:
  0.6 1.5 fusion.42
  2.2 4.7 %collective-permute-start = (bf16[32,4096]{1,0:T(8,128)(2,1)S(1)}, bf16[32,4096]{1,0:T(8,128)(2,1)S(1)}, u32[]{:S(2)}, u32[]{:S(2)}) collective-permute-start(bf16[32,4096]{1,0:T(8,128)(2,1)S(1)} %reshape.152), channel_id=1, source_target_pairs={{0,16},{16,32},{32,48},{48,64},{64,80},{80,96},{96,112},{112,128},... | collective-permute-start | bytes 786440 | tf_op jit(solution)/shard_map/ppermute | solution.py:413
  7.0 1.9 %collective-permute-start.1 = (bf16[32,4096]{1,0:T(8,128)(2,1)S(1)}, bf16[32,4096]{1,0:T(8,128)(2,1)S(1)}, u32[]{:S(2)}, u32[]{:S(2)}) collective-permute-start(bf16[32,4096]{1,0:T(8,128)(2,1)S(1)} %reshape.153), channel_id=1, source_target_pairs={{16,0},{32,16},{48,32},{64,48},{80,64},{96,80},{112,96},{128,112},... | collective-permute-start | bytes 786440 | tf_op jit(solution)/shard_map/ppermute | solution.py:414
  9.0 0.2 fusion.33
  9.2 0.3 fusion.30
  9.6 0.1 reshape.151
  9.8 0.4 reduce-precision_convert_fusion
  10.3 4.6 %smooth.1 = (bf16[16,256,256]{2,1,0:T(8,128)(2,1)}, f32[16,64,256]{2,1,0:T(8,128)S(1)}) custom-call(bf16[8,32,4096]{2,1,0:T(8,128)(2,1)} %movie_ref.1, bf16[512,256]{1,0:T(8,128)(2,1)S(1)} %pad_maximum_fusion.own_ref), custom_call_target="tpu_custom_call" | custom-call | tf_op jit(solution)/shard_map/smooth/pallas_call | solution.py:120
  15.5 0.1 copy.18.matrix_ref
  15.6 2.2 %collective-permute-done.1.high_ref = bf16[32,4096]{1,0:T(8,128)(2,1)S(1)} collective-permute-done((bf16[32,4096]{1,0:T(8,128)(2,1)S(1)}, bf16[32,4096]{1,0:T(8,128)(2,1)S(1)}, u32[]{:S(2)}, u32[]{:S(2)}) %collective-permute-start.1) | collective-permute-done | bytes 262176 | tf_op jit(solution)/shard_map/ppermute | solution.py:414
  17.8 1.3 edges.1
  19.1 60.2 %all_to_all.20.data_ref = bf16[16,256,256]{2,1,0:T(8,128)(2,1)} all-to-all(bf16[16,256,256]{2,1,0:T(8,128)(2,1)} %edges.1), channel_id=1, replica_groups=mesh['pix'=32,'tm'=16] {'tm'}, dimensions={0} | all-to-all | bytes 4194304 | tf_op jit(solution)/shard_map/all_to_all | solution.py:417
  79.3 3.6 %covariance.1 = f32[128,128]{1,0:T(8,128)S(1)} custom-call(bf16[16,256,256]{2,1,0:T(8,128)(2,1)} %all_to_all.20.data_ref), custom_call_target="tpu_custom_call" | custom-call | tf_op jit(solution)/shard_map/covariance/pallas_call | solution.py:177
  82.9 11.8 %all_to_all.21 = f32[16,8,128]{2,1,0:T(8,128)S(1)} all-to-all(f32[16,8,128]{2,1,0:T(8,128)S(1)} %bitcast.57), channel_id=1, replica_groups=mesh['pix'=32,'tm'=16] {'tm'}, dimensions={0} | all-to-all | bytes 131072 | tf_op jit(solution)/shard_map/all_to_all | solution.py:401
  94.8 0.6 broadcast_in_dim.330
  95.4 3.5 %all-to-all-start.2 = ((f32[16,8,128]{2,1,0:T(8,128)}), f32[16,8,128]{2,1,0:T(8,128)S(1)}, u32[]{:S(2)}, u32[]{:S(2)}) async-start(f32[16,8,128]{2,1,0:T(8,128)} %broadcast_in_dim.330), calls=%async_computation.2 | async-start | bytes 131072 | tf_op jit(solution)/shard_map/all_to_all | solution.py:403
  99.1 7.6 %all-to-all-done.2 = f32[16,8,128]{2,1,0:T(8,128)S(1)} async-done(((f32[16,8,128]{2,1,0:T(8,128)}), f32[16,8,128]{2,1,0:T(8,128)S(1)}, u32[]{:S(2)}, u32[]{:S(2)}) %all-to-all-start.2) | async-done | bytes 65568 | tf_op jit(solution)/shard_map/all_to_all | solution.py:403
  106.7 3.6 %basis.1 = (f32[96,128]{1,0:T(8,128)S(1)}, f32[96,128]{1,0:T(8,128)S(1)}) custom-call(f32[128,128]{1,0:T(8,128)S(1)} %bitcast.58, f32[128,128]{1,0:T(8,128)S(1)} %pad.8.test_ref), custom_call_target="tpu_custom_call" | custom-call | tf_op jit(solution)/shard_map/basis/pallas_call | solution.py:343
  110.3 1.9 %collective-permute-start.2 = (f32[96,128]{1,0:T(8,128)S(1)}, f32[96,128]{1,0:T(8,128)S(1)}, u32[]{:S(2)}, u32[]{:S(2)}) collective-permute-start(f32[96,128]{1,0:T(8,128)S(1)} %get-tuple-element.16.own_ref), channel_id=1, source_target_pairs={{0,16},{16,0},{32,48},{48,32},{64,80},{80,64},{96,112},{112,96},{1... | collective-permute-start | bytes 147464 | tf_op jit(solution)/shard_map/ppermute | solution.py:441
  112.3 4.0 %collective-permute-done.2.partner_ref = f32[96,128]{1,0:T(8,128)S(1)} collective-permute-done((f32[96,128]{1,0:T(8,128)S(1)}, f32[96,128]{1,0:T(8,128)S(1)}, u32[]{:S(2)}, u32[]{:S(2)}) %collective-permute-start.2) | collective-permute-done | bytes 49184 | tf_op jit(solution)/shard_map/ppermute | solution.py:441
  116.3 4.0 %merge.3 = (f32[96,128]{1,0:T(8,128)S(1)}, f32[96,128]{1,0:T(8,128)S(1)}) custom-call(s32[1]{0:T(128)} %bitcast.3.place_ref, f32[96,128]{1,0:T(8,128)S(1)} %get-tuple-element.16.own_ref, f32[96,128]{1,0:T(8,128)S(1)} %collective-permute-done.2.partner_ref, f32[96,128]{1,0:T(8,128)S(1)} %get-tuple-element.17.weights_ref, f32[192,128]{1,0:T(8,128)S(1)} %pad.9.probe_ref), custom_call_target="tpu_custom_call" | custom-call | tf_op jit(solution)/shard_map/merge/pallas_call | solution.py:375
  120.3 1.9 %collective-permute-start.3 = (f32[96,128]{1,0:T(8,128)S(1)}, f32[96,128]{1,0:T(8,128)S(1)}, u32[]{:S(2)}, u32[]{:S(2)}) collective-permute-start(f32[96,128]{1,0:T(8,128)S(1)} %get-tuple-element.18.own_ref), channel_id=1, source_target_pairs={{0,32},{16,48},{32,0},{48,16},{64,96},{80,112},{96,64},{112,80},{1... | collective-permute-start | bytes 147464 | tf_op jit(solution)/shard_map/ppermute | solution.py:441
  122.2 5.1 %collective-permute-done.3.partner_ref = f32[96,128]{1,0:T(8,128)S(1)} collective-permute-done((f32[96,128]{1,0:T(8,128)S(1)}, f32[96,128]{1,0:T(8,128)S(1)}, u32[]{:S(2)}, u32[]{:S(2)}) %collective-permute-start.3) | collective-permute-done | bytes 49184 | tf_op jit(solution)/shard_map/ppermute | solution.py:441
  127.3 4.0 %merge.4 = (f32[96,128]{1,0:T(8,128)S(1)}, f32[96,128]{1,0:T(8,128)S(1)}) custom-call(s32[1]{0:T(128)} %bitcast.2.place_ref, f32[96,128]{1,0:T(8,128)S(1)} %get-tuple-element.18.own_ref, f32[96,128]{1,0:T(8,128)S(1)} %collective-permute-done.3.partner_ref, f32[96,128]{1,0:T(8,128)S(1)} %get-tuple-element.19.weights_ref, f32[192,128]{1,0:T(8,128)S(1)} %pad.9.probe_ref), custom_call_target="tpu_custom_call" | custom-call | tf_op jit(solution)/shard_map/merge/pallas_call | solution.py:375
  131.3 3.9 %collective-permute-start.4 = (f32[96,128]{1,0:T(8,128)S(1)}, f32[96,128]{1,0:T(8,128)S(1)}, u32[]{:S(2)}, u32[]{:S(2)}) collective-permute-start(f32[96,128]{1,0:T(8,128)S(1)} %get-tuple-element.20.own_ref), channel_id=1, source_target_pairs={{0,64},{16,80},{32,96},{48,112},{64,0},{80,16},{96,32},{112,48},{1... | collective-permute-start | bytes 147464 | tf_op jit(solution)/shard_map/ppermute | solution.py:441
  135.2 6.5 %collective-permute-done.4.partner_ref = f32[96,128]{1,0:T(8,128)S(1)} collective-permute-done((f32[96,128]{1,0:T(8,128)S(1)}, f32[96,128]{1,0:T(8,128)S(1)}, u32[]{:S(2)}, u32[]{:S(2)}) %collective-permute-start.4) | collective-permute-done | bytes 49184 | tf_op jit(solution)/shard_map/ppermute | solution.py:441
  141.7 4.7 %merge.5 = (f32[4,96,128]{2,1,0:T(8,128)}, f32[96,128]{1,0:T(8,128)S(1)}) custom-call(s32[1]{0:T(128)} %bitcast.1.place_ref, f32[96,128]{1,0:T(8,128)S(1)} %get-tuple-element.20.own_ref, f32[96,128]{1,0:T(8,128)S(1)} %collective-permute-done.4.partner_ref, f32[96,128]{1,0:T(8,128)S(1)} %get-tuple-element.21.weights_ref, f32[192,128]{1,0:T(8,128)S(1)} %pad.9.probe_ref), custom_call_target="tpu_custom_call" | custom-call | tf_op jit(solution)/shard_map/merge/pallas_call | solution.py:375
  146.4 4.3 %all-to-all-start.3 = ((f32[4,96,128]{2,1,0:T(8,128)}), f32[4,96,128]{2,1,0:T(8,128)S(1)}, u32[]{:S(2)}, u32[]{:S(2)}) async-start(f32[4,96,128]{2,1,0:T(8,128)} %get-tuple-element.22), calls=%async_computation.3 | async-start | bytes 393216 | tf_op jit(solution)/shard_map/all_to_all | solution.py:437
  150.6 6.3 %all-to-all-done.3.rows_in_ref = f32[4,96,128]{2,1,0:T(8,128)S(1)} async-done(((f32[4,96,128]{2,1,0:T(8,128)}), f32[4,96,128]{2,1,0:T(8,128)S(1)}, u32[]{:S(2)}, u32[]{:S(2)}) %all-to-all-start.3) | async-done | bytes 196640 | tf_op jit(solution)/shard_map/all_to_all | solution.py:437
  157.0 9.0 %merge_four.1 = (f32[96,128]{1,0:T(8,128)S(1)}, f32[96,128]{1,0:T(8,128)S(1)}) custom-call(s32[1]{0:T(128)} %bitcast.place_ref, f32[4,96,128]{2,1,0:T(8,128)S(1)} %all-to-all-done.3.rows_in_ref, f32[96,128]{1,0:T(8,128)S(1)} %get-tuple-element.23.weights_ref, f32[192,128]{1,0:T(8,128)S(1)} %pad.9.probe_ref), custom_call_target="tpu_custom_call" | custom-call | tf_op jit(solution)/shard_map/merge_four/pallas_call | solution.py:393
  166.1 0.7 copy.20
  166.8 3.9 %loadings.1 = bf16[96,32,256]{2,1,0:T(8,128)(2,1)} custom-call(f32[96,128]{1,0:T(8,128)S(1)} %get-tuple-element.25.weights_ref, bf16[16,256,256]{2,1,0:T(8,128)(2,1)} %all_to_all.20.data_ref), custom_call_target="tpu_custom_call" | custom-call | tf_op jit(solution)/shard_map/loadings/pallas_call | solution.py:222
  (36 shorter events, 1.2 us)
Async XLA Ops:
  0.6 8.3 %copy-start.2 = (f32[6]{0:T(128)S(1)}, f32[6]{0:T(128)}, u32[]{:S(2)}) copy-start(f32[6]{0:T(128)} %param.7) | copy-start | bytes 76
  0.6 8.5 %copy-start.3 = (s32[32]{0:T(128)S(1)}, s32[32]{0:T(128)}, u32[]{:S(2)}) copy-start(s32[32]{0:T(128)} %param.6) | copy-start | bytes 388
  2.2 13.4 %collective-permute-start = (bf16[32,4096]{1,0:T(8,128)(2,1)S(1)}, bf16[32,4096]{1,0:T(8,128)(2,1)S(1)}, u32[]{:S(2)}, u32[]{:S(2)}) collective-permute-start(bf16[32,4096]{1,0:T(8,128)(2,1)S(1)} %reshape.152), channel_id=1, source_target_pairs={{0,16},{16,32},{32,48},{48,64},{64,80},{80,96},{96,112},{112,128},... | collective-permute-start | bytes 786440 | tf_op jit(solution)/shard_map/ppermute | solution.py:413
  7.0 10.9 %collective-permute-start.1 = (bf16[32,4096]{1,0:T(8,128)(2,1)S(1)}, bf16[32,4096]{1,0:T(8,128)(2,1)S(1)}, u32[]{:S(2)}, u32[]{:S(2)}) collective-permute-start(bf16[32,4096]{1,0:T(8,128)(2,1)S(1)} %reshape.153), channel_id=1, source_target_pairs={{16,0},{32,16},{48,32},{64,48},{80,64},{96,80},{112,96},{128,112},... | collective-permute-start | bytes 786440 | tf_op jit(solution)/shard_map/ppermute | solution.py:414
  79.3 19.6 %copy-start.1 = (f32[128,96]{0,1:T(8,128)S(1)}, f32[128,96]{0,1:T(8,128)}, u32[]{:S(2)}) copy-start(f32[128,96]{0,1:T(8,128)} %param.8) | copy-start | bytes 147460
  79.3 33.0 %copy-start = (f32[192,96]{1,0:T(8,128)S(1)}, f32[192,96]{1,0:T(8,128)}, u32[]{:S(2)}) copy-start(f32[192,96]{1,0:T(8,128)} %param.9) | copy-start | bytes 221188
  95.4 11.3 %all-to-all-start.2 = ((f32[16,8,128]{2,1,0:T(8,128)}), f32[16,8,128]{2,1,0:T(8,128)S(1)}, u32[]{:S(2)}, u32[]{:S(2)}) async-start(f32[16,8,128]{2,1,0:T(8,128)} %broadcast_in_dim.330), calls=%async_computation.2 | async-start | bytes 131072 | tf_op jit(solution)/shard_map/all_to_all | solution.py:403
  110.3 6.0 %collective-permute-start.2 = (f32[96,128]{1,0:T(8,128)S(1)}, f32[96,128]{1,0:T(8,128)S(1)}, u32[]{:S(2)}, u32[]{:S(2)}) collective-permute-start(f32[96,128]{1,0:T(8,128)S(1)} %get-tuple-element.16.own_ref), channel_id=1, source_target_pairs={{0,16},{16,0},{32,48},{48,32},{64,80},{80,64},{96,112},{112,96},{1... | collective-permute-start | bytes 147464 | tf_op jit(solution)/shard_map/ppermute | solution.py:441
  120.3 7.0 %collective-permute-start.3 = (f32[96,128]{1,0:T(8,128)S(1)}, f32[96,128]{1,0:T(8,128)S(1)}, u32[]{:S(2)}, u32[]{:S(2)}) collective-permute-start(f32[96,128]{1,0:T(8,128)S(1)} %get-tuple-element.18.own_ref), channel_id=1, source_target_pairs={{0,32},{16,48},{32,0},{48,16},{64,96},{80,112},{96,64},{112,80},{1... | collective-permute-start | bytes 147464 | tf_op jit(solution)/shard_map/ppermute | solution.py:441
  131.3 10.4 %collective-permute-start.4 = (f32[96,128]{1,0:T(8,128)S(1)}, f32[96,128]{1,0:T(8,128)S(1)}, u32[]{:S(2)}, u32[]{:S(2)}) collective-permute-start(f32[96,128]{1,0:T(8,128)S(1)} %get-tuple-element.20.own_ref), channel_id=1, source_target_pairs={{0,64},{16,80},{32,96},{48,112},{64,0},{80,16},{96,32},{112,48},{1... | collective-permute-start | bytes 147464 | tf_op jit(solution)/shard_map/ppermute | solution.py:441
  146.4 10.6 %all-to-all-start.3 = ((f32[4,96,128]{2,1,0:T(8,128)}), f32[4,96,128]{2,1,0:T(8,128)S(1)}, u32[]{:S(2)}, u32[]{:S(2)}) async-start(f32[4,96,128]{2,1,0:T(8,128)} %get-tuple-element.22), calls=%async_computation.3 | async-start | bytes 393216 | tf_op jit(solution)/shard_map/all_to_all | solution.py:437

commit v5 on v4

--- a/solution.py
+++ b/solution.py
@@ -15,7 +15,7 @@
 NDEPTH = 6
 BLOCK = 8
 SMOOTH_GROUP = 4
-PAIR_GROUP = 4
+PAIR_GROUP = 8
 LOADING_ROWS = 16
 
 highest = lax.Precision.HIGHEST
@@ -330,13 +330,16 @@
 
 def basis_kernel(covariance_ref, test_ref, rows_ref, weights_ref):
     covariance = covariance_ref[...] * (1.0 / (ROWS_DEV * COLS))
+    largest = jnp.max(jnp.max(covariance, axis=0, keepdims=True), axis=1, keepdims=True)
+    root = lax.rsqrt(largest)
+    covariance = covariance * root * root
     sketch = exact_dot(covariance, test_ref[...])
     image = exact_dot(covariance, sketch)
     turned = sketch.T[:RANK]
     system = exact_dot(turned, jnp.concatenate([image, covariance], axis=1))
     (solved,) = solve_with_factors([jnp.concatenate([system, turned], axis=1)])
-    store_rows(rows_ref, solved[:, :FRAMES])
-    weights_ref[...] = solved[:, FRAMES:]
+    store_rows(rows_ref, solved[:, :FRAMES] * (largest * root))
+    weights_ref[...] = solved[:, FRAMES:] * root
 
 
 def tile_basis(covariance, test_matrix, copies=1):
@@ -377,21 +380,33 @@
     )(place_in, *near(own, partner, weights, probe))
 
 
-def merge_four_kernel(place_ref, rows_in_ref, weights_ref, probe_ref, rows_ref, new_weights_ref):
+def merge_four_kernel(
+    place_ref, rows_in_ref, weights_ref, probe_ref, times_ref, new_weights_ref, turned_ref
+):
     spot = place_ref[0]
+    frames = times_ref.shape[0]
     probe = probe_ref[...]
     weights = weights_ref[...]
     stacks = [rows_in_ref[2 * m : 2 * m + 2].reshape(2 * RANK, FRAMES) for m in range(2)]
     placed = [place(weights, spot == 2 * m, spot == 2 * m + 1) for m in range(2)]
     rows, weights = merge_nodes(stacks, placed, probe)
     (rows,), weights = merge_nodes([jnp.concatenate(rows, axis=0)], [place(weights, spot < 2, spot >= 2)], probe)
-    store_rows(rows_ref, rows)
     new_weights_ref[...] = weights
-
-
-def merge_four(place_in, gathered, weights, probe, copies=1):
-    return pl.pallas_call(
-        merge_four_kernel, in_specs=[smem, vmem, vmem, vmem], name="merge_four", **rows_and_weights(copies)
+    turned_ref[...] = rows.T
+    times_ref[...] = turned_ref[pl.ds(pl.multiple_of(place_ref[1] * frames, frames), frames), :]
+
+
+def merge_four(place_in, gathered, weights, probe, frames):
+    return pl.pallas_call(
+        merge_four_kernel,
+        in_specs=[smem, vmem, vmem, vmem],
+        out_specs=[vmem, vmem],
+        out_shape=[
+            jax.ShapeDtypeStruct((frames, RANK), jnp.float32),
+            pltpu.VMEM((RANK, FRAMES), jnp.float32),
+        ],
+        scratch_shapes=[pltpu.VMEM((FRAMES, RANK), jnp.float32)],
+        name="merge_four",
     )(place_in, *near(gathered, weights, probe))
 
 
@@ -421,29 +436,19 @@
     probe = jnp.pad(merge_probe, ((0, 0), (0, spare)))
     position = lax.axis_index("pix").astype(jnp.int32)
     levels = count.bit_length() - 1
-    sizes = []
-    while sum(sizes) < levels:
-        sizes.append(2 if levels - sum(sizes) == 2 else 1)
-    copies = [4 if size == 2 else 1 for size in sizes[1:]] + [1]
-    rows, weights = tile_basis(covariance, test_matrix, 4 if sizes[0] == 2 else 1)
-    level = 0
-    for size, next_copies in zip(sizes, copies):
-        spot = (position >> level & (2**size - 1)).reshape(1)
-        if size == 2:
-            step = 1 << level
-            groups = [
-                [base + k * step for k in range(4)] for base in range(count) if not base & (3 * step)
-            ]
-            gathered = lax.all_to_all(rows, "pix", 0, 0, tiled=True, axis_index_groups=groups)
-            rows, weights = merge_four(spot, gathered, weights, probe, next_copies)
-        else:
-            pairs = [(source, source ^ (1 << level)) for source in range(count)]
-            partner = lax.ppermute(rows, "pix", pairs)
-            rows, weights = merge(spot, rows, partner, weights, probe, next_copies)
-        level += size
+    rows, weights = tile_basis(covariance, test_matrix)
+    for level in range(levels - 2):
+        pairs = [(source, source ^ (1 << level)) for source in range(count)]
+        partner = lax.ppermute(rows, "pix", pairs)
+        spot = (position >> level & 1).reshape(1)
+        rows, weights = merge(spot, rows, partner, weights, probe, 4 if level == levels - 3 else 1)
+    step = count // 4
+    groups = [[base + k * step for k in range(4)] for base in range(step)]
+    gathered = lax.all_to_all(rows, "pix", 0, 0, tiled=True, axis_index_groups=groups)
+    spot = jnp.stack([position // step, lax.axis_index("tm").astype(jnp.int32)])
+    own_times, weights = merge_four(spot, gathered, weights, probe, frames)
     loadings = loading_rows(weights, columns)
-    own_times = lax.dynamic_slice_in_dim(rows, lax.axis_index("tm") * frames, frames, 1)
-    return (own_times, loadings)
+    return (own_times.T, loadings)
 
 
 def solution(mesh):

time: 171 us -> 171 us (level)
  transfers between devices with their start and end apart: 7 -> 7, of which waited for: 6 -> 6; matrix products, arithmetic and copies ran while one was open for 1% -> 2% of each run, Pallas kernels for 3% -> 3%
where the time goes in v5:
time: 171 us; the launch traced here: 170 us
  blocking collectives  72 us (42%)
  Pallas kernels  39.1 us (23%)
  waiting for transfers between devices  31.2 us (18%)
  starting transfers between devices  22.1 us (13%)
  local copies, waits for them, and re-layouts  3.13 us (2%)
    all_to_all x1, blocking collectives, body(): columns = lax.all_to_all(smoothed, 'tm', 0, 0, tiled=True)  60.2 us
    ppermute x3, waiting for transfers between devices, body(): partner = lax.ppermute(rows, 'pix', pairs)  15.7 us
    pallas_call x3, Pallas kernels, merge(): pl.pallas_call(merge_kernel, in_specs=[smem, vmem, vmem, vmem, vmem], nam...  12.6 us
    all_to_all x1, blocking collectives, sum_over_tm(): lax.all_to_all(partial.reshape(parts, height, -1), 'tm', 0, 0, tiled=True)  11.8 us
    pallas_call x1, Pallas kernels, merge_four(): pl.pallas_call(merge_four_kernel, in_specs=[smem, vmem, vmem, vmem], out_...  10.4 us
    ppermute x3, starting transfers between devices, body(): partner = lax.ppermute(rows, 'pix', pairs)  7.68 us
    all_to_all x1, waiting for transfers between devices, sum_over_tm(): lax.all_to_all(jnp.broadcast_to(own, pieces.shape), 'tm', 0, 0, tiled=True)  7.65 us
    all_to_all x1, waiting for transfers between devices, body(): lax.all_to_all(rows, 'pix', 0, 0, tiled=True, axis_index_groups=groups)  5.71 us
  transfers between devices with their start and end apart: 7, of which 6 were waited for; matrix products, arithmetic and copies ran while one was open for 2% of the time, Pallas kernels for 3%

profile of v5, /device:TPU:24, one launch (start us, length us, event | category | flops | bytes accessed | tf_op | source)
XLA Modules:
  0.0 170.4 jit_solution(18343703669300726673)
XLA Ops:
  0.6 1.5 fusion.42
  2.2 4.7 %collective-permute-start = (bf16[32,4096]{1,0:T(8,128)(2,1)S(1)}, bf16[32,4096]{1,0:T(8,128)(2,1)S(1)}, u32[]{:S(2)}, u32[]{:S(2)}) collective-permute-start(bf16[32,4096]{1,0:T(8,128)(2,1)S(1)} %reshape.148), channel_id=1, source_target_pairs={{0,16},{16,32},{32,48},{48,64},{64,80},{80,96},{96,112},{112,128},... | collective-permute-start | bytes 786440 | tf_op jit(solution)/shard_map/ppermute | solution.py:428
  7.0 1.9 %collective-permute-start.1 = (bf16[32,4096]{1,0:T(8,128)(2,1)S(1)}, bf16[32,4096]{1,0:T(8,128)(2,1)S(1)}, u32[]{:S(2)}, u32[]{:S(2)}) collective-permute-start(bf16[32,4096]{1,0:T(8,128)(2,1)S(1)} %reshape.149), channel_id=1, source_target_pairs={{16,0},{32,16},{48,32},{64,48},{80,64},{96,80},{112,96},{128,112},... | collective-permute-start | bytes 786440 | tf_op jit(solution)/shard_map/ppermute | solution.py:429
  9.0 0.2 fusion.33
  9.2 0.3 fusion.30
  9.6 0.1 reshape.147
  9.8 0.4 reduce-precision_convert_fusion
  10.3 4.6 %smooth.1 = (bf16[16,256,256]{2,1,0:T(8,128)(2,1)}, f32[16,64,256]{2,1,0:T(8,128)S(1)}) custom-call(bf16[8,32,4096]{2,1,0:T(8,128)(2,1)} %movie_ref.1, bf16[512,256]{1,0:T(8,128)(2,1)S(1)} %pad_maximum_fusion.own_ref), custom_call_target="tpu_custom_call" | custom-call | tf_op jit(solution)/shard_map/smooth/pallas_call | solution.py:120
  15.5 0.1 copy.14.matrix_ref
  15.6 2.2 %collective-permute-done.1.high_ref = bf16[32,4096]{1,0:T(8,128)(2,1)S(1)} collective-permute-done((bf16[32,4096]{1,0:T(8,128)(2,1)S(1)}, bf16[32,4096]{1,0:T(8,128)(2,1)S(1)}, u32[]{:S(2)}, u32[]{:S(2)}) %collective-permute-start.1) | collective-permute-done | bytes 262176 | tf_op jit(solution)/shard_map/ppermute | solution.py:429
  17.8 1.3 edges.1
  19.1 60.2 %all_to_all.20.data_ref = bf16[16,256,256]{2,1,0:T(8,128)(2,1)} all-to-all(bf16[16,256,256]{2,1,0:T(8,128)(2,1)} %edges.1), channel_id=1, replica_groups=mesh['pix'=32,'tm'=16] {'tm'}, dimensions={0} | all-to-all | bytes 4194304 | tf_op jit(solution)/shard_map/all_to_all | solution.py:432
  79.3 2.6 %covariance.1 = f32[128,128]{1,0:T(8,128)S(1)} custom-call(bf16[16,256,256]{2,1,0:T(8,128)(2,1)} %all_to_all.20.data_ref), custom_call_target="tpu_custom_call" | custom-call | tf_op jit(solution)/shard_map/covariance/pallas_call | solution.py:177
  82.0 11.8 %all_to_all.21 = f32[16,8,128]{2,1,0:T(8,128)S(1)} all-to-all(f32[16,8,128]{2,1,0:T(8,128)S(1)} %bitcast.59), channel_id=1, replica_groups=mesh['pix'=32,'tm'=16] {'tm'}, dimensions={0} | all-to-all | bytes 131072 | tf_op jit(solution)/shard_map/all_to_all | solution.py:416
  93.8 0.6 broadcast_in_dim.330
  94.4 3.5 %all-to-all-start.2 = ((f32[16,8,128]{2,1,0:T(8,128)}), f32[16,8,128]{2,1,0:T(8,128)S(1)}, u32[]{:S(2)}, u32[]{:S(2)}) async-start(f32[16,8,128]{2,1,0:T(8,128)} %broadcast_in_dim.330), calls=%async_computation.2 | async-start | bytes 131072 | tf_op jit(solution)/shard_map/all_to_all | solution.py:418
  98.1 7.6 %all-to-all-done.2 = f32[16,8,128]{2,1,0:T(8,128)S(1)} async-done(((f32[16,8,128]{2,1,0:T(8,128)}), f32[16,8,128]{2,1,0:T(8,128)S(1)}, u32[]{:S(2)}, u32[]{:S(2)}) %all-to-all-start.2) | async-done | bytes 65568 | tf_op jit(solution)/shard_map/all_to_all | solution.py:418
  105.7 3.7 %basis.1 = (f32[96,128]{1,0:T(8,128)S(1)}, f32[96,128]{1,0:T(8,128)S(1)}) custom-call(f32[128,128]{1,0:T(8,128)S(1)} %bitcast.60, f32[128,128]{1,0:T(8,128)S(1)} %pad.8.test_ref), custom_call_target="tpu_custom_call" | custom-call | tf_op jit(solution)/shard_map/basis/pallas_call | solution.py:346
  109.5 1.9 %collective-permute-start.2 = (f32[96,128]{1,0:T(8,128)S(1)}, f32[96,128]{1,0:T(8,128)S(1)}, u32[]{:S(2)}, u32[]{:S(2)}) collective-permute-start(f32[96,128]{1,0:T(8,128)S(1)} %get-tuple-element.16.own_ref), channel_id=1, source_target_pairs={{0,16},{16,0},{32,48},{48,32},{64,80},{80,64},{96,112},{112,96},{1... | collective-permute-start | bytes 147464 | tf_op jit(solution)/shard_map/ppermute | solution.py:442
  111.4 4.0 %collective-permute-done.2.partner_ref = f32[96,128]{1,0:T(8,128)S(1)} collective-permute-done((f32[96,128]{1,0:T(8,128)S(1)}, f32[96,128]{1,0:T(8,128)S(1)}, u32[]{:S(2)}, u32[]{:S(2)}) %collective-permute-start.2) | collective-permute-done | bytes 49184 | tf_op jit(solution)/shard_map/ppermute | solution.py:442
  115.4 4.0 %merge.3 = (f32[96,128]{1,0:T(8,128)S(1)}, f32[96,128]{1,0:T(8,128)S(1)}) custom-call(s32[1]{0:T(128)} %bitcast.4.place_ref, f32[96,128]{1,0:T(8,128)S(1)} %get-tuple-element.16.own_ref, f32[96,128]{1,0:T(8,128)S(1)} %collective-permute-done.2.partner_ref, f32[96,128]{1,0:T(8,128)S(1)} %get-tuple-element.17.weights_ref, f32[192,128]{1,0:T(8,128)S(1)} %pad.9.probe_ref), custom_call_target="tpu_custom_call" | custom-call | tf_op jit(solution)/shard_map/merge/pallas_call | solution.py:378
  119.4 1.9 %collective-permute-start.3 = (f32[96,128]{1,0:T(8,128)S(1)}, f32[96,128]{1,0:T(8,128)S(1)}, u32[]{:S(2)}, u32[]{:S(2)}) collective-permute-start(f32[96,128]{1,0:T(8,128)S(1)} %get-tuple-element.18.own_ref), channel_id=1, source_target_pairs={{0,32},{16,48},{32,0},{48,16},{64,96},{80,112},{96,64},{112,80},{1... | collective-permute-start | bytes 147464 | tf_op jit(solution)/shard_map/ppermute | solution.py:442
  121.3 5.1 %collective-permute-done.3.partner_ref = f32[96,128]{1,0:T(8,128)S(1)} collective-permute-done((f32[96,128]{1,0:T(8,128)S(1)}, f32[96,128]{1,0:T(8,128)S(1)}, u32[]{:S(2)}, u32[]{:S(2)}) %collective-permute-start.3) | collective-permute-done | bytes 49184 | tf_op jit(solution)/shard_map/ppermute | solution.py:442
  126.5 4.0 %merge.4 = (f32[96,128]{1,0:T(8,128)S(1)}, f32[96,128]{1,0:T(8,128)S(1)}) custom-call(s32[1]{0:T(128)} %bitcast.3.place_ref, f32[96,128]{1,0:T(8,128)S(1)} %get-tuple-element.18.own_ref, f32[96,128]{1,0:T(8,128)S(1)} %collective-permute-done.3.partner_ref, f32[96,128]{1,0:T(8,128)S(1)} %get-tuple-element.19.weights_ref, f32[192,128]{1,0:T(8,128)S(1)} %pad.9.probe_ref), custom_call_target="tpu_custom_call" | custom-call | tf_op jit(solution)/shard_map/merge/pallas_call | solution.py:378
  130.4 3.8 %collective-permute-start.4 = (f32[96,128]{1,0:T(8,128)S(1)}, f32[96,128]{1,0:T(8,128)S(1)}, u32[]{:S(2)}, u32[]{:S(2)}) collective-permute-start(f32[96,128]{1,0:T(8,128)S(1)} %get-tuple-element.20.own_ref), channel_id=1, source_target_pairs={{0,64},{16,80},{32,96},{48,112},{64,0},{80,16},{96,32},{112,48},{1... | collective-permute-start | bytes 147464 | tf_op jit(solution)/shard_map/ppermute | solution.py:442
  134.3 6.5 %collective-permute-done.4.partner_ref = f32[96,128]{1,0:T(8,128)S(1)} collective-permute-done((f32[96,128]{1,0:T(8,128)S(1)}, f32[96,128]{1,0:T(8,128)S(1)}, u32[]{:S(2)}, u32[]{:S(2)}) %collective-permute-start.4) | collective-permute-done | bytes 49184 | tf_op jit(solution)/shard_map/ppermute | solution.py:442
  140.8 4.7 %merge.5 = (f32[4,96,128]{2,1,0:T(8,128)}, f32[96,128]{1,0:T(8,128)S(1)}) custom-call(s32[1]{0:T(128)} %bitcast.2.place_ref, f32[96,128]{1,0:T(8,128)S(1)} %get-tuple-element.20.own_ref, f32[96,128]{1,0:T(8,128)S(1)} %collective-permute-done.4.partner_ref, f32[96,128]{1,0:T(8,128)S(1)} %get-tuple-element.21.weights_ref, f32[192,128]{1,0:T(8,128)S(1)} %pad.9.probe_ref), custom_call_target="tpu_custom_call" | custom-call | tf_op jit(solution)/shard_map/merge/pallas_call | solution.py:378
  145.5 4.3 %all-to-all-start.3 = ((f32[4,96,128]{2,1,0:T(8,128)}), f32[4,96,128]{2,1,0:T(8,128)S(1)}, u32[]{:S(2)}, u32[]{:S(2)}) async-start(f32[4,96,128]{2,1,0:T(8,128)} %get-tuple-element.22), calls=%async_computation.3 | async-start | bytes 393216 | tf_op jit(solution)/shard_map/all_to_all | solution.py:447
  149.7 0.6 pad_add_fusion.place_ref
  150.4 5.7 %all-to-all-done.3.rows_in_ref = f32[4,96,128]{2,1,0:T(8,128)S(1)} async-done(((f32[4,96,128]{2,1,0:T(8,128)}), f32[4,96,128]{2,1,0:T(8,128)S(1)}, u32[]{:S(2)}, u32[]{:S(2)}) %all-to-all-start.3) | async-done | bytes 196640 | tf_op jit(solution)/shard_map/all_to_all | solution.py:447
  156.1 10.4 %merge_four.1 = (f32[8,96]{1,0:T(8,128)}, f32[96,128]{1,0:T(8,128)S(1)}) custom-call(s32[2]{0:T(128)} %pad_add_fusion.place_ref, f32[4,96,128]{2,1,0:T(8,128)S(1)} %all-to-all-done.3.rows_in_ref, f32[96,128]{1,0:T(8,128)S(1)} %get-tuple-element.23.weights_ref, f32[192,128]{1,0:T(8,128)S(1)} %pad.9.probe_ref), custom_call_target="tpu_custom_call" | custom-call | tf_op jit(solution)/shard_map/merge_four/pallas_call | solution.py:400
  166.5 3.9 %loadings.1 = bf16[96,32,256]{2,1,0:T(8,128)(2,1)} custom-call(f32[96,128]{1,0:T(8,128)S(1)} %get-tuple-element.25.weights_ref, bf16[16,256,256]{2,1,0:T(8,128)(2,1)} %all_to_all.20.data_ref), custom_call_target="tpu_custom_call" | custom-call | tf_op jit(solution)/shard_map/loadings/pallas_call | solution.py:222
  (35 shorter events, 1.1 us)
Async XLA Ops:
  0.6 8.3 %copy-start.2 = (f32[6]{0:T(128)S(1)}, f32[6]{0:T(128)}, u32[]{:S(2)}) copy-start(f32[6]{0:T(128)} %param.7) | copy-start | bytes 76
  0.6 8.5 %copy-start.3 = (s32[32]{0:T(128)S(1)}, s32[32]{0:T(128)}, u32[]{:S(2)}) copy-start(s32[32]{0:T(128)} %param.6) | copy-start | bytes 388
  2.2 13.4 %collective-permute-start = (bf16[32,4096]{1,0:T(8,128)(2,1)S(1)}, bf16[32,4096]{1,0:T(8,128)(2,1)S(1)}, u32[]{:S(2)}, u32[]{:S(2)}) collective-permute-start(bf16[32,4096]{1,0:T(8,128)(2,1)S(1)} %reshape.148), channel_id=1, source_target_pairs={{0,16},{16,32},{32,48},{48,64},{64,80},{80,96},{96,112},{112,128},... | collective-permute-start | bytes 786440 | tf_op jit(solution)/shard_map/ppermute | solution.py:428
  7.0 10.9 %collective-permute-start.1 = (bf16[32,4096]{1,0:T(8,128)(2,1)S(1)}, bf16[32,4096]{1,0:T(8,128)(2,1)S(1)}, u32[]{:S(2)}, u32[]{:S(2)}) collective-permute-start(bf16[32,4096]{1,0:T(8,128)(2,1)S(1)} %reshape.149), channel_id=1, source_target_pairs={{16,0},{32,16},{48,32},{64,48},{80,64},{96,80},{112,96},{128,112},... | collective-permute-start | bytes 786440 | tf_op jit(solution)/shard_map/ppermute | solution.py:429
  79.3 18.7 %copy-start.1 = (f32[128,96]{0,1:T(8,128)S(1)}, f32[128,96]{0,1:T(8,128)}, u32[]{:S(2)}) copy-start(f32[128,96]{0,1:T(8,128)} %param.8) | copy-start | bytes 147460
  79.3 32.1 %copy-start = (f32[192,96]{1,0:T(8,128)S(1)}, f32[192,96]{1,0:T(8,128)}, u32[]{:S(2)}) copy-start(f32[192,96]{1,0:T(8,128)} %param.9) | copy-start | bytes 221188
  94.4 11.3 %all-to-all-start.2 = ((f32[16,8,128]{2,1,0:T(8,128)}), f32[16,8,128]{2,1,0:T(8,128)S(1)}, u32[]{:S(2)}, u32[]{:S(2)}) async-start(f32[16,8,128]{2,1,0:T(8,128)} %broadcast_in_dim.330), calls=%async_computation.2 | async-start | bytes 131072 | tf_op jit(solution)/shard_map/all_to_all | solution.py:418
  109.5 6.0 %collective-permute-start.2 = (f32[96,128]{1,0:T(8,128)S(1)}, f32[96,128]{1,0:T(8,128)S(1)}, u32[]{:S(2)}, u32[]{:S(2)}) collective-permute-start(f32[96,128]{1,0:T(8,128)S(1)} %get-tuple-element.16.own_ref), channel_id=1, source_target_pairs={{0,16},{16,0},{32,48},{48,32},{64,80},{80,64},{96,112},{112,96},{1... | collective-permute-start | bytes 147464 | tf_op jit(solution)/shard_map/ppermute | solution.py:442
  119.4 7.0 %collective-permute-start.3 = (f32[96,128]{1,0:T(8,128)S(1)}, f32[96,128]{1,0:T(8,128)S(1)}, u32[]{:S(2)}, u32[]{:S(2)}) collective-permute-start(f32[96,128]{1,0:T(8,128)S(1)} %get-tuple-element.18.own_ref), channel_id=1, source_target_pairs={{0,32},{16,48},{32,0},{48,16},{64,96},{80,112},{96,64},{112,80},{1... | collective-permute-start | bytes 147464 | tf_op jit(solution)/shard_map/ppermute | solution.py:442
  130.4 10.4 %collective-permute-start.4 = (f32[96,128]{1,0:T(8,128)S(1)}, f32[96,128]{1,0:T(8,128)S(1)}, u32[]{:S(2)}, u32[]{:S(2)}) collective-permute-start(f32[96,128]{1,0:T(8,128)S(1)} %get-tuple-element.20.own_ref), channel_id=1, source_target_pairs={{0,64},{16,80},{32,96},{48,112},{64,0},{80,16},{96,32},{112,48},{1... | collective-permute-start | bytes 147464 | tf_op jit(solution)/shard_map/ppermute | solution.py:442
  145.5 10.6 %all-to-all-start.3 = ((f32[4,96,128]{2,1,0:T(8,128)}), f32[4,96,128]{2,1,0:T(8,128)S(1)}, u32[]{:S(2)}, u32[]{:S(2)}) async-start(f32[4,96,128]{2,1,0:T(8,128)} %get-tuple-element.22), calls=%async_computation.3 | async-start | bytes 393216 | tf_op jit(solution)/shard_map/all_to_all | solution.py:447

commit v6 on v5

--- a/solution.py
+++ b/solution.py
@@ -185,7 +185,9 @@
     )(columns)
 
 
-def loading_kernel(weights_ref, data_ref, out_ref, matrix_ref, turn_ref):
+def loading_kernel(
+    span_ref, rows_ref, weights_ref, data_ref, out_ref, times_ref, matrix_ref, turn_ref, times_all_ref
+):
     rank, height, width = out_ref.shape
     parts, rows, _ = data_ref.shape
     frames = rows // height
@@ -200,6 +202,8 @@
                 weights, selector, (((1,), (1,)), ((), ())), preferred_element_type=jnp.float32
             )
             matrix_ref[parity * rank : (parity + 1) * rank, :] = spread.astype(jnp.bfloat16)
+        times_all_ref[...] = rows_ref[...].T
+        times_ref[...] = times_all_ref[pl.ds(pl.multiple_of(span_ref[0] * frames, frames), frames), :]
 
     matrix = matrix_ref[...]
     for i in range(height // 2):
@@ -216,21 +220,29 @@
         out_ref[:, :, lanes] = turn_ref[half].reshape(rank, height, 128).astype(jnp.bfloat16)
 
 
-def loading_rows(weights, columns):
+def loading_rows(span, root_rows, weights, columns):
     parts, rows, width = columns.shape
     height = LOADING_ROWS
+    frames = rows // ROWS_DEV
     return pl.pallas_call(
         loading_kernel,
         grid=(ROWS_DEV // height,),
-        in_specs=[vmem, pl.BlockSpec((parts, height * (rows // ROWS_DEV), width), lambda i: (0, i, 0))],
-        out_specs=pl.BlockSpec((RANK, height, width), lambda i: (0, i, 0)),
-        out_shape=jax.ShapeDtypeStruct((RANK, ROWS_DEV, width), jnp.bfloat16),
+        in_specs=[smem, vmem, vmem, pl.BlockSpec((parts, height * frames, width), lambda i: (0, i, 0))],
+        out_specs=[
+            pl.BlockSpec((RANK, height, width), lambda i: (0, i, 0)),
+            pl.BlockSpec((frames, RANK), lambda i: (0, 0)),
+        ],
+        out_shape=[
+            jax.ShapeDtypeStruct((RANK, ROWS_DEV, width), jnp.bfloat16),
+            jax.ShapeDtypeStruct((frames, RANK), jnp.float32),
+        ],
         scratch_shapes=[
             pltpu.VMEM((2 * RANK, 2 * FRAMES), jnp.bfloat16),
             pltpu.VMEM((width // 128, RANK * height, 128), jnp.float32),
+            pltpu.VMEM((FRAMES, RANK), jnp.float32),
         ],
         name="loadings",
-    )(*near(weights), columns)
+    )(span, *near(root_rows, weights), columns)
 
 
 def split_in_three(value):
@@ -380,33 +392,21 @@
     )(place_in, *near(own, partner, weights, probe))
 
 
-def merge_four_kernel(
-    place_ref, rows_in_ref, weights_ref, probe_ref, times_ref, new_weights_ref, turned_ref
-):
+def merge_four_kernel(place_ref, rows_in_ref, weights_ref, probe_ref, rows_ref, new_weights_ref):
     spot = place_ref[0]
-    frames = times_ref.shape[0]
     probe = probe_ref[...]
     weights = weights_ref[...]
     stacks = [rows_in_ref[2 * m : 2 * m + 2].reshape(2 * RANK, FRAMES) for m in range(2)]
     placed = [place(weights, spot == 2 * m, spot == 2 * m + 1) for m in range(2)]
     rows, weights = merge_nodes(stacks, placed, probe)
     (rows,), weights = merge_nodes([jnp.concatenate(rows, axis=0)], [place(weights, spot < 2, spot >= 2)], probe)
+    store_rows(rows_ref, rows)
     new_weights_ref[...] = weights
-    turned_ref[...] = rows.T
-    times_ref[...] = turned_ref[pl.ds(pl.multiple_of(place_ref[1] * frames, frames), frames), :]
-
-
-def merge_four(place_in, gathered, weights, probe, frames):
-    return pl.pallas_call(
-        merge_four_kernel,
-        in_specs=[smem, vmem, vmem, vmem],
-        out_specs=[vmem, vmem],
-        out_shape=[
-            jax.ShapeDtypeStruct((frames, RANK), jnp.float32),
-            pltpu.VMEM((RANK, FRAMES), jnp.float32),
-        ],
-        scratch_shapes=[pltpu.VMEM((FRAMES, RANK), jnp.float32)],
-        name="merge_four",
+
+
+def merge_four(place_in, gathered, weights, probe):
+    return pl.pallas_call(
+        merge_four_kernel, in_specs=[smem, vmem, vmem, vmem], name="merge_four", **rows_and_weights(1)
     )(place_in, *near(gathered, weights, probe))
 
 
@@ -445,9 +445,9 @@
     step = count // 4
     groups = [[base + k * step for k in range(4)] for base in range(step)]
     gathered = lax.all_to_all(rows, "pix", 0, 0, tiled=True, axis_index_groups=groups)
-    spot = jnp.stack([position // step, lax.axis_index("tm").astype(jnp.int32)])
-    own_times, weights = merge_four(spot, gathered, weights, probe, frames)
-    loadings = loading_rows(weights, columns)
+    rows, weights = merge_four((position // step).reshape(1), gathered, weights, probe)
+    span = lax.axis_index("tm").astype(jnp.int32).reshape(1)
+    loadings, own_times = loading_rows(span, rows, weights, columns)
     return (own_times.T, loadings)
 
 

time: 171 us -> 170 us (level)
  transfers between devices with their start and end apart: 7 -> 7, of which waited for: 6 -> 6; matrix products, arithmetic and copies ran while one was open for 2% -> 1% of each run, Pallas kernels for 3% -> 3%
where the time goes in v6:
time: 170 us; the launch traced here: 169 us
  blocking collectives  72 us (42%)
  Pallas kernels  37.8 us (22%)
  waiting for transfers between devices  31.9 us (19%)
  starting transfers between devices  22.1 us (13%)
  local copies, waits for them, and re-layouts  3.13 us (2%)
    all_to_all x1, blocking collectives, body(): columns = lax.all_to_all(smoothed, 'tm', 0, 0, tiled=True)  60.2 us
    ppermute x3, waiting for transfers between devices, body(): partner = lax.ppermute(rows, 'pix', pairs)  15.7 us
    pallas_call x3, Pallas kernels, merge(): pl.pallas_call(merge_kernel, in_specs=[smem, vmem, vmem, vmem, vmem], nam...  12.6 us
    all_to_all x1, blocking collectives, sum_over_tm(): lax.all_to_all(partial.reshape(parts, height, -1), 'tm', 0, 0, tiled=True)  11.8 us
    pallas_call x1, Pallas kernels, merge_four(): pl.pallas_call(merge_four_kernel, in_specs=[smem, vmem, vmem, vmem], name...  9.05 us
    ppermute x3, starting transfers between devices, body(): partner = lax.ppermute(rows, 'pix', pairs)  7.67 us
    all_to_all x1, waiting for transfers between devices, sum_over_tm(): lax.all_to_all(jnp.broadcast_to(own, pieces.shape), 'tm', 0, 0, tiled=True)  7.65 us
    all_to_all x1, waiting for transfers between devices, body(): lax.all_to_all(rows, 'pix', 0, 0, tiled=True, axis_index_groups=groups)  6.33 us
  transfers between devices with their start and end apart: 7, of which 6 were waited for; matrix products, arithmetic and copies ran while one was open for 1% of the time, Pallas kernels for 3%

profile of v6, /device:TPU:24, one launch (start us, length us, event | category | flops | bytes accessed | tf_op | source)
XLA Modules:
  0.0 169.1 jit_solution(14736768761267467431)
XLA Ops:
  0.6 1.5 fusion.42
  2.2 4.7 %collective-permute-start = (bf16[32,4096]{1,0:T(8,128)(2,1)S(1)}, bf16[32,4096]{1,0:T(8,128)(2,1)S(1)}, u32[]{:S(2)}, u32[]{:S(2)}) collective-permute-start(bf16[32,4096]{1,0:T(8,128)(2,1)S(1)} %reshape.156), channel_id=1, source_target_pairs={{0,16},{16,32},{32,48},{48,64},{64,80},{80,96},{96,112},{112,128},... | collective-permute-start | bytes 786440 | tf_op jit(solution)/shard_map/ppermute | solution.py:428
  7.0 1.9 %collective-permute-start.1 = (bf16[32,4096]{1,0:T(8,128)(2,1)S(1)}, bf16[32,4096]{1,0:T(8,128)(2,1)S(1)}, u32[]{:S(2)}, u32[]{:S(2)}) collective-permute-start(bf16[32,4096]{1,0:T(8,128)(2,1)S(1)} %reshape.157), channel_id=1, source_target_pairs={{16,0},{32,16},{48,32},{64,48},{80,64},{96,80},{112,96},{128,112},... | collective-permute-start | bytes 786440 | tf_op jit(solution)/shard_map/ppermute | solution.py:429
  9.0 0.2 fusion.33
  9.2 0.3 fusion.30
  9.5 0.1 broadcast_in_dim.270
  9.6 0.1 reshape.155
  9.8 0.4 reduce-precision_convert_fusion
  10.3 4.6 %smooth.1 = (bf16[16,256,256]{2,1,0:T(8,128)(2,1)}, f32[16,64,256]{2,1,0:T(8,128)S(1)}) custom-call(bf16[8,32,4096]{2,1,0:T(8,128)(2,1)} %movie_ref.1, bf16[512,256]{1,0:T(8,128)(2,1)S(1)} %pad_maximum_fusion.own_ref), custom_call_target="tpu_custom_call" | custom-call | tf_op jit(solution)/shard_map/smooth/pallas_call | solution.py:120
  15.5 0.1 copy.14.matrix_ref
  15.6 2.2 %collective-permute-done.1.high_ref = bf16[32,4096]{1,0:T(8,128)(2,1)S(1)} collective-permute-done((bf16[32,4096]{1,0:T(8,128)(2,1)S(1)}, bf16[32,4096]{1,0:T(8,128)(2,1)S(1)}, u32[]{:S(2)}, u32[]{:S(2)}) %collective-permute-start.1) | collective-permute-done | bytes 262176 | tf_op jit(solution)/shard_map/ppermute | solution.py:429
  17.8 1.3 edges.1
  19.1 60.2 %all_to_all.20.data_ref = bf16[16,256,256]{2,1,0:T(8,128)(2,1)} all-to-all(bf16[16,256,256]{2,1,0:T(8,128)(2,1)} %edges.1), channel_id=1, replica_groups=mesh['pix'=32,'tm'=16] {'tm'}, dimensions={0} | all-to-all | bytes 4194304 | tf_op jit(solution)/shard_map/all_to_all | solution.py:432
  79.3 2.6 %covariance.1 = f32[128,128]{1,0:T(8,128)S(1)} custom-call(bf16[16,256,256]{2,1,0:T(8,128)(2,1)} %all_to_all.20.data_ref), custom_call_target="tpu_custom_call" | custom-call | tf_op jit(solution)/shard_map/covariance/pallas_call | solution.py:177
  81.9 11.8 %all_to_all.21 = f32[16,8,128]{2,1,0:T(8,128)S(1)} all-to-all(f32[16,8,128]{2,1,0:T(8,128)S(1)} %bitcast.59), channel_id=1, replica_groups=mesh['pix'=32,'tm'=16] {'tm'}, dimensions={0} | all-to-all | bytes 131072 | tf_op jit(solution)/shard_map/all_to_all | solution.py:416
  93.8 0.6 broadcast_in_dim.330
  94.4 3.5 %all-to-all-start.2 = ((f32[16,8,128]{2,1,0:T(8,128)}), f32[16,8,128]{2,1,0:T(8,128)S(1)}, u32[]{:S(2)}, u32[]{:S(2)}) async-start(f32[16,8,128]{2,1,0:T(8,128)} %broadcast_in_dim.330), calls=%async_computation.2 | async-start | bytes 131072 | tf_op jit(solution)/shard_map/all_to_all | solution.py:418
  98.1 7.6 %all-to-all-done.2 = f32[16,8,128]{2,1,0:T(8,128)S(1)} async-done(((f32[16,8,128]{2,1,0:T(8,128)}), f32[16,8,128]{2,1,0:T(8,128)S(1)}, u32[]{:S(2)}, u32[]{:S(2)}) %all-to-all-start.2) | async-done | bytes 65568 | tf_op jit(solution)/shard_map/all_to_all | solution.py:418
  105.7 3.7 %basis.1 = (f32[96,128]{1,0:T(8,128)S(1)}, f32[96,128]{1,0:T(8,128)S(1)}) custom-call(f32[128,128]{1,0:T(8,128)S(1)} %bitcast.60, f32[128,128]{1,0:T(8,128)S(1)} %pad.8.test_ref), custom_call_target="tpu_custom_call" | custom-call | tf_op jit(solution)/shard_map/basis/pallas_call | solution.py:358
  109.5 1.9 %collective-permute-start.2 = (f32[96,128]{1,0:T(8,128)S(1)}, f32[96,128]{1,0:T(8,128)S(1)}, u32[]{:S(2)}, u32[]{:S(2)}) collective-permute-start(f32[96,128]{1,0:T(8,128)S(1)} %get-tuple-element.18.own_ref), channel_id=1, source_target_pairs={{0,16},{16,0},{32,48},{48,32},{64,80},{80,64},{96,112},{112,96},{1... | collective-permute-start | bytes 147464 | tf_op jit(solution)/shard_map/ppermute | solution.py:442
  111.4 4.0 %collective-permute-done.2.partner_ref = f32[96,128]{1,0:T(8,128)S(1)} collective-permute-done((f32[96,128]{1,0:T(8,128)S(1)}, f32[96,128]{1,0:T(8,128)S(1)}, u32[]{:S(2)}, u32[]{:S(2)}) %collective-permute-start.2) | collective-permute-done | bytes 49184 | tf_op jit(solution)/shard_map/ppermute | solution.py:442
  115.4 4.0 %merge.3 = (f32[96,128]{1,0:T(8,128)S(1)}, f32[96,128]{1,0:T(8,128)S(1)}) custom-call(s32[1]{0:T(128)} %bitcast.4.place_ref, f32[96,128]{1,0:T(8,128)S(1)} %get-tuple-element.18.own_ref, f32[96,128]{1,0:T(8,128)S(1)} %collective-permute-done.2.partner_ref, f32[96,128]{1,0:T(8,128)S(1)} %get-tuple-element.19.weights_ref, f32[192,128]{1,0:T(8,128)S(1)} %pad.9.probe_ref), custom_call_target="tpu_custom_call" | custom-call | tf_op jit(solution)/shard_map/merge/pallas_call | solution.py:390
  119.4 1.9 %collective-permute-start.3 = (f32[96,128]{1,0:T(8,128)S(1)}, f32[96,128]{1,0:T(8,128)S(1)}, u32[]{:S(2)}, u32[]{:S(2)}) collective-permute-start(f32[96,128]{1,0:T(8,128)S(1)} %get-tuple-element.20.own_ref), channel_id=1, source_target_pairs={{0,32},{16,48},{32,0},{48,16},{64,96},{80,112},{96,64},{112,80},{1... | collective-permute-start | bytes 147464 | tf_op jit(solution)/shard_map/ppermute | solution.py:442
  121.3 5.1 %collective-permute-done.3.partner_ref = f32[96,128]{1,0:T(8,128)S(1)} collective-permute-done((f32[96,128]{1,0:T(8,128)S(1)}, f32[96,128]{1,0:T(8,128)S(1)}, u32[]{:S(2)}, u32[]{:S(2)}) %collective-permute-start.3) | collective-permute-done | bytes 49184 | tf_op jit(solution)/shard_map/ppermute | solution.py:442
  126.5 4.0 %merge.4 = (f32[96,128]{1,0:T(8,128)S(1)}, f32[96,128]{1,0:T(8,128)S(1)}) custom-call(s32[1]{0:T(128)} %bitcast.3.place_ref, f32[96,128]{1,0:T(8,128)S(1)} %get-tuple-element.20.own_ref, f32[96,128]{1,0:T(8,128)S(1)} %collective-permute-done.3.partner_ref, f32[96,128]{1,0:T(8,128)S(1)} %get-tuple-element.21.weights_ref, f32[192,128]{1,0:T(8,128)S(1)} %pad.9.probe_ref), custom_call_target="tpu_custom_call" | custom-call | tf_op jit(solution)/shard_map/merge/pallas_call | solution.py:390
  130.4 3.8 %collective-permute-start.4 = (f32[96,128]{1,0:T(8,128)S(1)}, f32[96,128]{1,0:T(8,128)S(1)}, u32[]{:S(2)}, u32[]{:S(2)}) collective-permute-start(f32[96,128]{1,0:T(8,128)S(1)} %get-tuple-element.22.own_ref), channel_id=1, source_target_pairs={{0,64},{16,80},{32,96},{48,112},{64,0},{80,16},{96,32},{112,48},{1... | collective-permute-start | bytes 147464 | tf_op jit(solution)/shard_map/ppermute | solution.py:442
  134.3 6.5 %collective-permute-done.4.partner_ref = f32[96,128]{1,0:T(8,128)S(1)} collective-permute-done((f32[96,128]{1,0:T(8,128)S(1)}, f32[96,128]{1,0:T(8,128)S(1)}, u32[]{:S(2)}, u32[]{:S(2)}) %collective-permute-start.4) | collective-permute-done | bytes 49184 | tf_op jit(solution)/shard_map/ppermute | solution.py:442
  140.8 4.7 %merge.5 = (f32[4,96,128]{2,1,0:T(8,128)}, f32[96,128]{1,0:T(8,128)S(1)}) custom-call(s32[1]{0:T(128)} %bitcast.2.place_ref, f32[96,128]{1,0:T(8,128)S(1)} %get-tuple-element.22.own_ref, f32[96,128]{1,0:T(8,128)S(1)} %collective-permute-done.4.partner_ref, f32[96,128]{1,0:T(8,128)S(1)} %get-tuple-element.23.weights_ref, f32[192,128]{1,0:T(8,128)S(1)} %pad.9.probe_ref), custom_call_target="tpu_custom_call" | custom-call | tf_op jit(solution)/shard_map/merge/pallas_call | solution.py:390
  145.5 4.3 %all-to-all-start.3 = ((f32[4,96,128]{2,1,0:T(8,128)}), f32[4,96,128]{2,1,0:T(8,128)S(1)}, u32[]{:S(2)}, u32[]{:S(2)}) async-start(f32[4,96,128]{2,1,0:T(8,128)} %get-tuple-element.24), calls=%async_computation.3 | async-start | bytes 393216 | tf_op jit(solution)/shard_map/all_to_all | solution.py:447
  149.8 6.3 %all-to-all-done.3.rows_in_ref = f32[4,96,128]{2,1,0:T(8,128)S(1)} async-done(((f32[4,96,128]{2,1,0:T(8,128)}), f32[4,96,128]{2,1,0:T(8,128)S(1)}, u32[]{:S(2)}, u32[]{:S(2)}) %all-to-all-start.3) | async-done | bytes 196640 | tf_op jit(solution)/shard_map/all_to_all | solution.py:447
  156.1 9.0 %merge_four.1 = (f32[96,128]{1,0:T(8,128)S(1)}, f32[96,128]{1,0:T(8,128)S(1)}) custom-call(s32[1]{0:T(128)} %bitcast.1.place_ref, f32[4,96,128]{2,1,0:T(8,128)S(1)} %all-to-all-done.3.rows_in_ref, f32[96,128]{1,0:T(8,128)S(1)} %get-tuple-element.25.weights_ref, f32[192,128]{1,0:T(8,128)S(1)} %pad.9.probe_ref), custom_call_target="tpu_custom_call" | custom-call | tf_op jit(solution)/shard_map/merge_four/pallas_call | solution.py:408
  165.1 3.9 %loadings.1 = (bf16[96,32,256]{2,1,0:T(8,128)(2,1)}, f32[8,96]{1,0:T(8,128)}) custom-call(s32[1]{0:T(128)} %bitcast.span_ref, f32[96,128]{1,0:T(8,128)S(1)} %get-tuple-element.26.rows_ref, f32[96,128]{1,0:T(8,128)S(1)} %get-tuple-element.27.weights_ref, bf16[16,256,256]{2,1,0:T(8,128)(2,1)} %all_to_all.20.data_ref), custom_call_target="tpu_custom_call" | custom-call | tf_op jit(solution)/shard_map/loadings/pallas_call | solution.py:227
  (34 shorter events, 1.0 us)
Async XLA Ops:
  0.6 8.3 %copy-start.2 = (f32[6]{0:T(128)S(1)}, f32[6]{0:T(128)}, u32[]{:S(2)}) copy-start(f32[6]{0:T(128)} %param.7) | copy-start | bytes 76
  0.6 8.5 %copy-start.3 = (s32[32]{0:T(128)S(1)}, s32[32]{0:T(128)}, u32[]{:S(2)}) copy-start(s32[32]{0:T(128)} %param.6) | copy-start | bytes 388
  2.2 13.4 %collective-permute-start = (bf16[32,4096]{1,0:T(8,128)(2,1)S(1)}, bf16[32,4096]{1,0:T(8,128)(2,1)S(1)}, u32[]{:S(2)}, u32[]{:S(2)}) collective-permute-start(bf16[32,4096]{1,0:T(8,128)(2,1)S(1)} %reshape.156), channel_id=1, source_target_pairs={{0,16},{16,32},{32,48},{48,64},{64,80},{80,96},{96,112},{112,128},... | collective-permute-start | bytes 786440 | tf_op jit(solution)/shard_map/ppermute | solution.py:428
  7.0 10.9 %collective-permute-start.1 = (bf16[32,4096]{1,0:T(8,128)(2,1)S(1)}, bf16[32,4096]{1,0:T(8,128)(2,1)S(1)}, u32[]{:S(2)}, u32[]{:S(2)}) collective-permute-start(bf16[32,4096]{1,0:T(8,128)(2,1)S(1)} %reshape.157), channel_id=1, source_target_pairs={{16,0},{32,16},{48,32},{64,48},{80,64},{96,80},{112,96},{128,112},... | collective-permute-start | bytes 786440 | tf_op jit(solution)/shard_map/ppermute | solution.py:429
  79.3 18.7 %copy-start.1 = (f32[128,96]{0,1:T(8,128)S(1)}, f32[128,96]{0,1:T(8,128)}, u32[]{:S(2)}) copy-start(f32[128,96]{0,1:T(8,128)} %param.8) | copy-start | bytes 147460
  79.3 32.1 %copy-start = (f32[192,96]{1,0:T(8,128)S(1)}, f32[192,96]{1,0:T(8,128)}, u32[]{:S(2)}) copy-start(f32[192,96]{1,0:T(8,128)} %param.9) | copy-start | bytes 221188
  94.4 11.3 %all-to-all-start.2 = ((f32[16,8,128]{2,1,0:T(8,128)}), f32[16,8,128]{2,1,0:T(8,128)S(1)}, u32[]{:S(2)}, u32[]{:S(2)}) async-start(f32[16,8,128]{2,1,0:T(8,128)} %broadcast_in_dim.330), calls=%async_computation.2 | async-start | bytes 131072 | tf_op jit(solution)/shard_map/all_to_all | solution.py:418
  109.5 6.0 %collective-permute-start.2 = (f32[96,128]{1,0:T(8,128)S(1)}, f32[96,128]{1,0:T(8,128)S(1)}, u32[]{:S(2)}, u32[]{:S(2)}) collective-permute-start(f32[96,128]{1,0:T(8,128)S(1)} %get-tuple-element.18.own_ref), channel_id=1, source_target_pairs={{0,16},{16,0},{32,48},{48,32},{64,80},{80,64},{96,112},{112,96},{1... | collective-permute-start | bytes 147464 | tf_op jit(solution)/shard_map/ppermute | solution.py:442
  119.4 7.0 %collective-permute-start.3 = (f32[96,128]{1,0:T(8,128)S(1)}, f32[96,128]{1,0:T(8,128)S(1)}, u32[]{:S(2)}, u32[]{:S(2)}) collective-permute-start(f32[96,128]{1,0:T(8,128)S(1)} %get-tuple-element.20.own_ref), channel_id=1, source_target_pairs={{0,32},{16,48},{32,0},{48,16},{64,96},{80,112},{96,64},{112,80},{1... | collective-permute-start | bytes 147464 | tf_op jit(solution)/shard_map/ppermute | solution.py:442
  130.4 10.4 %collective-permute-start.4 = (f32[96,128]{1,0:T(8,128)S(1)}, f32[96,128]{1,0:T(8,128)S(1)}, u32[]{:S(2)}, u32[]{:S(2)}) collective-permute-start(f32[96,128]{1,0:T(8,128)S(1)} %get-tuple-element.22.own_ref), channel_id=1, source_target_pairs={{0,64},{16,80},{32,96},{48,112},{64,0},{80,16},{96,32},{112,48},{1... | collective-permute-start | bytes 147464 | tf_op jit(solution)/shard_map/ppermute | solution.py:442
  145.5 10.6 %all-to-all-start.3 = ((f32[4,96,128]{2,1,0:T(8,128)}), f32[4,96,128]{2,1,0:T(8,128)S(1)}, u32[]{:S(2)}, u32[]{:S(2)}) async-start(f32[4,96,128]{2,1,0:T(8,128)} %get-tuple-element.24), calls=%async_computation.3 | async-start | bytes 393216 | tf_op jit(solution)/shard_map/all_to_all | solution.py:447

commit v7 on v6

--- a/solution.py
+++ b/solution.py
@@ -15,7 +15,7 @@
 NDEPTH = 6
 BLOCK = 8
 SMOOTH_GROUP = 4
-PAIR_GROUP = 8
+PAIR_GROUP = 16
 LOADING_ROWS = 16
 
 highest = lax.Precision.HIGHEST

time: 170 us -> 170 us (level)
  no operation moved by 1% of the time
where the time goes in v7:
time: 170 us; the launch traced here: 169 us
  blocking collectives  72 us (42%)
  Pallas kernels  38.2 us (22%)
  waiting for transfers between devices  31.9 us (19%)
  starting transfers between devices  22.1 us (13%)
  local copies, waits for them, and re-layouts  3.13 us (2%)
    all_to_all x1, blocking collectives, body(): columns = lax.all_to_all(smoothed, 'tm', 0, 0, tiled=True)  60.2 us
    ppermute x3, waiting for transfers between devices, body(): partner = lax.ppermute(rows, 'pix', pairs)  15.7 us
    pallas_call x3, Pallas kernels, merge(): pl.pallas_call(merge_kernel, in_specs=[smem, vmem, vmem, vmem, vmem], nam...  12.6 us
    all_to_all x1, blocking collectives, sum_over_tm(): lax.all_to_all(partial.reshape(parts, height, -1), 'tm', 0, 0, tiled=True)  11.8 us
    pallas_call x1, Pallas kernels, merge_four(): pl.pallas_call(merge_four_kernel, in_specs=[smem, vmem, vmem, vmem], name...  9.05 us
    ppermute x3, starting transfers between devices, body(): partner = lax.ppermute(rows, 'pix', pairs)  7.68 us
    all_to_all x1, waiting for transfers between devices, sum_over_tm(): lax.all_to_all(jnp.broadcast_to(own, pieces.shape), 'tm', 0, 0, tiled=True)  7.65 us
    all_to_all x1, waiting for transfers between devices, body(): lax.all_to_all(rows, 'pix', 0, 0, tiled=True, axis_index_groups=groups)  6.33 us
  transfers between devices with their start and end apart: 7, of which 6 were waited for; matrix products, arithmetic and copies ran while one was open for 1% of the time, Pallas kernels for 3%

profile of v7, /device:TPU:24, one launch (start us, length us, event | category | flops | bytes accessed | tf_op | source)
XLA Modules:
  0.0 169.5 jit_solution(2719936729799839084)
XLA Ops:
  0.6 1.5 fusion.42
  2.2 4.7 %collective-permute-start = (bf16[32,4096]{1,0:T(8,128)(2,1)S(1)}, bf16[32,4096]{1,0:T(8,128)(2,1)S(1)}, u32[]{:S(2)}, u32[]{:S(2)}) collective-permute-start(bf16[32,4096]{1,0:T(8,128)(2,1)S(1)} %reshape.156), channel_id=1, source_target_pairs={{0,16},{16,32},{32,48},{48,64},{64,80},{80,96},{96,112},{112,128},... | collective-permute-start | bytes 786440 | tf_op jit(solution)/shard_map/ppermute | solution.py:428
  7.0 1.9 %collective-permute-start.1 = (bf16[32,4096]{1,0:T(8,128)(2,1)S(1)}, bf16[32,4096]{1,0:T(8,128)(2,1)S(1)}, u32[]{:S(2)}, u32[]{:S(2)}) collective-permute-start(bf16[32,4096]{1,0:T(8,128)(2,1)S(1)} %reshape.157), channel_id=1, source_target_pairs={{16,0},{32,16},{48,32},{64,48},{80,64},{96,80},{112,96},{128,112},... | collective-permute-start | bytes 786440 | tf_op jit(solution)/shard_map/ppermute | solution.py:429
  9.0 0.2 fusion.33
  9.2 0.3 fusion.30
  9.5 0.1 broadcast_in_dim.270
  9.6 0.1 reshape.155
  9.8 0.4 reduce-precision_convert_fusion
  10.3 4.6 %smooth.1 = (bf16[16,256,256]{2,1,0:T(8,128)(2,1)}, f32[16,64,256]{2,1,0:T(8,128)S(1)}) custom-call(bf16[8,32,4096]{2,1,0:T(8,128)(2,1)} %movie_ref.1, bf16[512,256]{1,0:T(8,128)(2,1)S(1)} %pad_maximum_fusion.own_ref), custom_call_target="tpu_custom_call" | custom-call | tf_op jit(solution)/shard_map/smooth/pallas_call | solution.py:120
  15.5 0.1 copy.14.matrix_ref
  15.6 2.2 %collective-permute-done.1.high_ref = bf16[32,4096]{1,0:T(8,128)(2,1)S(1)} collective-permute-done((bf16[32,4096]{1,0:T(8,128)(2,1)S(1)}, bf16[32,4096]{1,0:T(8,128)(2,1)S(1)}, u32[]{:S(2)}, u32[]{:S(2)}) %collective-permute-start.1) | collective-permute-done | bytes 262176 | tf_op jit(solution)/shard_map/ppermute | solution.py:429
  17.8 1.3 edges.1
  19.1 60.2 %all_to_all.20.data_ref = bf16[16,256,256]{2,1,0:T(8,128)(2,1)} all-to-all(bf16[16,256,256]{2,1,0:T(8,128)(2,1)} %edges.1), channel_id=1, replica_groups=mesh['pix'=32,'tm'=16] {'tm'}, dimensions={0} | all-to-all | bytes 4194304 | tf_op jit(solution)/shard_map/all_to_all | solution.py:432
  79.3 3.0 %covariance.1 = f32[128,128]{1,0:T(8,128)S(1)} custom-call(bf16[16,256,256]{2,1,0:T(8,128)(2,1)} %all_to_all.20.data_ref), custom_call_target="tpu_custom_call" | custom-call | tf_op jit(solution)/shard_map/covariance/pallas_call | solution.py:177
  82.3 11.8 %all_to_all.21 = f32[16,8,128]{2,1,0:T(8,128)S(1)} all-to-all(f32[16,8,128]{2,1,0:T(8,128)S(1)} %bitcast.59), channel_id=1, replica_groups=mesh['pix'=32,'tm'=16] {'tm'}, dimensions={0} | all-to-all | bytes 131072 | tf_op jit(solution)/shard_map/all_to_all | solution.py:416
  94.2 0.6 broadcast_in_dim.330
  94.8 3.5 %all-to-all-start.2 = ((f32[16,8,128]{2,1,0:T(8,128)}), f32[16,8,128]{2,1,0:T(8,128)S(1)}, u32[]{:S(2)}, u32[]{:S(2)}) async-start(f32[16,8,128]{2,1,0:T(8,128)} %broadcast_in_dim.330), calls=%async_computation.2 | async-start | bytes 131072 | tf_op jit(solution)/shard_map/all_to_all | solution.py:418
  98.5 7.6 %all-to-all-done.2 = f32[16,8,128]{2,1,0:T(8,128)S(1)} async-done(((f32[16,8,128]{2,1,0:T(8,128)}), f32[16,8,128]{2,1,0:T(8,128)S(1)}, u32[]{:S(2)}, u32[]{:S(2)}) %all-to-all-start.2) | async-done | bytes 65568 | tf_op jit(solution)/shard_map/all_to_all | solution.py:418
  106.1 3.7 %basis.1 = (f32[96,128]{1,0:T(8,128)S(1)}, f32[96,128]{1,0:T(8,128)S(1)}) custom-call(f32[128,128]{1,0:T(8,128)S(1)} %bitcast.60, f32[128,128]{1,0:T(8,128)S(1)} %pad.8.test_ref), custom_call_target="tpu_custom_call" | custom-call | tf_op jit(solution)/shard_map/basis/pallas_call | solution.py:358
  109.9 1.9 %collective-permute-start.2 = (f32[96,128]{1,0:T(8,128)S(1)}, f32[96,128]{1,0:T(8,128)S(1)}, u32[]{:S(2)}, u32[]{:S(2)}) collective-permute-start(f32[96,128]{1,0:T(8,128)S(1)} %get-tuple-element.18.own_ref), channel_id=1, source_target_pairs={{0,16},{16,0},{32,48},{48,32},{64,80},{80,64},{96,112},{112,96},{1... | collective-permute-start | bytes 147464 | tf_op jit(solution)/shard_map/ppermute | solution.py:442
  111.8 4.0 %collective-permute-done.2.partner_ref = f32[96,128]{1,0:T(8,128)S(1)} collective-permute-done((f32[96,128]{1,0:T(8,128)S(1)}, f32[96,128]{1,0:T(8,128)S(1)}, u32[]{:S(2)}, u32[]{:S(2)}) %collective-permute-start.2) | collective-permute-done | bytes 49184 | tf_op jit(solution)/shard_map/ppermute | solution.py:442
  115.8 4.0 %merge.3 = (f32[96,128]{1,0:T(8,128)S(1)}, f32[96,128]{1,0:T(8,128)S(1)}) custom-call(s32[1]{0:T(128)} %bitcast.4.place_ref, f32[96,128]{1,0:T(8,128)S(1)} %get-tuple-element.18.own_ref, f32[96,128]{1,0:T(8,128)S(1)} %collective-permute-done.2.partner_ref, f32[96,128]{1,0:T(8,128)S(1)} %get-tuple-element.19.weights_ref, f32[192,128]{1,0:T(8,128)S(1)} %pad.9.probe_ref), custom_call_target="tpu_custom_call" | custom-call | tf_op jit(solution)/shard_map/merge/pallas_call | solution.py:390
  119.8 1.9 %collective-permute-start.3 = (f32[96,128]{1,0:T(8,128)S(1)}, f32[96,128]{1,0:T(8,128)S(1)}, u32[]{:S(2)}, u32[]{:S(2)}) collective-permute-start(f32[96,128]{1,0:T(8,128)S(1)} %get-tuple-element.20.own_ref), channel_id=1, source_target_pairs={{0,32},{16,48},{32,0},{48,16},{64,96},{80,112},{96,64},{112,80},{1... | collective-permute-start | bytes 147464 | tf_op jit(solution)/shard_map/ppermute | solution.py:442
  121.7 5.1 %collective-permute-done.3.partner_ref = f32[96,128]{1,0:T(8,128)S(1)} collective-permute-done((f32[96,128]{1,0:T(8,128)S(1)}, f32[96,128]{1,0:T(8,128)S(1)}, u32[]{:S(2)}, u32[]{:S(2)}) %collective-permute-start.3) | collective-permute-done | bytes 49184 | tf_op jit(solution)/shard_map/ppermute | solution.py:442
  126.8 4.0 %merge.4 = (f32[96,128]{1,0:T(8,128)S(1)}, f32[96,128]{1,0:T(8,128)S(1)}) custom-call(s32[1]{0:T(128)} %bitcast.3.place_ref, f32[96,128]{1,0:T(8,128)S(1)} %get-tuple-element.20.own_ref, f32[96,128]{1,0:T(8,128)S(1)} %collective-permute-done.3.partner_ref, f32[96,128]{1,0:T(8,128)S(1)} %get-tuple-element.21.weights_ref, f32[192,128]{1,0:T(8,128)S(1)} %pad.9.probe_ref), custom_call_target="tpu_custom_call" | custom-call | tf_op jit(solution)/shard_map/merge/pallas_call | solution.py:390
  130.8 3.8 %collective-permute-start.4 = (f32[96,128]{1,0:T(8,128)S(1)}, f32[96,128]{1,0:T(8,128)S(1)}, u32[]{:S(2)}, u32[]{:S(2)}) collective-permute-start(f32[96,128]{1,0:T(8,128)S(1)} %get-tuple-element.22.own_ref), channel_id=1, source_target_pairs={{0,64},{16,80},{32,96},{48,112},{64,0},{80,16},{96,32},{112,48},{1... | collective-permute-start | bytes 147464 | tf_op jit(solution)/shard_map/ppermute | solution.py:442
  134.7 6.5 %collective-permute-done.4.partner_ref = f32[96,128]{1,0:T(8,128)S(1)} collective-permute-done((f32[96,128]{1,0:T(8,128)S(1)}, f32[96,128]{1,0:T(8,128)S(1)}, u32[]{:S(2)}, u32[]{:S(2)}) %collective-permute-start.4) | collective-permute-done | bytes 49184 | tf_op jit(solution)/shard_map/ppermute | solution.py:442
  141.2 4.7 %merge.5 = (f32[4,96,128]{2,1,0:T(8,128)}, f32[96,128]{1,0:T(8,128)S(1)}) custom-call(s32[1]{0:T(128)} %bitcast.2.place_ref, f32[96,128]{1,0:T(8,128)S(1)} %get-tuple-element.22.own_ref, f32[96,128]{1,0:T(8,128)S(1)} %collective-permute-done.4.partner_ref, f32[96,128]{1,0:T(8,128)S(1)} %get-tuple-element.23.weights_ref, f32[192,128]{1,0:T(8,128)S(1)} %pad.9.probe_ref), custom_call_target="tpu_custom_call" | custom-call | tf_op jit(solution)/shard_map/merge/pallas_call | solution.py:390
  145.9 4.3 %all-to-all-start.3 = ((f32[4,96,128]{2,1,0:T(8,128)}), f32[4,96,128]{2,1,0:T(8,128)S(1)}, u32[]{:S(2)}, u32[]{:S(2)}) async-start(f32[4,96,128]{2,1,0:T(8,128)} %get-tuple-element.24), calls=%async_computation.3 | async-start | bytes 393216 | tf_op jit(solution)/shard_map/all_to_all | solution.py:447
  150.2 6.3 %all-to-all-done.3.rows_in_ref = f32[4,96,128]{2,1,0:T(8,128)S(1)} async-done(((f32[4,96,128]{2,1,0:T(8,128)}), f32[4,96,128]{2,1,0:T(8,128)S(1)}, u32[]{:S(2)}, u32[]{:S(2)}) %all-to-all-start.3) | async-done | bytes 196640 | tf_op jit(solution)/shard_map/all_to_all | solution.py:447
  156.5 9.0 %merge_four.1 = (f32[96,128]{1,0:T(8,128)S(1)}, f32[96,128]{1,0:T(8,128)S(1)}) custom-call(s32[1]{0:T(128)} %bitcast.1.place_ref, f32[4,96,128]{2,1,0:T(8,128)S(1)} %all-to-all-done.3.rows_in_ref, f32[96,128]{1,0:T(8,128)S(1)} %get-tuple-element.25.weights_ref, f32[192,128]{1,0:T(8,128)S(1)} %pad.9.probe_ref), custom_call_target="tpu_custom_call" | custom-call | tf_op jit(solution)/shard_map/merge_four/pallas_call | solution.py:408
  165.5 3.9 %loadings.1 = (bf16[96,32,256]{2,1,0:T(8,128)(2,1)}, f32[8,96]{1,0:T(8,128)}) custom-call(s32[1]{0:T(128)} %bitcast.span_ref, f32[96,128]{1,0:T(8,128)S(1)} %get-tuple-element.26.rows_ref, f32[96,128]{1,0:T(8,128)S(1)} %get-tuple-element.27.weights_ref, bf16[16,256,256]{2,1,0:T(8,128)(2,1)} %all_to_all.20.data_ref), custom_call_target="tpu_custom_call" | custom-call | tf_op jit(solution)/shard_map/loadings/pallas_call | solution.py:227
  (34 shorter events, 1.0 us)
Async XLA Ops:
  0.6 8.3 %copy-start.2 = (f32[6]{0:T(128)S(1)}, f32[6]{0:T(128)}, u32[]{:S(2)}) copy-start(f32[6]{0:T(128)} %param.7) | copy-start | bytes 76
  0.6 8.5 %copy-start.3 = (s32[32]{0:T(128)S(1)}, s32[32]{0:T(128)}, u32[]{:S(2)}) copy-start(s32[32]{0:T(128)} %param.6) | copy-start | bytes 388
  2.2 13.4 %collective-permute-start = (bf16[32,4096]{1,0:T(8,128)(2,1)S(1)}, bf16[32,4096]{1,0:T(8,128)(2,1)S(1)}, u32[]{:S(2)}, u32[]{:S(2)}) collective-permute-start(bf16[32,4096]{1,0:T(8,128)(2,1)S(1)} %reshape.156), channel_id=1, source_target_pairs={{0,16},{16,32},{32,48},{48,64},{64,80},{80,96},{96,112},{112,128},... | collective-permute-start | bytes 786440 | tf_op jit(solution)/shard_map/ppermute | solution.py:428
  7.0 10.9 %collective-permute-start.1 = (bf16[32,4096]{1,0:T(8,128)(2,1)S(1)}, bf16[32,4096]{1,0:T(8,128)(2,1)S(1)}, u32[]{:S(2)}, u32[]{:S(2)}) collective-permute-start(bf16[32,4096]{1,0:T(8,128)(2,1)S(1)} %reshape.157), channel_id=1, source_target_pairs={{16,0},{32,16},{48,32},{64,48},{80,64},{96,80},{112,96},{128,112},... | collective-permute-start | bytes 786440 | tf_op jit(solution)/shard_map/ppermute | solution.py:429
  79.3 19.1 %copy-start.1 = (f32[128,96]{0,1:T(8,128)S(1)}, f32[128,96]{0,1:T(8,128)}, u32[]{:S(2)}) copy-start(f32[128,96]{0,1:T(8,128)} %param.8) | copy-start | bytes 147460
  79.3 32.5 %copy-start = (f32[192,96]{1,0:T(8,128)S(1)}, f32[192,96]{1,0:T(8,128)}, u32[]{:S(2)}) copy-start(f32[192,96]{1,0:T(8,128)} %param.9) | copy-start | bytes 221188
  94.8 11.3 %all-to-all-start.2 = ((f32[16,8,128]{2,1,0:T(8,128)}), f32[16,8,128]{2,1,0:T(8,128)S(1)}, u32[]{:S(2)}, u32[]{:S(2)}) async-start(f32[16,8,128]{2,1,0:T(8,128)} %broadcast_in_dim.330), calls=%async_computation.2 | async-start | bytes 131072 | tf_op jit(solution)/shard_map/all_to_all | solution.py:418
  109.9 6.0 %collective-permute-start.2 = (f32[96,128]{1,0:T(8,128)S(1)}, f32[96,128]{1,0:T(8,128)S(1)}, u32[]{:S(2)}, u32[]{:S(2)}) collective-permute-start(f32[96,128]{1,0:T(8,128)S(1)} %get-tuple-element.18.own_ref), channel_id=1, source_target_pairs={{0,16},{16,0},{32,48},{48,32},{64,80},{80,64},{96,112},{112,96},{1... | collective-permute-start | bytes 147464 | tf_op jit(solution)/shard_map/ppermute | solution.py:442
  119.8 7.0 %collective-permute-start.3 = (f32[96,128]{1,0:T(8,128)S(1)}, f32[96,128]{1,0:T(8,128)S(1)}, u32[]{:S(2)}, u32[]{:S(2)}) collective-permute-start(f32[96,128]{1,0:T(8,128)S(1)} %get-tuple-element.20.own_ref), channel_id=1, source_target_pairs={{0,32},{16,48},{32,0},{48,16},{64,96},{80,112},{96,64},{112,80},{1... | collective-permute-start | bytes 147464 | tf_op jit(solution)/shard_map/ppermute | solution.py:442
  130.8 10.4 %collective-permute-start.4 = (f32[96,128]{1,0:T(8,128)S(1)}, f32[96,128]{1,0:T(8,128)S(1)}, u32[]{:S(2)}, u32[]{:S(2)}) collective-permute-start(f32[96,128]{1,0:T(8,128)S(1)} %get-tuple-element.22.own_ref), channel_id=1, source_target_pairs={{0,64},{16,80},{32,96},{48,112},{64,0},{80,16},{96,32},{112,48},{1... | collective-permute-start | bytes 147464 | tf_op jit(solution)/shard_map/ppermute | solution.py:442
  145.9 10.6 %all-to-all-start.3 = ((f32[4,96,128]{2,1,0:T(8,128)}), f32[4,96,128]{2,1,0:T(8,128)S(1)}, u32[]{:S(2)}, u32[]{:S(2)}) async-start(f32[4,96,128]{2,1,0:T(8,128)} %get-tuple-element.24), calls=%async_computation.3 | async-start | bytes 393216 | tf_op jit(solution)/shard_map/all_to_all | solution.py:447
